TPU v7x, 32 devices: a whole 2x2x4 slice. The times are simulated.
32 devices in a mesh: hour: 16 (over z, y, x), region: 2 (over core).
Axes of the slice: x: 2, y: 2, z: 4, core: 2. Of those that a mesh axis runs over, the one named last changes fastest.
Arguments:
- demand: float32 [2240, 1024], P('hour', 'region'), may hold values from 0.2 to 2
- avail_factor: bfloat16 [2240, 8, 1024], P('hour', None, 'region'), may hold values from 0 to 1
- tech_mask: int32 [8, 1024], P(None, 'region'), may hold values 0 or 1
- var_cost: float32 [8, 1024], P(None, 'region'), may hold values from 0.1 to 2
- inv_cost: float32 [8, 1024], P(None, 'region'), may hold values from 0.2 to 1
- ramp_rate: float32 [8, 1024], P(None, 'region'), may hold values from 0.1 to 1
- network: float32 [1024, 1024], P('region'), as said below
- pattern: int32 [8, 8], replicated, may hold values from 0 to 1, as said below
- live_hours: int32 [1], replicated, may hold values from 1961 to 2100
- generation: float32 [2240, 8, 1024], P('hour', None, 'region'), may hold values from 0 to 1
- angles: float32 [2240, 1024], P('hour', 'region'), may hold values from -3 to 3
- levels: float32 [2240, 1024], P('hour', 'region'), may hold values from 0 to 2
- net_power: float32 [2240, 1024], P('hour', 'region'), may hold values from -3 to 3
- capacity: float32 [8, 1024], P(None, 'region'), may hold values from 0.5 to 2
- balance_dual: float32 [2240, 1024], P('hour', 'region'), may hold values from -3 to 3
- storage_dual: float32 [2240, 1024], P('hour', 'region'), may hold values from -3 to 3
- limit_dual: float32 [2240, 8, 1024], P('hour', None, 'region'), may hold values from 0 to 1.5
- ramp_dual: float32 [2240, 8, 1024], P('hour', None, 'region'), may hold values from 0 to 0.5
Outputs:
- final_generation: float32 [2240, 8, 1024], P('hour', None, 'region')
- final_angles: float32 [2240, 1024], P('hour', 'region')
- final_levels: float32 [2240, 1024], P('hour', 'region')
- final_power: float32 [2240, 1024], P('hour', 'region')
- final_capacity: float32 [8, 1024], P(None, 'region')
- final_balance: float32 [2240, 1024], P('hour', 'region')
- final_storage: float32 [2240, 1024], P('hour', 'region')
- final_limit: float32 [2240, 8, 1024], P('hour', None, 'region')
- final_ramp: float32 [2240, 8, 1024], P('hour', None, 'region')
Inputs may be any that keep to these rules, and one draw needn't show every extreme that they name: pattern is symmetric with ones on its diagonal. network is symmetric.
All inputs are finite; a program needn't handle non-finite values. No bound on the sum of `tech_mask` on one device may be relied on, other than what follows from the above.
Results may differ from a plain program's by a relative error of at most 0.0003.
Values sent between devices are 32-bit elements; how exact they have to be, the bound alone decides.
No kernel may reach another device: no remote copies, remote signals or barrier semaphores. Data moves between devices by JAX's collectives and lax.ppermute only.
A program may use at most 64 MiB of HBM per device.

v0:
```python
import jax
import jax.numpy as jnp
from jax import lax
from jax.sharding import PartitionSpec as P

BUS = 1024
TECH = 8
BLOCK = 128
ITERS = 2


primal_step = 0.2
capacity_step = 4.0
dual_scale = 0.06


def shifted(block, axis, distance):
    devices = range(lax.axis_size(axis))
    route = [((i - distance) % len(devices), i) for i in devices]
    return lax.ppermute(block, axis, route)


def per_device(
    demand,
    avail_factor,
    tech_mask,
    var_cost,
    inv_cost,
    ramp_rate,
    network,
    pattern,
    live_hours,
    generation,
    angles,
    levels,
    net_power,
    capacity,
    balance_dual,
    storage_dual,
    limit_dual,
    ramp_dual,
):
    hour_rows = demand.shape[0]
    local_bus = demand.shape[1]
    total_hours = hour_rows * lax.axis_size("hour")
    first_hour = lax.axis_index("hour") * hour_rows
    live_rows = (first_hour + jnp.arange(hour_rows, dtype=jnp.int32) < live_hours[0]).astype(
        jnp.float32
    )
    available = (
        avail_factor.astype(jnp.float32)
        * tech_mask.astype(jnp.float32)[None]
        * live_rows[:, None, None]
    )
    live_load = demand * live_rows[:, None]
    blocks_here = local_bus // BLOCK
    pattern_rows = lax.dynamic_slice_in_dim(
        pattern, lax.axis_index("region") * blocks_here, blocks_here, 0
    )
    block_mask = jnp.repeat(jnp.repeat(pattern_rows.astype(jnp.float32), BLOCK, 0), BLOCK, 1)
    matrix = network * block_mask
    entry_count = float(total_hours * (TECH + 3) * BUS)

    def fold_part(segment):
        return lax.dot_general(
            segment,
            matrix,
            (((1,), (1,)), ((), ())),
            precision=lax.Precision.HIGHEST,
            preferred_element_type=jnp.float32,
        )

    for iteration in range(ITERS):
        behind = shifted((ramp_dual[-1:], storage_dual[-1:]), "hour", 1)
        prev_ramp = jnp.concatenate([behind[0], ramp_dual[:-1]], axis=0)
        prev_store = jnp.concatenate([behind[1], storage_dual[:-1]], axis=0)
        gen_new = jnp.maximum(
            0.0,
            generation
            - primal_step
            * (var_cost[None] + balance_dual[:, None, :] + limit_dual + prev_ramp - ramp_dual),
        )
        ang_new = angles + primal_step * fold_part(
            lax.all_gather(balance_dual, "region", axis=1, tiled=True)
        )
        pow_new = net_power - primal_step * (balance_dual + storage_dual)
        lev_new = jnp.maximum(0.0, levels - primal_step * (prev_store - storage_dual))
        square_part = (
            jnp.sum((gen_new - generation) ** 2)
            + jnp.sum((ang_new - angles) ** 2)
            + jnp.sum((pow_new - net_power) ** 2)
            + jnp.sum((lev_new - levels) ** 2)
        )
        invest_part = jnp.sum(available * limit_dual + ramp_rate[None] * ramp_dual, axis=0)
        invest = lax.psum(invest_part, "hour")
        squares = lax.psum(square_part, ("hour", "region"))
        cap_new = jnp.maximum(
            0.0, capacity - capacity_step * (inv_cost - invest / float(total_hours))
        )
        step_size = jnp.sqrt(squares / entry_count + 1e-06)
        dual_step = dual_scale / step_size
        gen_bar = 2.0 * gen_new - generation
        ang_bar = 2.0 * ang_new - angles
        pow_bar = 2.0 * pow_new - net_power
        lev_bar = 2.0 * lev_new - levels
        cap_bar = 2.0 * cap_new - capacity
        forward = shifted((gen_bar[:1], lev_bar[:1]), "hour", -1)
        next_gen = jnp.concatenate([gen_bar[1:], forward[0]], axis=0)
        next_level = jnp.concatenate([lev_bar[1:], forward[1]], axis=0)
        balance_dual = balance_dual + dual_step * (
            jnp.sum(gen_bar, axis=1)
            + pow_bar
            - fold_part(lax.all_gather(ang_bar, "region", axis=1, tiled=True))
            - live_load
        )
        storage_dual = storage_dual + dual_step * (next_level - lev_bar + pow_bar)
        limit_dual = jnp.maximum(
            0.0, limit_dual + dual_step * (gen_bar - available * cap_bar[None])
        )
        ramp_dual = jnp.maximum(
            0.0, ramp_dual + dual_step * (next_gen - gen_bar - ramp_rate[None] * cap_bar[None])
        )
        generation, angles, net_power, levels, capacity = (
            gen_new,
            ang_new,
            pow_new,
            lev_new,
            cap_new,
        )
    return (
        generation,
        angles,
        levels,
        net_power,
        capacity,
        balance_dual,
        storage_dual,
        limit_dual,
        ramp_dual,
    )


def solution(mesh):
    return jax.shard_map(
        per_device,
        mesh=mesh,
        in_specs=(
            P("hour", "region"),
            P("hour", None, "region"),
            P(None, "region"),
            P(None, "region"),
            P(None, "region"),
            P(None, "region"),
            P("region", None),
            P(),
            P(),
            P("hour", None, "region"),
            P("hour", "region"),
            P("hour", "region"),
            P("hour", "region"),
            P(None, "region"),
            P("hour", "region"),
            P("hour", "region"),
            P("hour", None, "region"),
            P("hour", None, "region"),
        ),
        out_specs=(
            P("hour", None, "region"),
            P("hour", "region"),
            P("hour", "region"),
            P("hour", "region"),
            P(None, "region"),
            P("hour", "region"),
            P("hour", "region"),
            P("hour", None, "region"),
            P("hour", None, "region"),
        ),
        check_vma=False,
    )
```

profile of v0, /device:TPU:0, one launch (start us, length us, event | category | flops | bytes accessed | tf_op | source)
XLA Modules:
  0.0 319.3 jit_solution(14245832103954252068)
XLA Ops:
  0.6 0.7 slice.50
  1.4 2.9 collective-permute-start.1
  4.3 0.7 slice.48
  5.0 1.5 collective-permute-start
  7.2 2.4 all_gather.12
  9.6 0.8 dynamic-slice_convert_fusion
  10.5 0.6 broadcast_in_dim.5
  11.2 0.7 bitcast_multiply_fusion
  11.9 0.2 copy-done.28
  12.2 3.7 %multiply_subtract_fusion.7 = (f32[140,512]{1,0:T(8,128)S(1)}, f32[]{:T(128)}, f32[140,512]{1,0:T(8,128)}) fusion(f32[140,512]{1,0:T(8,128)S(1)} %copy-done.28, f32[512,1024]{1,0:T(8,128)S(1)} %bitcast_multiply_fusion, f32[140,1024]{1,0:T(8,128)S(1)} %all_gather.12), kind=kOutput, calls=%fused_computation.61 | convolution fusion | flops 881305600 | bytes 3530756 | tf_op jit(solution)/shard_map/dot_general | solution.py:65
  15.9 2.2 all_gather.13
  18.1 3.0 fusion.39
  21.2 0.6 copy-done.36
  21.9 0.2 copy-done.15
  22.3 3.0 multiply_subtract_fusion.6
  25.3 0.7 multiply_reduce_fusion.5
  26.1 4.1 %collective-permute-start.4 = (f32[1,512]{1,0:T(1,128)S(1)}, f32[1,512]{1,0:T(1,128)S(1)}, u32[]{:S(2)}, u32[]{:S(2)}) collective-permute-start(f32[1,512]{1,0:T(1,128)S(1)} %slice.69), channel_id=1, source_target_pairs={{2,0},{4,2},{6,4},{8,6},{10,8},{12,10},{14,12},{16,14},{18,16},{20... | collective-permute-start | bytes 6152 | tf_op jit(solution)/shard_map/ppermute | solution.py:20
  30.2 6.1 %fusion.36 = (f32[140,512]{1,0:T(8,128)}, f32[140,8,512]{2,1,0:T(8,128)}, f32[140,8,512]{2,1,0:T(8,128)S(1)}, f32[8,512]{1,0:T(8,128)S(1)}) fusion(f32[140,8,512]{2,1,0:T(8,128)} %param.27, f32[140,8,512]{2,1,0:T(8,128)S(1)} %copy-done.5, f32[139,8,512]{2,1,0:T(8,128)S(1)} %slice-done, f32[1,8,512]{2,1,0:T(8,128)S(1)} %collective-permute-done, ...), kind=kLoop, calls=%fused_computation.74 | loop fusion | flops 10246144 | bytes 15548976 | tf_op jit(solution)/shard_map/reduce_sum | solution.py:111
  36.3 1.3 multiply_reduce_fusion.1
  40.2 1.7 slice.68
  41.9 37.6 %psum.28 = f32[]{:T(128)} all-reduce(f32[]{:T(128)S(6)} %add.149), channel_id=1, replica_groups=mesh['hour'=16,'region'=2] {'hour','region'}, use_global_device_ids=true, to_apply=%region_4.0 | all-reduce | flops 1 | bytes 8 | tf_op jit(solution)/shard_map/psum | solution.py:96
  80.3 3.3 %multiply_reduce_fusion.3 = (f32[]{:T(128)}, f32[140,512]{1,0:T(8,128)}, f32[140,512]{1,0:T(8,128)S(1)}, f32[140,512]{1,0:T(8,128)}) fusion(f32[140,512]{1,0:T(8,128)} %get-tuple-element.42, f32[140,512]{1,0:T(8,128)} %param.33, f32[140,512]{1,0:T(8,128)} %param.30, f32[140,512]{1,0:T(8,128)} %copy-done.20, f32[1,512]{1,0:T(1,128)S(1)} %collective-permute-done.4, ...), kind=kLoop, calls=%fused_computation.56 | loop fusion | flops 1361919 | bytes 3441208 | tf_op jit(solution)/shard_map/reduce_sum | solution.py:91
  83.6 0.7 copy-done.10
  84.3 2.3 collective-permute-start.5
  86.6 75.0 %psum.29 = f32[8,512]{1,0:T(8,128)S(1)} all-reduce(f32[8,512]{1,0:T(8,128)S(1)} %get-tuple-element.32), channel_id=1, replica_groups=mesh['hour'=16,'region'=2] {'hour'}, use_global_device_ids=true, to_apply=%region_7.0 | all-reduce | flops 4096 | bytes 32768 | tf_op jit(solution)/shard_map/psum | solution.py:95
  161.5 0.9 slice.65
  162.4 2.6 all_gather.14
  165.0 4.8 %multiply_reduce_fusion.4 = (f32[]{:T(128)}, f32[140,512]{1,0:T(8,128)}, f32[140,512]{1,0:T(8,128)}) fusion(f32[140,512]{1,0:T(8,128)} %get-tuple-element.43, f32[140,1024]{1,0:T(8,128)S(1)} %all_gather.14, f32[512,1024]{1,0:T(8,128)S(1)} %bitcast_multiply_fusion), kind=kOutput, calls=%fused_computation.57 | convolution fusion | flops 881305600 | bytes 3530756 | tf_op jit(solution)/shard_map/dot_general | solution.py:65
  169.9 0.2 slice.64
  170.1 0.7 copy-done.11
  170.9 0.8 multiply_subtract_fusion.2
  171.7 0.9 fusion.7
  172.6 2.1 collective-permute-start.3
  174.7 0.7 multiply_reduce_fusion.2
  175.3 0.2 slice.67
  175.5 4.4 %collective-permute-done.3 = f32[1,8,512]{2,1,0:T(8,128)S(1)} collective-permute-done((f32[1,8,512]{2,1,0:T(8,128)S(1)}, f32[1,8,512]{2,1,0:T(8,128)S(1)}, u32[]{:S(2)}, u32[]{:S(2)}) %collective-permute-start.3) | collective-permute-done | bytes 16416 | tf_op jit(solution)/shard_map/ppermute | solution.py:20
  180.0 4.3 %multiply_reduce_fusion = (f32[]{:T(128)}, f32[140,8,512]{2,1,0:T(8,128)}, f32[140,8,512]{2,1,0:T(8,128)}) fusion(f32[140,8,512]{2,1,0:T(8,128)S(1)} %copy-done.3, f32[140,8,512]{2,1,0:T(8,128)S(1)} %fusion.7, f32[139,8,512]{2,1,0:T(8,128)S(1)} %slice.67, f32[1,8,512]{2,1,0:T(8,128)S(1)} %collective-permute-done.3, f32[140,512]{1,0:T(8,128)S(1)} %copy-done.16, ...), kind=kLoop, calls=%fused_computation.22 | loop fusion | flops 10895359 | bytes 17539640 | tf_op jit(solution)/shard_map/reduce_sum | solution.py:89
  186.8 3.9 %all_gather.15 = f32[140,1024]{1,0:T(8,128)} all-gather(f32[140,512]{1,0:T(8,128)} %get-tuple-element.38), channel_id=1, replica_groups=mesh['hour'=16,'region'=2] {'region'}, dimensions={1}, use_global_device_ids=true | all-gather | bytes 860160 | tf_op jit(solution)/shard_map/all_gather | solution.py:113
  190.7 36.8 %psum.31 = f32[]{:T(128)} all-reduce(f32[]{:T(128)S(6)} %add.169), channel_id=1, replica_groups=mesh['hour'=16,'region'=2] {'hour','region'}, use_global_device_ids=true, to_apply=%region_14.0 | all-reduce | flops 1 | bytes 8 | tf_op jit(solution)/shard_map/psum | solution.py:96
  228.2 2.2 add_reduce_fusion
  230.4 75.8 %psum.30 = f32[8,512]{1,0:T(8,128)S(1)} all-reduce(f32[8,512]{1,0:T(8,128)S(1)} %add_reduce_fusion), channel_id=1, replica_groups=mesh['hour'=16,'region'=2] {'hour'}, use_global_device_ids=true, to_apply=%region_9.0 | all-reduce | flops 4096 | bytes 32768 | tf_op jit(solution)/shard_map/psum | solution.py:95
  306.2 0.6 fusion.31
  306.9 5.3 %add_maximum_fusion = (f32[140,8,512]{2,1,0:T(8,128)}, f32[140,8,512]{2,1,0:T(8,128)S(1)}) fusion(f32[140,8,512]{2,1,0:T(8,128)} %get-tuple-element.22, bf16[140,8,512]{2,1,0:T(8,128)(2,1)S(1)} %copy-done.7, f32[8,512]{1,0:T(8,128)S(1)} %get-tuple-element.10, f32[]{:T(128)S(6)} %div.23, f32[140]{0:T(256)} %copy-done.33, ...), kind=kLoop, calls=%fused_computation.20 | loop fusion | flops 5734400 | bytes 12649012 | tf_op jit(solution)/shard_map/max | solution.py:117
  312.2 2.3 fusion.40
  314.7 0.2 slice.74
  314.9 1.1 collective-permute-done.7
  316.0 2.3 fusion.15
  318.3 1.0 fusion.30
  (90 shorter events, 0.8 us)
Async XLA Ops:
  1.4 20.5 %collective-permute-start.1 = (f32[1,512]{1,0:T(1,128)S(1)}, f32[1,512]{1,0:T(1,128)S(1)}, u32[]{:S(2)}, u32[]{:S(2)}) collective-permute-start(f32[1,512]{1,0:T(1,128)S(1)} %slice.50), channel_id=1, source_target_pairs={{30,0},{0,2},{2,4},{4,6},{6,8},{8,10},{10,12},{12,14},{14,16},{16,... | collective-permute-start | bytes 6152 | tf_op jit(solution)/shard_map/ppermute | solution.py:20
  5.0 25.2 %collective-permute-start = (f32[1,8,512]{2,1,0:T(8,128)S(1)}, f32[1,8,512]{2,1,0:T(8,128)S(1)}, u32[]{:S(2)}, u32[]{:S(2)}) collective-permute-start(f32[1,8,512]{2,1,0:T(8,128)S(1)} %slice.48), channel_id=1, source_target_pairs={{30,0},{0,2},{2,4},{4,6},{6,8},{8,10},{10,12},{12,14},{14,16},{16,... | collective-permute-start | bytes 49160 | tf_op jit(solution)/shard_map/ppermute | solution.py:20
  9.6 1.6 copy-start.23
  11.2 1.0 copy-start.28
  12.2 152.8 %copy-start = (f32[512,1024]{1,0:T(8,128)}, f32[512,1024]{1,0:T(8,128)S(1)}, u32[]{:S(2)}) copy-start(f32[512,1024]{1,0:T(8,128)S(1)} %bitcast_multiply_fusion) | copy-start | bytes 6291460
  21.1 0.7 copy-start.36
  21.1 59.1 %copy-start.33 = (f32[140]{0:T(256)}, f32[140]{0:T(256)S(1)}, u32[]{:S(2)}) copy-start(f32[140]{0:T(256)S(1)} %compare_convert_fusion) | copy-start | bytes 1684
  21.1 1.0 copy-start.15
  21.2 1.0 copy-start.18
  21.2 1.1 copy-start.24
  21.2 9.0 %copy-start.5 = (f32[140,8,512]{2,1,0:T(8,128)S(1)}, f32[140,8,512]{2,1,0:T(8,128)}, u32[]{:S(2)}) copy-start(f32[140,8,512]{2,1,0:T(8,128)} %param.35) | copy-start | bytes 6881284
  21.2 9.0 %copy-start.7 = (bf16[140,8,512]{2,1,0:T(8,128)(2,1)S(1)}, bf16[140,8,512]{2,1,0:T(8,128)(2,1)}, u32[]{:S(2)}) copy-start(bf16[140,8,512]{2,1,0:T(8,128)(2,1)} %param.19) | copy-start | bytes 3440644
  21.9 8.4 %slice-start = ((f32[140,8,512]{2,1,0:T(8,128)}), f32[139,8,512]{2,1,0:T(8,128)S(1)}, s32[]{:S(2)}) async-start(f32[140,8,512]{2,1,0:T(8,128)} %param.35), calls=%async_computation | async-start | bytes 4554752 | tf_op jit(solution)/shard_map/slice | solution.py:75
  21.9 8.4 %copy-start.29 = (f32[8,512]{1,0:T(8,128)S(1)}, f32[8,512]{1,0:T(8,128)}, u32[]{:S(2)}) copy-start(f32[8,512]{1,0:T(8,128)} %param.23) | copy-start | bytes 49156
  21.9 8.4 %copy-start.32 = (f32[8,512]{1,0:T(8,128)S(1)}, f32[8,512]{1,0:T(8,128)}, u32[]{:S(2)}) copy-start(f32[8,512]{1,0:T(8,128)} %param.21) | copy-start | bytes 49156
  25.3 0.7 copy-start.20
  25.3 4.8 %copy-start.13 = (f32[140,512]{1,0:T(8,128)}, f32[140,512]{1,0:T(8,128)S(1)}, u32[]{:S(2)}) copy-start(f32[140,512]{1,0:T(8,128)S(1)} %get-tuple-element.24) | copy-start | bytes 860164
  26.1 10.3 %copy-start.8 = (f32[140,8,512]{2,1,0:T(8,128)S(1)}, f32[140,8,512]{2,1,0:T(8,128)}, u32[]{:S(2)}) copy-start(f32[140,8,512]{2,1,0:T(8,128)} %param.27) | copy-start | bytes 6881284
  26.1 54.2 %collective-permute-start.4 = (f32[1,512]{1,0:T(1,128)S(1)}, f32[1,512]{1,0:T(1,128)S(1)}, u32[]{:S(2)}, u32[]{:S(2)}) collective-permute-start(f32[1,512]{1,0:T(1,128)S(1)} %slice.69), channel_id=1, source_target_pairs={{2,0},{4,2},{6,4},{8,6},{10,8},{12,10},{14,12},{16,14},{18,16},{20... | collective-permute-start | bytes 6152 | tf_op jit(solution)/shard_map/ppermute | solution.py:20
  36.3 1.4 copy-start.2
  83.6 0.7 copy-start.10
  83.6 86.2 %copy-start.30 = (f32[8,512]{1,0:T(8,128)S(1)}, f32[8,512]{1,0:T(8,128)}, u32[]{:S(2)}) copy-start(f32[8,512]{1,0:T(8,128)} %param.31) | copy-start | bytes 49156
  83.6 86.2 %copy-start.31 = (f32[8,512]{1,0:T(8,128)S(1)}, f32[8,512]{1,0:T(8,128)}, u32[]{:S(2)}) copy-start(f32[8,512]{1,0:T(8,128)} %param.22) | copy-start | bytes 49156
  84.3 85.8 %collective-permute-start.5 = (f32[1,512]{1,0:T(1,128)S(1)}, f32[1,512]{1,0:T(1,128)S(1)}, u32[]{:S(2)}, u32[]{:S(2)}) collective-permute-start(f32[1,512]{1,0:T(1,128)S(1)} %slice.70), channel_id=1, source_target_pairs={{30,0},{0,2},{2,4},{4,6},{6,8},{8,10},{10,12},{12,14},{14,16},{16,... | collective-permute-start | bytes 6152 | tf_op jit(solution)/shard_map/ppermute | solution.py:20
  161.5 8.3 %copy-start.4 = (f32[140,8,512]{2,1,0:T(8,128)S(1)}, f32[140,8,512]{2,1,0:T(8,128)}, u32[]{:S(2)}) copy-start(f32[140,8,512]{2,1,0:T(8,128)} %get-tuple-element.26) | copy-start | bytes 6881284
  162.4 9.3 %collective-permute-start.2 = (f32[1,8,512]{2,1,0:T(8,128)S(1)}, f32[1,8,512]{2,1,0:T(8,128)S(1)}, u32[]{:S(2)}, u32[]{:S(2)}) collective-permute-start(f32[1,8,512]{2,1,0:T(8,128)S(1)} %slice.65), channel_id=1, source_target_pairs={{2,0},{4,2},{6,4},{8,6},{10,8},{12,10},{14,12},{16,14},{18,16},{20... | collective-permute-start | bytes 49160 | tf_op jit(solution)/shard_map/ppermute | solution.py:20
  169.9 1.0 copy-start.11
  169.9 1.0 copy-start.14
  169.9 1.9 copy-start.6
  171.7 3.0 copy-start.27
  172.6 7.4 %collective-permute-start.3 = (f32[1,8,512]{2,1,0:T(8,128)S(1)}, f32[1,8,512]{2,1,0:T(8,128)S(1)}, u32[]{:S(2)}, u32[]{:S(2)}) collective-permute-start(f32[1,8,512]{2,1,0:T(8,128)S(1)} %slice.66), channel_id=1, source_target_pairs={{30,0},{0,2},{2,4},{4,6},{6,8},{8,10},{10,12},{12,14},{14,16},{16,... | collective-permute-start | bytes 49160 | tf_op jit(solution)/shard_map/ppermute | solution.py:20
  174.7 5.3 %copy-start.9 = (f32[140,8,512]{2,1,0:T(8,128)S(1)}, f32[140,8,512]{2,1,0:T(8,128)}, u32[]{:S(2)}) copy-start(f32[140,8,512]{2,1,0:T(8,128)} %param.34) | copy-start | bytes 6881284
  175.3 4.7 %copy-start.3 = (f32[140,8,512]{2,1,0:T(8,128)S(1)}, f32[140,8,512]{2,1,0:T(8,128)}, u32[]{:S(2)}) copy-start(f32[140,8,512]{2,1,0:T(8,128)} %copy-done.2) | copy-start | bytes 6881284
  175.3 4.7 %copy-start.16 = (f32[140,512]{1,0:T(8,128)S(1)}, f32[140,512]{1,0:T(8,128)}, u32[]{:S(2)}) copy-start(f32[140,512]{1,0:T(8,128)} %get-tuple-element.19) | copy-start | bytes 860164
  175.3 4.7 %copy-start.34 = (f32[140]{0:T(256)S(1)}, f32[140]{0:T(256)}, u32[]{:S(2)}) copy-start(f32[140]{0:T(256)} %copy-done.33) | copy-start | bytes 1684
  306.9 5.4 %copy-start.1 = (f32[512,1024]{1,0:T(8,128)S(1)}, f32[512,1024]{1,0:T(8,128)}, u32[]{:S(2)}) copy-start(f32[512,1024]{1,0:T(8,128)} %copy-done) | copy-start | bytes 6291460
  306.9 5.4 %copy-start.22 = (f32[140,1024]{1,0:T(8,128)S(1)}, f32[140,1024]{1,0:T(8,128)}, u32[]{:S(2)}) copy-start(f32[140,1024]{1,0:T(8,128)} %all_gather.15) | copy-start | bytes 1720324
  312.2 2.4 copy-start.19
  312.2 3.7 %collective-permute-start.7 = (f32[1,8,512]{2,1,0:T(8,128)S(1)}, f32[1,8,512]{2,1,0:T(8,128)S(1)}, u32[]{:S(2)}, u32[]{:S(2)}) collective-permute-start(f32[1,8,512]{2,1,0:T(8,128)S(1)} %slice.75), channel_id=1, source_target_pairs={{2,0},{4,2},{6,4},{8,6},{10,8},{12,10},{14,12},{16,14},{18,16},{20... | collective-permute-start | bytes 49160 | tf_op jit(solution)/shard_map/ppermute | solution.py:20
  314.6 3.6 %collective-permute-start.6 = (f32[1,512]{1,0:T(1,128)S(1)}, f32[1,512]{1,0:T(1,128)S(1)}, u32[]{:S(2)}, u32[]{:S(2)}) collective-permute-start(f32[1,512]{1,0:T(1,128)S(1)} %slice.73), channel_id=1, source_target_pairs={{2,0},{4,2},{6,4},{8,6},{10,8},{12,10},{14,12},{16,14},{18,16},{20... | collective-permute-start | bytes 6152 | tf_op jit(solution)/shard_map/ppermute | solution.py:20
  315.9 2.3 copy-start.12
  315.9 2.3 copy-start.17
  315.9 2.3 copy-start.21
  316.0 2.3 copy-start.25
  316.0 2.3 copy-start.26
  316.0 2.3 copy-start.35
where the time goes:
time: 320 us; the launch traced here: 319 us
  blocking collectives  236 us (74%)
  other arithmetic  33.9 us (11%)
  matrix products  13.8 us (4%)
  starting transfers between devices  13 us (4%)
  local copies, waits for them, and re-layouts  8.49 us (3%)
  between operations  8.08 us (3%)
  waiting for transfers between devices  5.53 us (2%)
    psum x2, blocking collectives, per_device(): invest = lax.psum(invest_part, 'hour')  151 us
    psum x2, blocking collectives, per_device(): squares = lax.psum(square_part, ('hour', 'region'))  74.5 us
    dot_general x4, matrix products, fold_part(): lax.dot_general(segment, matrix, (((1,), (1,)), ((), ())), precision=lax....  13.8 us
    ppermute x8, starting transfers between devices, shifted(): return lax.ppermute(block, axis, route)  13 us
  transfers between devices with their start and end apart: 8, of which 2 were waited for; matrix products, arithmetic and copies ran while one was open for 11% of the time, Pallas kernels for 0%

commit v1 on v0

--- a/solution.py
+++ b/solution.py
@@ -18,6 +18,16 @@
     devices = range(lax.axis_size(axis))
     route = [((i - distance) % len(devices), i) for i in devices]
     return lax.ppermute(block, axis, route)
+
+
+def summed(block, axis):
+    size = lax.axis_size(axis)
+    distance = 1
+    while distance < size:
+        route = [(i, i ^ distance) for i in range(size)]
+        block = block + lax.ppermute(block, axis, route)
+        distance *= 2
+    return block
 
 
 def per_device(
@@ -92,8 +102,10 @@
             + jnp.sum((lev_new - levels) ** 2)
         )
         invest_part = jnp.sum(available * limit_dual + ramp_rate[None] * ramp_dual, axis=0)
-        invest = lax.psum(invest_part, "hour")
-        squares = lax.psum(square_part, ("hour", "region"))
+        square_part = summed(jnp.full((8, invest_part.shape[1]), square_part), "region")
+        totals = summed(jnp.concatenate([invest_part, square_part], axis=0), "hour")
+        invest = totals[:TECH]
+        squares = totals[TECH, 0]
         cap_new = jnp.maximum(
             0.0, capacity - capacity_step * (inv_cost - invest / float(total_hours))
         )

time: 320 us -> 117 us (0.37)
  blocking collectives: 236 us -> 9.52 us
  starting transfers between devices: 13 us -> 30.1 us
  waiting for transfers between devices: 5.53 us -> 15 us
    psum x4 -> x0, blocking collectives: 225 us -> none  [the longest x2 151 us: per_device(): invest = lax.psum(invest_part, 'hour')]
    ppermute x0 -> x10, waiting for transfers between devices: none -> 14.9 us  [summed(): block = block + lax.ppermute(block, axis, route)]
    ppermute x0 -> x10, starting transfers between devices: none -> 12 us  [summed(): block = block + lax.ppermute(block, axis, route)]
    ppermute x8, waiting for transfers between devices: 5.53 us -> 0.02 us  [shifted(): return lax.ppermute(block, axis, route)]
    ppermute x8, starting transfers between devices: 13 us -> 18.1 us  [shifted(): return lax.ppermute(block, axis, route)]
  transfers between devices with their start and end apart: 8 -> 18, of which waited for: 2 -> 9; matrix products, arithmetic and copies ran while one was open for 11% -> 25% of each run, Pallas kernels for 0% -> 0%
where the time goes in v1:
time: 117 us; the launch traced here: 116 us
  other arithmetic  33.5 us (29%)
  starting transfers between devices  30.1 us (26%)
  waiting for transfers between devices  15 us (13%)
  matrix products  12.3 us (11%)
  blocking collectives  9.52 us (8%)
  between operations  8.69 us (7%)
  local copies, waits for them, and re-layouts  7.03 us (6%)
    ppermute x8, starting transfers between devices, shifted(): return lax.ppermute(block, axis, route)  18.1 us
    ppermute x10, waiting for transfers between devices, summed(): block = block + lax.ppermute(block, axis, route)  14.9 us
    dot_general x4, matrix products, fold_part(): lax.dot_general(segment, matrix, (((1,), (1,)), ((), ())), precision=lax....  12.3 us
    ppermute x10, starting transfers between devices, summed(): block = block + lax.ppermute(block, axis, route)  12 us
    reduce_sum x1, other arithmetic, per_device(): jnp.sum(gen_bar, axis=1) + pow_bar  5.22 us
    max x1, other arithmetic, per_device(): jnp.maximum(0.0, limit_dual + dual_step * (gen_bar - available * cap_bar[...  5.21 us
    all_gather x2, blocking collectives, per_device(): lax.all_gather(ang_bar, 'region', axis=1, tiled=True)  4.85 us
    all_gather x2, blocking collectives, per_device(): lax.all_gather(balance_dual, 'region', axis=1, tiled=True)  4.67 us
  transfers between devices with their start and end apart: 18, of which 9 were waited for; matrix products, arithmetic and copies ran while one was open for 25% of the time, Pallas kernels for 0%

profile of v1, /device:TPU:0, one launch (start us, length us, event | category | flops | bytes accessed | tf_op | source)
XLA Modules:
  0.0 116.1 jit_solution(4802184084274955663)
XLA Ops:
  0.6 0.7 slice.62
  1.4 2.9 %collective-permute-start.1 = (f32[1,512]{1,0:T(1,128)S(1)}, f32[1,512]{1,0:T(1,128)S(1)}, u32[]{:S(2)}, u32[]{:S(2)}) collective-permute-start(f32[1,512]{1,0:T(1,128)S(1)} %slice.62), channel_id=1, source_target_pairs={{30,0},{0,2},{2,4},{4,6},{6,8},{8,10},{10,12},{12,14},{14,16},{16,... | collective-permute-start | bytes 6152 | tf_op jit(solution)/shard_map/ppermute | solution.py:20
  4.3 1.3 %slice.60 = f32[1,8,512]{2,1,0:T(8,128)} slice(f32[140,8,512]{2,1,0:T(8,128)} %param.35), slice={[139:140], [0:8], [0:512]} | slice | bytes 32768 | tf_op jit(solution)/shard_map/slice | solution.py:84
  5.6 1.5 %collective-permute-start = (f32[1,8,512]{2,1,0:T(8,128)}, f32[1,8,512]{2,1,0:T(8,128)}, u32[]{:S(2)}, u32[]{:S(2)}) collective-permute-start(f32[1,8,512]{2,1,0:T(8,128)} %slice.60), channel_id=1, source_target_pairs={{30,0},{0,2},{2,4},{4,6},{6,8},{8,10},{10,12},{12,14},{14,16},{16,... | collective-permute-start | bytes 49160 | tf_op jit(solution)/shard_map/ppermute | solution.py:20
  7.8 2.4 %all_gather.12 = f32[140,1024]{1,0:T(8,128)S(1)} all-gather(f32[140,512]{1,0:T(8,128)} %param.32), channel_id=1, replica_groups=mesh['hour'=16,'region'=2] {'region'}, dimensions={1}, use_global_device_ids=true | all-gather | bytes 860160 | tf_op jit(solution)/shard_map/all_gather | solution.py:94
  10.2 0.8 dynamic-slice_convert_fusion
  12.8 3.9 %multiply_subtract_fusion.7 = (f32[140,512]{1,0:T(8,128)}, f32[]{:T(128)}, f32[140,512]{1,0:T(8,128)}) fusion(f32[140,512]{1,0:T(8,128)S(1)} %copy-done.35, f32[512,1024]{1,0:T(8,128)S(1)} %bitcast_multiply_fusion, f32[140,1024]{1,0:T(8,128)S(1)} %all_gather.12), kind=kOutput, calls=%fused_computation.61 | convolution fusion | flops 881305600 | bytes 3530756 | tf_op jit(solution)/shard_map/dot_general | solution.py:75
  18.0 2.6 %multiply_subtract_fusion.6 = (f32[140,512]{1,0:T(8,128)S(1)}, f32[140,512]{1,0:T(8,128)S(1)}, f32[]{:T(128)}, f32[140,512]{1,0:T(8,128)}) fusion(f32[140,512]{1,0:T(8,128)S(1)} %copy-done.26, f32[140,512]{1,0:T(8,128)S(1)} %copy-done.18, f32[139,512]{1,0:T(8,128)S(1)} %bitcast.24, f32[1,512]{1,0:T(1,128)} %copy-done.47, f32[140,512]{1,0:T(8,128)S(1)} %copy-done.27, ...), kind=kLoop, calls=%fused_computation.59 | loop fusion | flops 931839 | bytes 2293764 | tf_op jit(solution)/shard_map/sub | solution.py:117
  21.4 5.2 %fusion.48 = (f32[140,512]{1,0:T(8,128)}, f32[140,8,512]{2,1,0:T(8,128)}, f32[140,8,512]{2,1,0:T(8,128)S(1)}, f32[8,512]{1,0:T(8,128)}) fusion(f32[140,8,512]{2,1,0:T(8,128)S(1)} %copy-done.9, f32[140,8,512]{2,1,0:T(8,128)S(1)} %copy-done.4, f32[139,8,512]{2,1,0:T(8,128)S(1)} %slice-done, f32[1,8,512]{2,1,0:T(8,128)} %collective-permute-done, ...), kind=kLoop, calls=%fused_computation.88 | loop fusion | flops 10246144 | bytes 15548976 | tf_op jit(solution)/shard_map/reduce_sum | solution.py:123
  26.6 1.3 %multiply_reduce_fusion.1 = f32[]{:T(128)} fusion(f32[140,8,512]{2,1,0:T(8,128)S(1)} %get-tuple-element.29, f32[140,8,512]{2,1,0:T(8,128)S(1)} %copy-done.9), kind=kLoop, calls=%fused_computation.26 | loop fusion | flops 1720319 | bytes 4587524 | tf_op jit(solution)/shard_map/reduce_sum | solution.py:99
  30.8 1.0 collective-permute-done.2
  32.5 1.5 %collective-permute-start.3 = (f32[16,512]{1,0:T(8,128)S(1)}, f32[16,512]{1,0:T(8,128)S(1)}, u32[]{:S(2)}, u32[]{:S(2)}) collective-permute-start(f32[16,512]{1,0:T(8,128)S(1)} %pad_maximum_fusion), channel_id=1, source_target_pairs={{0,2},{2,0},{4,6},{6,4},{8,10},{10,8},{12,14},{14,12},{16,18},{18,... | collective-permute-start | bytes 98312 | tf_op jit(solution)/shard_map/ppermute | solution.py:28
  34.0 2.4 %collective-permute-done.3 = f32[16,512]{1,0:T(8,128)S(1)} collective-permute-done((f32[16,512]{1,0:T(8,128)S(1)}, f32[16,512]{1,0:T(8,128)S(1)}, u32[]{:S(2)}, u32[]{:S(2)}) %collective-permute-start.3) | collective-permute-done | bytes 32800 | tf_op jit(solution)/shard_map/ppermute | solution.py:28
  36.4 0.7 fusion.40
  37.2 1.5 %collective-permute-start.4 = (f32[16,512]{1,0:T(8,128)S(1)}, f32[16,512]{1,0:T(8,128)S(1)}, u32[]{:S(2)}, u32[]{:S(2)}) collective-permute-start(f32[16,512]{1,0:T(8,128)S(1)} %fusion.40), channel_id=1, source_target_pairs={{0,4},{2,6},{4,0},{6,2},{8,12},{10,14},{12,8},{14,10},{16,20},{18,... | collective-permute-start | bytes 98312 | tf_op jit(solution)/shard_map/ppermute | solution.py:28
  38.7 2.4 %collective-permute-done.4 = f32[16,512]{1,0:T(8,128)S(1)} collective-permute-done((f32[16,512]{1,0:T(8,128)S(1)}, f32[16,512]{1,0:T(8,128)S(1)}, u32[]{:S(2)}, u32[]{:S(2)}) %collective-permute-start.4) | collective-permute-done | bytes 32800 | tf_op jit(solution)/shard_map/ppermute | solution.py:28
  41.1 1.6 %collective-permute-start.5 = (f32[16,512]{1,0:T(8,128)S(1)}, f32[16,512]{1,0:T(8,128)S(1)}, u32[]{:S(2)}, u32[]{:S(2)}) collective-permute-start(f32[16,512]{1,0:T(8,128)S(1)} %add.179), channel_id=1, source_target_pairs={{0,8},{2,10},{4,12},{6,14},{8,0},{10,2},{12,4},{14,6},{16,24},{18,... | collective-permute-start | bytes 98312 | tf_op jit(solution)/shard_map/ppermute | solution.py:28
  42.7 2.4 %all_gather.13 = f32[140,1024]{1,0:T(8,128)S(1)} all-gather(f32[140,512]{1,0:T(8,128)} %get-tuple-element.41), channel_id=1, replica_groups=mesh['hour'=16,'region'=2] {'region'}, dimensions={1}, use_global_device_ids=true | all-gather | bytes 860160 | tf_op jit(solution)/shard_map/all_gather | solution.py:125
  45.2 4.4 %collective-permute-start.9 = (f32[1,512]{1,0:T(1,128)S(1)}, f32[1,512]{1,0:T(1,128)S(1)}, u32[]{:S(2)}, u32[]{:S(2)}) collective-permute-start(f32[1,512]{1,0:T(1,128)S(1)} %slice.87), channel_id=1, source_target_pairs={{2,0},{4,2},{6,4},{8,6},{10,8},{12,10},{14,12},{16,14},{18,16},{20... | collective-permute-start | bytes 6152 | tf_op jit(solution)/shard_map/ppermute | solution.py:20
  49.6 2.3 %fusion.51 = f32[140,512]{1,0:T(8,128)S(1)} fusion(f32[140,1024]{1,0:T(8,128)S(1)} %all_gather.13, f32[512,1024]{1,0:T(8,128)S(1)} %bitcast_multiply_fusion), kind=kOutput, calls=%fused_computation.90 | convolution fusion | flops 880803840 | bytes 2957312 | tf_op jit(solution)/shard_map/dot_general | solution.py:75
  52.3 1.3 %collective-permute-start.7 = (f32[1,8,512]{2,1,0:T(8,128)S(1)}, f32[1,8,512]{2,1,0:T(8,128)S(1)}, u32[]{:S(2)}, u32[]{:S(2)}) collective-permute-start(f32[1,8,512]{2,1,0:T(8,128)S(1)} %slice.83), channel_id=1, source_target_pairs={{2,0},{4,2},{6,4},{8,6},{10,8},{12,10},{14,12},{16,14},{18,16},{20... | collective-permute-start | bytes 49160 | tf_op jit(solution)/shard_map/ppermute | solution.py:20
  53.7 0.7 collective-permute-done.6
  56.0 1.6 %multiply_reduce_fusion.3 = (f32[]{:T(128)}, f32[140,512]{1,0:T(8,128)}, f32[140,512]{1,0:T(8,128)S(1)}, f32[140,512]{1,0:T(8,128)S(1)}) fusion(f32[140,512]{1,0:T(8,128)S(1)} %copy-done.23, f32[140,512]{1,0:T(8,128)S(1)} %copy-done.19, f32[140,512]{1,0:T(8,128)S(1)} %copy-done.28, f32[140,512]{1,0:T(8,128)S(1)} %copy-done.22, ...), kind=kLoop, calls=%fused_computation.56 | loop fusion | flops 1361919 | bytes 3441208 | tf_op jit(solution)/shard_map/reduce_sum | solution.py:101
  57.7 2.2 %all_gather.14 = f32[140,1024]{1,0:T(8,128)S(1)} all-gather(f32[140,512]{1,0:T(8,128)S(1)} %get-tuple-element.22), channel_id=1, replica_groups=mesh['hour'=16,'region'=2] {'region'}, dimensions={1}, use_global_device_ids=true | all-gather | bytes 860160 | tf_op jit(solution)/shard_map/all_gather | solution.py:94
  59.9 2.8 %add_reduce_fusion = (f32[8,512]{1,0:T(8,128)}, f32[140,8,512]{2,1,0:T(8,128)S(1)}, f32[140,8,512]{2,1,0:T(8,128)S(1)}) fusion(bf16[140,8,512]{2,1,0:T(8,128)(2,1)S(1)} %copy-done.8, f32[8,512]{1,0:T(8,128)S(1)} %copy-done.37, f32[140]{0:T(256)S(1)} %copy-done.44, f32[8,512]{1,0:T(8,128)S(1)} %convert_element_type.21, f32[140,8,512]{2,1,0:T(8,128)S(1)} %copy-done.11, ...), kind=kLoop, calls=%fused_computation.23 | loop fusion | flops 10317824 | bytes 14991924 | tf_op jit(solution)/shard_map/reduce_sum | solution.py:104
  62.8 1.3 %collective-permute-start.8 = (f32[1,8,512]{2,1,0:T(8,128)S(1)}, f32[1,8,512]{2,1,0:T(8,128)S(1)}, u32[]{:S(2)}, u32[]{:S(2)}) collective-permute-start(f32[1,8,512]{2,1,0:T(8,128)S(1)} %slice.84), channel_id=1, source_target_pairs={{30,0},{0,2},{2,4},{4,6},{6,8},{8,10},{10,12},{12,14},{14,16},{16,... | collective-permute-start | bytes 49160 | tf_op jit(solution)/shard_map/ppermute | solution.py:20
  64.1 3.8 %multiply_subtract_fusion.3 = (f32[140,512]{1,0:T(8,128)}, f32[]{:T(128)}, f32[140,512]{1,0:T(8,128)}) fusion(f32[140,512]{1,0:T(8,128)S(1)} %copy-done.33, f32[140,1024]{1,0:T(8,128)S(1)} %all_gather.14, f32[512,1024]{1,0:T(8,128)S(1)} %bitcast_multiply_fusion), kind=kOutput, calls=%fused_computation.53 | convolution fusion | flops 881305600 | bytes 3530756 | tf_op jit(solution)/shard_map/dot_general | solution.py:75
  68.1 0.7 copy-done.15
  68.8 0.8 multiply_subtract_fusion.2
  69.7 0.8 multiply_reduce_fusion.2
  70.5 3.4 %multiply_reduce_fusion = (f32[]{:T(128)}, f32[140,8,512]{2,1,0:T(8,128)}) fusion(f32[140,8,512]{2,1,0:T(8,128)S(1)} %copy-done.1, f32[140,8,512]{2,1,0:T(8,128)S(1)} %get-tuple-element.18, f32[139,8,512]{2,1,0:T(8,128)S(1)} %slice.85, f32[1,8,512]{2,1,0:T(8,128)S(1)} %collective-permute-done.8, f32[140,8,512]{2,1,0:T(8,128)S(1)} %get-tuple-element.17, ...), kind=kLoop, calls=%fused_computation.22 | loop fusion | flops 6307839 | bytes 11771908 | tf_op jit(solution)/shard_map/reduce_sum | solution.py:99
  76.5 1.2 %collective-permute-done.11 = f32[8,512]{1,0:T(8,128)S(1)} collective-permute-done((f32[8,512]{1,0:T(8,128)S(1)}, f32[8,512]{1,0:T(8,128)S(1)}, u32[]{:S(2)}, u32[]{:S(2)}) %collective-permute-start.11) | collective-permute-done | bytes 16416 | tf_op jit(solution)/shard_map/ppermute | solution.py:28
  78.4 1.5 %collective-permute-start.12 = (f32[16,512]{1,0:T(8,128)S(1)}, f32[16,512]{1,0:T(8,128)S(1)}, u32[]{:S(2)}, u32[]{:S(2)}) collective-permute-start(f32[16,512]{1,0:T(8,128)S(1)} %pad_maximum_fusion.1), channel_id=1, source_target_pairs={{0,2},{2,0},{4,6},{6,4},{8,10},{10,8},{12,14},{14,12},{16,18},{18,... | collective-permute-start | bytes 98312 | tf_op jit(solution)/shard_map/ppermute | solution.py:28
  79.9 2.4 %collective-permute-done.12 = f32[16,512]{1,0:T(8,128)S(1)} collective-permute-done((f32[16,512]{1,0:T(8,128)S(1)}, f32[16,512]{1,0:T(8,128)S(1)}, u32[]{:S(2)}, u32[]{:S(2)}) %collective-permute-start.12) | collective-permute-done | bytes 32800 | tf_op jit(solution)/shard_map/ppermute | solution.py:28
  82.3 0.7 fusion.39
  83.0 1.7 %collective-permute-start.13 = (f32[16,512]{1,0:T(8,128)S(1)}, f32[16,512]{1,0:T(8,128)S(1)}, u32[]{:S(2)}, u32[]{:S(2)}) collective-permute-start(f32[16,512]{1,0:T(8,128)S(1)} %fusion.39), channel_id=1, source_target_pairs={{0,4},{2,6},{4,0},{6,2},{8,12},{10,14},{12,8},{14,10},{16,20},{18,... | collective-permute-start | bytes 98312 | tf_op jit(solution)/shard_map/ppermute | solution.py:28
  84.7 2.2 %collective-permute-done.13 = f32[16,512]{1,0:T(8,128)S(1)} collective-permute-done((f32[16,512]{1,0:T(8,128)S(1)}, f32[16,512]{1,0:T(8,128)S(1)}, u32[]{:S(2)}, u32[]{:S(2)}) %collective-permute-start.13) | collective-permute-done | bytes 32800 | tf_op jit(solution)/shard_map/ppermute | solution.py:28
  86.9 1.5 %collective-permute-start.14 = (f32[16,512]{1,0:T(8,128)S(1)}, f32[16,512]{1,0:T(8,128)S(1)}, u32[]{:S(2)}, u32[]{:S(2)}) collective-permute-start(f32[16,512]{1,0:T(8,128)S(1)} %add.201), channel_id=1, source_target_pairs={{0,8},{2,10},{4,12},{6,14},{8,0},{10,2},{12,4},{14,6},{16,24},{18,... | collective-permute-start | bytes 98312 | tf_op jit(solution)/shard_map/ppermute | solution.py:28
  88.4 2.4 %collective-permute-done.14 = f32[16,512]{1,0:T(8,128)S(1)} collective-permute-done((f32[16,512]{1,0:T(8,128)S(1)}, f32[16,512]{1,0:T(8,128)S(1)}, u32[]{:S(2)}, u32[]{:S(2)}) %collective-permute-start.14) | collective-permute-done | bytes 32800 | tf_op jit(solution)/shard_map/ppermute | solution.py:28
  90.8 2.2 %collective-permute-start.15 = (f32[16,512]{1,0:T(8,128)S(1)}, f32[16,512]{1,0:T(8,128)S(1)}, u32[]{:S(2)}, u32[]{:S(2)}) collective-permute-start(f32[16,512]{1,0:T(8,128)S(1)} %add.202), channel_id=1, source_target_pairs={{0,16},{2,18},{4,20},{6,22},{8,24},{10,26},{12,28},{14,30},{16,0},... | collective-permute-start | bytes 98312 | tf_op jit(solution)/shard_map/ppermute | solution.py:28
  93.1 2.4 %all_gather.15 = f32[140,1024]{1,0:T(8,128)S(1)} all-gather(f32[140,512]{1,0:T(8,128)} %get-tuple-element.39), channel_id=1, replica_groups=mesh['hour'=16,'region'=2] {'region'}, dimensions={1}, use_global_device_ids=true | all-gather | bytes 860160 | tf_op jit(solution)/shard_map/all_gather | solution.py:125
  96.2 1.4 %fusion.41 = (f32[8,512]{1,0:T(8,128)S(1)}, f32[8,512]{1,0:T(8,128)S(1)}, f32[8,512]{1,0:T(8,128)}) fusion(f32[8,512]{1,0:T(8,128)} %param.23, f32[8,512]{1,0:T(8,128)} %param.31, f32[8,512]{1,0:T(8,128)} %param.22, f32[16,512]{1,0:T(8,128)} %copy-done.38, f32[16,512]{1,0:T(8,128)S(1)} %add.203), kind=kLoop, calls=%fused_computation.87 | loop fusion | flops 53248 | bytes 131072 | tf_op jit(solution)/shard_map/mul | solution.py:133
  98.3 5.2 %add_maximum_fusion = (f32[140,8,512]{2,1,0:T(8,128)}, f32[140,8,512]{2,1,0:T(8,128)S(1)}) fusion(f32[140,8,512]{2,1,0:T(8,128)} %copy-done.6, bf16[140,8,512]{2,1,0:T(8,128)(2,1)S(1)} %copy-done.8, f32[8,512]{1,0:T(8,128)S(1)} %get-tuple-element.10, f32[]{:T(128)} %bitcast.4, f32[140]{0:T(256)} %copy-done.43, f32[8,512]{1,0:T(8,128)S(1)} %convert_element_type.21, ...), kind=kLoop, calls=%fused_computation.20 | loop fusion | flops 5734400 | bytes 12649012 | tf_op jit(solution)/shard_map/max | solution.py:129
  103.5 4.5 %collective-permute-start.17 = (f32[1,8,512]{2,1,0:T(8,128)S(1)}, f32[1,8,512]{2,1,0:T(8,128)S(1)}, u32[]{:S(2)}, u32[]{:S(2)}) collective-permute-start(f32[1,8,512]{2,1,0:T(8,128)S(1)} %slice.95), channel_id=1, source_target_pairs={{2,0},{4,2},{6,4},{8,6},{10,8},{12,10},{14,12},{16,14},{18,16},{20... | collective-permute-start | bytes 49160 | tf_op jit(solution)/shard_map/ppermute | solution.py:20
  108.0 2.3 %fusion.52 = f32[140,512]{1,0:T(8,128)S(1)} fusion(f32[140,1024]{1,0:T(8,128)S(1)} %all_gather.15, f32[512,1024]{1,0:T(8,128)S(1)} %bitcast_multiply_fusion), kind=kOutput, calls=%fused_computation.91 | convolution fusion | flops 880803840 | bytes 2957312 | tf_op jit(solution)/shard_map/dot_general | solution.py:75
  110.4 2.1 %collective-permute-start.16 = (f32[1,512]{1,0:T(1,128)S(1)}, f32[1,512]{1,0:T(1,128)S(1)}, u32[]{:S(2)}, u32[]{:S(2)}) collective-permute-start(f32[1,512]{1,0:T(1,128)S(1)} %slice.93), channel_id=1, source_target_pairs={{2,0},{4,2},{6,4},{8,6},{10,8},{12,10},{14,12},{16,14},{18,16},{20... | collective-permute-start | bytes 6152 | tf_op jit(solution)/shard_map/ppermute | solution.py:20
  112.8 2.3 %fusion.15 = (f32[140,8,512]{2,1,0:T(8,128)}, f32[140,512]{1,0:T(8,128)S(1)}) fusion(f32[140,8,512]{2,1,0:T(8,128)S(1)} %copy-done.3, f32[140,8,512]{2,1,0:T(8,128)S(1)} %get-tuple-element.13, f32[1,8,512]{2,1,0:T(8,128)S(1)} %collective-permute-done.17, f32[139,8,512]{2,1,0:T(8,128)S(1)} %slice.94, f32[8,512]{1,0:T(8,128)S(1)} %get-tuple-element.9, f32[]{:T(128)} %bitcast.4), kind=kLoop, calls=%fused_computation.19 | loop fusion | flops 3942400 | bytes 9478148 | tf_op jit(solution)/shard_map/max | solution.py:132
  115.1 1.0 fusion.30
  (143 shorter events, 7.7 us)
Async XLA Ops:
  1.4 16.0 %collective-permute-start.1 = (f32[1,512]{1,0:T(1,128)S(1)}, f32[1,512]{1,0:T(1,128)S(1)}, u32[]{:S(2)}, u32[]{:S(2)}) collective-permute-start(f32[1,512]{1,0:T(1,128)S(1)} %slice.62), channel_id=1, source_target_pairs={{30,0},{0,2},{2,4},{4,6},{6,8},{8,10},{10,12},{12,14},{14,16},{16,... | collective-permute-start | bytes 6152 | tf_op jit(solution)/shard_map/ppermute | solution.py:20
  5.6 15.7 %collective-permute-start = (f32[1,8,512]{2,1,0:T(8,128)}, f32[1,8,512]{2,1,0:T(8,128)}, u32[]{:S(2)}, u32[]{:S(2)}) collective-permute-start(f32[1,8,512]{2,1,0:T(8,128)} %slice.60), channel_id=1, source_target_pairs={{30,0},{0,2},{2,4},{4,6},{6,8},{8,10},{10,12},{12,14},{14,16},{16,... | collective-permute-start | bytes 49160 | tf_op jit(solution)/shard_map/ppermute | solution.py:20
  11.8 6.2 %copy-start.26 = (f32[140,512]{1,0:T(8,128)S(1)}, f32[140,512]{1,0:T(8,128)}, u32[]{:S(2)}) copy-start(f32[140,512]{1,0:T(8,128)} %param.29) | copy-start | bytes 860164
  11.8 6.2 %copy-start.27 = (f32[140,512]{1,0:T(8,128)S(1)}, f32[140,512]{1,0:T(8,128)}, u32[]{:S(2)}) copy-start(f32[140,512]{1,0:T(8,128)} %param.30) | copy-start | bytes 860164
  12.8 5.2 %copy-start.16 = (f32[140,512]{1,0:T(8,128)S(1)}, f32[140,512]{1,0:T(8,128)}, u32[]{:S(2)}) copy-start(f32[140,512]{1,0:T(8,128)} %param.32) | copy-start | bytes 860164
  12.8 5.2 %copy-start.18 = (f32[140,512]{1,0:T(8,128)S(1)}, f32[140,512]{1,0:T(8,128)}, u32[]{:S(2)}) copy-start(f32[140,512]{1,0:T(8,128)} %param.33) | copy-start | bytes 860164
  12.8 8.6 %copy-start.9 = (f32[140,8,512]{2,1,0:T(8,128)S(1)}, f32[140,8,512]{2,1,0:T(8,128)}, u32[]{:S(2)}) copy-start(f32[140,8,512]{2,1,0:T(8,128)} %param.27) | copy-start | bytes 6881284
  12.8 8.6 %copy-start.10 = (f32[140,8,512]{2,1,0:T(8,128)S(1)}, f32[140,8,512]{2,1,0:T(8,128)}, u32[]{:S(2)}) copy-start(f32[140,8,512]{2,1,0:T(8,128)} %param.34) | copy-start | bytes 6881284
  16.7 4.7 %copy-start.43 = (f32[140]{0:T(256)}, f32[140]{0:T(256)S(1)}, u32[]{:S(2)}) copy-start(f32[140]{0:T(256)S(1)} %compare_convert_fusion) | copy-start | bytes 1684
  16.7 4.7 %copy-start.4 = (f32[140,8,512]{2,1,0:T(8,128)S(1)}, f32[140,8,512]{2,1,0:T(8,128)}, u32[]{:S(2)}) copy-start(f32[140,8,512]{2,1,0:T(8,128)} %param.35) | copy-start | bytes 6881284
  16.7 4.7 %copy-start.8 = (bf16[140,8,512]{2,1,0:T(8,128)(2,1)S(1)}, bf16[140,8,512]{2,1,0:T(8,128)(2,1)}, u32[]{:S(2)}) copy-start(bf16[140,8,512]{2,1,0:T(8,128)(2,1)} %param.19) | copy-start | bytes 3440644
  17.4 4.0 %slice-start = ((f32[140,8,512]{2,1,0:T(8,128)}), f32[139,8,512]{2,1,0:T(8,128)S(1)}, s32[]{:S(2)}) async-start(f32[140,8,512]{2,1,0:T(8,128)} %param.35), calls=%async_computation | async-start | bytes 4554752 | tf_op jit(solution)/shard_map/slice | solution.py:85
  17.4 4.0 %copy-start.36 = (f32[8,512]{1,0:T(8,128)S(1)}, f32[8,512]{1,0:T(8,128)}, u32[]{:S(2)}) copy-start(f32[8,512]{1,0:T(8,128)} %param.23) | copy-start | bytes 49156
  17.4 4.0 %copy-start.41 = (f32[8,512]{1,0:T(8,128)S(1)}, f32[8,512]{1,0:T(8,128)}, u32[]{:S(2)}) copy-start(f32[8,512]{1,0:T(8,128)} %param.21) | copy-start | bytes 49156
  20.6 31.3 %copy-start.21 = (f32[140,512]{1,0:T(8,128)}, f32[140,512]{1,0:T(8,128)S(1)}, u32[]{:S(2)}) copy-start(f32[140,512]{1,0:T(8,128)S(1)} %get-tuple-element.25) | copy-start | bytes 860164
  30.6 1.2 %collective-permute-start.2 = (f32[8,512]{1,0:T(8,128)S(1)}, f32[8,512]{1,0:T(8,128)S(1)}, u32[]{:S(2)}, u32[]{:S(2)}) collective-permute-start(f32[8,512]{1,0:T(8,128)S(1)} %broadcast_in_dim.10), channel_id=1, source_target_pairs={{0,1},{1,0},{2,3},{3,2},{4,5},{5,4},{6,7},{7,6},{8,9},{9,8},{10,11... | collective-permute-start | bytes 49160 | tf_op jit(solution)/shard_map/ppermute | solution.py:28
  32.5 3.9 %collective-permute-start.3 = (f32[16,512]{1,0:T(8,128)S(1)}, f32[16,512]{1,0:T(8,128)S(1)}, u32[]{:S(2)}, u32[]{:S(2)}) collective-permute-start(f32[16,512]{1,0:T(8,128)S(1)} %pad_maximum_fusion), channel_id=1, source_target_pairs={{0,2},{2,0},{4,6},{6,4},{8,10},{10,8},{12,14},{14,12},{16,18},{18,... | collective-permute-start | bytes 98312 | tf_op jit(solution)/shard_map/ppermute | solution.py:28
  37.2 3.9 %collective-permute-start.4 = (f32[16,512]{1,0:T(8,128)S(1)}, f32[16,512]{1,0:T(8,128)S(1)}, u32[]{:S(2)}, u32[]{:S(2)}) collective-permute-start(f32[16,512]{1,0:T(8,128)S(1)} %fusion.40), channel_id=1, source_target_pairs={{0,4},{2,6},{4,0},{6,2},{8,12},{10,14},{12,8},{14,10},{16,20},{18,... | collective-permute-start | bytes 98312 | tf_op jit(solution)/shard_map/ppermute | solution.py:28
  41.1 10.9 %copy-start.7 = (f32[140,8,512]{2,1,0:T(8,128)S(1)}, f32[140,8,512]{2,1,0:T(8,128)}, u32[]{:S(2)}) copy-start(f32[140,8,512]{2,1,0:T(8,128)} %get-tuple-element.28) | copy-start | bytes 6881284
  41.1 8.4 %collective-permute-start.5 = (f32[16,512]{1,0:T(8,128)S(1)}, f32[16,512]{1,0:T(8,128)S(1)}, u32[]{:S(2)}, u32[]{:S(2)}) collective-permute-start(f32[16,512]{1,0:T(8,128)S(1)} %add.179), channel_id=1, source_target_pairs={{0,8},{2,10},{4,12},{6,14},{8,0},{10,2},{12,4},{14,6},{16,24},{18,... | collective-permute-start | bytes 98312 | tf_op jit(solution)/shard_map/ppermute | solution.py:28
  45.2 10.8 %collective-permute-start.9 = (f32[1,512]{1,0:T(1,128)S(1)}, f32[1,512]{1,0:T(1,128)S(1)}, u32[]{:S(2)}, u32[]{:S(2)}) collective-permute-start(f32[1,512]{1,0:T(1,128)S(1)} %slice.87), channel_id=1, source_target_pairs={{2,0},{4,2},{6,4},{8,6},{10,8},{12,10},{14,12},{16,14},{18,16},{20... | collective-permute-start | bytes 6152 | tf_op jit(solution)/shard_map/ppermute | solution.py:20
  49.5 4.9 %collective-permute-start.6 = (f32[16,512]{1,0:T(8,128)S(1)}, f32[16,512]{1,0:T(8,128)S(1)}, u32[]{:S(2)}, u32[]{:S(2)}) collective-permute-start(f32[16,512]{1,0:T(8,128)S(1)} %add.180), channel_id=1, source_target_pairs={{0,16},{2,18},{4,20},{6,22},{8,24},{10,26},{12,28},{14,30},{16,0},... | collective-permute-start | bytes 98312 | tf_op jit(solution)/shard_map/ppermute | solution.py:28
  52.0 3.9 %copy-start.17 = (f32[140,512]{1,0:T(8,128)S(1)}, f32[140,512]{1,0:T(8,128)}, u32[]{:S(2)}) copy-start(f32[140,512]{1,0:T(8,128)} %param.32) | copy-start | bytes 860164
  52.0 3.9 %copy-start.19 = (f32[140,512]{1,0:T(8,128)S(1)}, f32[140,512]{1,0:T(8,128)}, u32[]{:S(2)}) copy-start(f32[140,512]{1,0:T(8,128)} %param.33) | copy-start | bytes 860164
  52.0 3.9 %copy-start.22 = (f32[140,512]{1,0:T(8,128)S(1)}, f32[140,512]{1,0:T(8,128)}, u32[]{:S(2)}) copy-start(f32[140,512]{1,0:T(8,128)} %copy-done.21) | copy-start | bytes 860164
  52.0 3.9 %copy-start.23 = (f32[140,512]{1,0:T(8,128)S(1)}, f32[140,512]{1,0:T(8,128)}, u32[]{:S(2)}) copy-start(f32[140,512]{1,0:T(8,128)} %get-tuple-element.44) | copy-start | bytes 860164
  52.0 3.9 %copy-start.28 = (f32[140,512]{1,0:T(8,128)S(1)}, f32[140,512]{1,0:T(8,128)}, u32[]{:S(2)}) copy-start(f32[140,512]{1,0:T(8,128)} %param.30) | copy-start | bytes 860164
  52.3 5.3 %copy-start.37 = (f32[8,512]{1,0:T(8,128)S(1)}, f32[8,512]{1,0:T(8,128)}, u32[]{:S(2)}) copy-start(f32[8,512]{1,0:T(8,128)} %param.23) | copy-start | bytes 49156
  52.3 5.3 %copy-start.39 = (f32[8,512]{1,0:T(8,128)S(1)}, f32[8,512]{1,0:T(8,128)}, u32[]{:S(2)}) copy-start(f32[8,512]{1,0:T(8,128)} %param.31) | copy-start | bytes 49156
  52.3 5.3 %copy-start.40 = (f32[8,512]{1,0:T(8,128)S(1)}, f32[8,512]{1,0:T(8,128)}, u32[]{:S(2)}) copy-start(f32[8,512]{1,0:T(8,128)} %param.22) | copy-start | bytes 49156
  52.3 7.6 %collective-permute-start.7 = (f32[1,8,512]{2,1,0:T(8,128)S(1)}, f32[1,8,512]{2,1,0:T(8,128)S(1)}, u32[]{:S(2)}, u32[]{:S(2)}) collective-permute-start(f32[1,8,512]{2,1,0:T(8,128)S(1)} %slice.83), channel_id=1, source_target_pairs={{2,0},{4,2},{6,4},{8,6},{10,8},{12,10},{14,12},{16,14},{18,16},{20... | collective-permute-start | bytes 49160 | tf_op jit(solution)/shard_map/ppermute | solution.py:20
  54.4 5.5 %copy-start.11 = (f32[140,8,512]{2,1,0:T(8,128)S(1)}, f32[140,8,512]{2,1,0:T(8,128)}, u32[]{:S(2)}) copy-start(f32[140,8,512]{2,1,0:T(8,128)} %param.34) | copy-start | bytes 6881284
  54.4 8.3 %copy-start.38 = (f32[16,512]{1,0:T(8,128)}, f32[16,512]{1,0:T(8,128)S(1)}, u32[]{:S(2)}) copy-start(f32[16,512]{1,0:T(8,128)S(1)} %add.181) | copy-start | bytes 98308
  54.4 5.5 %copy-start.5 = (f32[140,8,512]{2,1,0:T(8,128)S(1)}, f32[140,8,512]{2,1,0:T(8,128)}, u32[]{:S(2)}) copy-start(f32[140,8,512]{2,1,0:T(8,128)} %param.35) | copy-start | bytes 6881284
  57.6 12.8 %copy-start.12 = (f32[140,512]{1,0:T(8,128)}, f32[140,512]{1,0:T(8,128)S(1)}, u32[]{:S(2)}) copy-start(f32[140,512]{1,0:T(8,128)S(1)} %get-tuple-element.22) | copy-start | bytes 860164
  57.6 10.5 %collective-permute-start.10 = (f32[1,512]{1,0:T(1,128)S(1)}, f32[1,512]{1,0:T(1,128)S(1)}, u32[]{:S(2)}, u32[]{:S(2)}) collective-permute-start(f32[1,512]{1,0:T(1,128)S(1)} %slice.88), channel_id=1, source_target_pairs={{30,0},{0,2},{2,4},{4,6},{6,8},{8,10},{10,12},{12,14},{14,16},{16,... | collective-permute-start | bytes 6152 | tf_op jit(solution)/shard_map/ppermute | solution.py:20
  59.9 4.2 %copy-start.33 = (f32[140,512]{1,0:T(8,128)S(1)}, f32[140,512]{1,0:T(8,128)}, u32[]{:S(2)}) copy-start(f32[140,512]{1,0:T(8,128)} %get-tuple-element.45) | copy-start | bytes 860164
  62.8 7.7 %copy-start.2 = (f32[140,8,512]{2,1,0:T(8,128)}, f32[140,8,512]{2,1,0:T(8,128)S(1)}, u32[]{:S(2)}) copy-start(f32[140,8,512]{2,1,0:T(8,128)S(1)} %get-tuple-element.18) | copy-start | bytes 6881284
  62.8 7.7 %copy-start.6 = (f32[140,8,512]{2,1,0:T(8,128)}, f32[140,8,512]{2,1,0:T(8,128)S(1)}, u32[]{:S(2)}) copy-start(f32[140,8,512]{2,1,0:T(8,128)S(1)} %get-tuple-element.17) | copy-start | bytes 6881284
  62.8 7.7 %collective-permute-start.8 = (f32[1,8,512]{2,1,0:T(8,128)S(1)}, f32[1,8,512]{2,1,0:T(8,128)S(1)}, u32[]{:S(2)}, u32[]{:S(2)}) collective-permute-start(f32[1,8,512]{2,1,0:T(8,128)S(1)} %slice.84), channel_id=1, source_target_pairs={{30,0},{0,2},{2,4},{4,6},{6,8},{8,10},{10,12},{12,14},{14,16},{16,... | collective-permute-start | bytes 49160 | tf_op jit(solution)/shard_map/ppermute | solution.py:20
  76.4 1.2 %collective-permute-start.11 = (f32[8,512]{1,0:T(8,128)S(1)}, f32[8,512]{1,0:T(8,128)S(1)}, u32[]{:S(2)}, u32[]{:S(2)}) collective-permute-start(f32[8,512]{1,0:T(8,128)S(1)} %broadcast_in_dim.11), channel_id=1, source_target_pairs={{0,1},{1,0},{2,3},{3,2},{4,5},{5,4},{6,7},{7,6},{8,9},{9,8},{10,11... | collective-permute-start | bytes 49160 | tf_op jit(solution)/shard_map/ppermute | solution.py:28
  78.4 3.9 %collective-permute-start.12 = (f32[16,512]{1,0:T(8,128)S(1)}, f32[16,512]{1,0:T(8,128)S(1)}, u32[]{:S(2)}, u32[]{:S(2)}) collective-permute-start(f32[16,512]{1,0:T(8,128)S(1)} %pad_maximum_fusion.1), channel_id=1, source_target_pairs={{0,2},{2,0},{4,6},{6,4},{8,10},{10,8},{12,14},{14,12},{16,18},{18,... | collective-permute-start | bytes 98312 | tf_op jit(solution)/shard_map/ppermute | solution.py:28
  83.0 3.9 %collective-permute-start.13 = (f32[16,512]{1,0:T(8,128)S(1)}, f32[16,512]{1,0:T(8,128)S(1)}, u32[]{:S(2)}, u32[]{:S(2)}) collective-permute-start(f32[16,512]{1,0:T(8,128)S(1)} %fusion.39), channel_id=1, source_target_pairs={{0,4},{2,6},{4,0},{6,2},{8,12},{10,14},{12,8},{14,10},{16,20},{18,... | collective-permute-start | bytes 98312 | tf_op jit(solution)/shard_map/ppermute | solution.py:28
  86.9 3.9 %collective-permute-start.14 = (f32[16,512]{1,0:T(8,128)S(1)}, f32[16,512]{1,0:T(8,128)S(1)}, u32[]{:S(2)}, u32[]{:S(2)}) collective-permute-start(f32[16,512]{1,0:T(8,128)S(1)} %add.201), channel_id=1, source_target_pairs={{0,8},{2,10},{4,12},{6,14},{8,0},{10,2},{12,4},{14,6},{16,24},{18,... | collective-permute-start | bytes 98312 | tf_op jit(solution)/shard_map/ppermute | solution.py:28
  90.8 4.8 %collective-permute-start.15 = (f32[16,512]{1,0:T(8,128)S(1)}, f32[16,512]{1,0:T(8,128)S(1)}, u32[]{:S(2)}, u32[]{:S(2)}) collective-permute-start(f32[16,512]{1,0:T(8,128)S(1)} %add.202), channel_id=1, source_target_pairs={{0,16},{2,18},{4,20},{6,22},{8,24},{10,26},{12,28},{14,30},{16,0},... | collective-permute-start | bytes 98312 | tf_op jit(solution)/shard_map/ppermute | solution.py:28
  103.5 6.9 %copy-start.20 = (f32[140,512]{1,0:T(8,128)S(1)}, f32[140,512]{1,0:T(8,128)}, u32[]{:S(2)}) copy-start(f32[140,512]{1,0:T(8,128)} %get-tuple-element.14) | copy-start | bytes 860164
  103.5 9.2 %collective-permute-start.17 = (f32[1,8,512]{2,1,0:T(8,128)S(1)}, f32[1,8,512]{2,1,0:T(8,128)S(1)}, u32[]{:S(2)}, u32[]{:S(2)}) collective-permute-start(f32[1,8,512]{2,1,0:T(8,128)S(1)} %slice.95), channel_id=1, source_target_pairs={{2,0},{4,2},{6,4},{8,6},{10,8},{12,10},{14,12},{16,14},{18,16},{20... | collective-permute-start | bytes 49160 | tf_op jit(solution)/shard_map/ppermute | solution.py:20
  110.4 4.7 %collective-permute-start.16 = (f32[1,512]{1,0:T(1,128)S(1)}, f32[1,512]{1,0:T(1,128)S(1)}, u32[]{:S(2)}, u32[]{:S(2)}) collective-permute-start(f32[1,512]{1,0:T(1,128)S(1)} %slice.93), channel_id=1, source_target_pairs={{2,0},{4,2},{6,4},{8,6},{10,8},{12,10},{14,12},{16,14},{18,16},{20... | collective-permute-start | bytes 6152 | tf_op jit(solution)/shard_map/ppermute | solution.py:20
  (19 other events, 38.5 us)

commit v2 on v0

v2 whole, which is shorter than its diff:
```python
import functools

import jax
import jax.numpy as jnp
from jax import lax
from jax.experimental import pallas as pl
from jax.experimental.pallas import tpu as pltpu
from jax.sharding import PartitionSpec as P

BUS = 1024
TECH = 8
BLOCK = 128
ITERS = 2

primal_step = 0.2
capacity_step = 4.0
dual_scale = 0.06

F32 = jnp.float32
VMEM = pl.BlockSpec(memory_space=pltpu.VMEM)
SMEM = pl.BlockSpec(memory_space=pltpu.SMEM)
HBM = pl.BlockSpec(memory_space=pltpu.HBM)


def shifted(block, axis, distance):
    devices = range(lax.axis_size(axis))
    route = [((i - distance) % len(devices), i) for i in devices]
    return lax.ppermute(block, axis, route)


def partner(block, axis, distance):
    return lax.ppermute(block, axis, [(i, i ^ distance) for i in range(lax.axis_size(axis))])


def distances(axis):
    size = lax.axis_size(axis)
    return [1 << i for i in range(size.bit_length() - 1)]


def summed(block, axis):
    for distance in distances(axis):
        block = block + partner(block, axis, distance)
    return block


def after(block, earlier):
    return lax.optimization_barrier((block, earlier))[0]


def divisor(extent, most):
    return max(d for d in range(1, most + 1) if extent % d == 0)


def split(value):
    high = value.astype(jnp.bfloat16)
    return high, (value - high.astype(F32)).astype(jnp.bfloat16)


def network_product(sources, high_ref, low_ref):
    total, at = None, 0
    for source in sources:
        columns = slice(at, at + source.shape[1])
        at += source.shape[1]
        high, low = split(source[...])
        for left, right in ((high, high_ref), (low, high_ref), (high, low_ref)):
            term = lax.dot_general(
                left, right[:, columns], (((1,), (1,)), ((), ())), preferred_element_type=F32
            )
            total = term if total is None else total + term
    return total


def call(body, operands, specs, outs, out_specs=None, scratch=(), flops=1 << 22, moved=1 << 23, room=8, name=None):
    operands = [
        pltpu.with_memory_space_constraint(operand, pltpu.HBM) if spec is HBM else operand
        for operand, spec in zip(operands, specs)
    ]
    return pl.pallas_call(
        body,
        out_shape=[jax.ShapeDtypeStruct(shape, dtype) for shape, dtype in outs],
        in_specs=specs,
        out_specs=out_specs or [VMEM] * len(outs),
        scratch_shapes=list(scratch),
        compiler_params=pltpu.CompilerParams(vmem_limit_bytes=room << 20),
        cost_estimate=pl.CostEstimate(flops=flops, bytes_accessed=moved, transcendentals=0),
        name=name,
    )(*operands)


def load_body(
    swap, gen_h, lim_h, ramp_h, av_h, net_h, mask_h, vc_h, rr_h, bal_h, demand_h, pat_h, live_s,
    bar_ref, new_ref, lim_ref, ramp_ref, avail_ref, high_ref, low_ref, invest_ref, square_ref, load_ref,
    av_v, net_v, mask_v, vc_v, rr_v, bal_v, demand_v, pat_s, sems, net_sem, small_sem,
):
    rows, _, buses = gen_h.shape
    chunk = divisor(rows, 28)
    unroll = divisor(chunk, 7)
    chunks = rows // chunk
    region = lax.axis_index("region")
    pieces = 2 if swap else 1
    width = BUS // pieces

    def network_copy(piece):
        at = pl.multiple_of(lax.rem(region + piece, pieces) * width, BLOCK) if swap else 0
        return pltpu.make_async_copy(
            net_h.at[:, pl.ds(at, width)], net_v.at[:, pl.ds(piece * width, width)], net_sem.at[piece]
        )

    def copies(i):
        rows_here = pl.ds(i * chunk, chunk)
        return [
            pltpu.make_async_copy(source.at[rows_here], target.at[rows_here], sems.at[i, k])
            for k, (source, target) in enumerate(
                ((gen_h, bar_ref), (lim_h, lim_ref), (ramp_h, ramp_ref), (av_h, av_v))
            )
        ]

    small = [
        pltpu.make_async_copy(source, target, small_sem.at[k])
        for k, (source, target) in enumerate(
            ((pat_h, pat_s), (mask_h, mask_v), (vc_h, vc_v), (rr_h, rr_v), (bal_h, bal_v),
             (demand_h, demand_v))
        )
    ]
    for copy in small[:-1]:
        copy.start()
    for piece in range(pieces):
        network_copy(piece).start()
    for i in range(chunks):
        for copy in copies(i):
            copy.start()
    small[-1].start()

    for copy in small[:-1]:
        copy.wait()
    blocks = buses // BLOCK
    shift = region * blocks if swap else 0
    for piece in range(pieces):
        network_copy(piece).wait()
        for i in range(blocks):
            for j in range(piece * width // BLOCK, (piece + 1) * width // BLOCK):
                at = (slice(i * BLOCK, (i + 1) * BLOCK), slice(j * BLOCK, (j + 1) * BLOCK))
                coupled = pat_s[region * blocks + i, lax.rem(j + shift, BUS // BLOCK)].astype(F32)
                high, low = split(net_v[at] * coupled)
                high_ref[at] = high
                low_ref[at] = low

    mask = mask_v[...].astype(F32)
    cost = vc_v[...]
    live = live_s[0] - lax.axis_index("hour") * rows

    def step(t, carry, first=False):
        before, limit_sum, ramp_sum, squares = carry
        gen, lim, ramp = bar_ref[t], lim_ref[t], ramp_ref[t]
        alive = jnp.where(t < live, 1.0, 0.0).astype(F32)
        avail = av_v[t].astype(F32) * mask * alive
        avail_ref[t] = avail
        limit_sum += avail * lim
        ramp_sum += ramp
        if not first:
            dual = jnp.broadcast_to(bal_v[pl.ds(t, 1), :], (TECH, buses))
            new = jnp.maximum(0.0, gen - primal_step * (cost + dual + lim + before - ramp))
            squares += (new - gen) ** 2
            new_ref[t] = new
            bar_ref[t] = 2.0 * new - gen
        return ramp, limit_sum, ramp_sum, squares

    carry = (jnp.zeros((TECH, buses), F32),) * 4
    for i in range(chunks):
        for copy in copies(i):
            copy.wait()
        start = i * chunk
        if i == 0:
            for t in range(unroll):
                carry = step(t, carry, t == 0)
            start = unroll

        def several(j, carry, start=start):
            for k in range(unroll):
                carry = step(start + j * unroll + k, carry)
            return carry

        carry = lax.fori_loop(0, ((i + 1) * chunk - start) // unroll, several, carry)
    _, limit_sum, ramp_sum, squares = carry
    invest_ref[...] = limit_sum + rr_v[...] * ramp_sum
    square_ref[...] = squares
    small[-1].wait()
    row = lax.broadcasted_iota(jnp.int32, (rows, buses), 0)
    load_ref[...] = jnp.where(row < live, demand_v[...], 0.0)


def fold_rows(square):
    rows = square.shape[0]
    full = rows // TECH * TECH
    total = jnp.sum(square[:full].reshape(full // TECH, TECH, square.shape[1]), axis=0)
    return total, square[full:]


def put_totals(out_ref, invest, squares, rows_of_one, cubes):
    buses = invest.shape[1]
    out_ref[:, :buses] = invest
    lone = [jnp.sum(squares, axis=0, keepdims=True), *rows_of_one]
    for i, row in enumerate(lone):
        out_ref[i : i + 1, buses : 2 * buses] = row
    out_ref[len(lone) :, buses : 2 * buses] = jnp.zeros((TECH - len(lone), buses), F32)
    for i, cube in enumerate(cubes):
        out_ref[:, (i + 2) * buses : (i + 3) * buses] = cube


def get_totals(entries, buses, here_ref, squares_ref, other_ref):
    squares = jnp.sum(squares_ref[0:1, buses : 2 * buses] + other_ref[0:1, buses : 2 * buses])
    return here_ref[:, :buses], dual_scale * lax.rsqrt(jnp.full((1, 1), squares / entries + 1e-06, F32))


def neighbour(passed, ahead, index):
    device = lax.axis_index("hour")
    block = passed[0][index]
    for k in range(1, len(passed)):
        low = lax.rem(device, 1 << k)
        differs = low == (1 << k) - 1 if ahead else low == 0
        block = jnp.where(differs, passed[k][index], block)
    return block


def add_squares(total, *terms):
    for term in terms:
        full, rest = fold_rows(term * term)
        total = total + full
        if rest.shape[0]:
            rest = jnp.sum(rest, axis=0, keepdims=True)
            row = lax.broadcasted_iota(jnp.int32, total.shape, 0)
            total = total + jnp.where(row == 0, rest, 0.0)
    return total


def first_body(
    pieces, bar_ref, lim_ref, ramp_ref, halo_ref, vc_ref, invest_ref, square_ref, bal_ref, *refs,
):
    others, refs = refs[: pieces], refs[pieces:]
    (
        ang_ref, pow_ref, lev_ref, sto_ref, high_ref, low_ref,
        row_ref, flow_ref, angbar_ref, pownew_ref, powbar_ref, levnew_ref, levbar_ref,
        total_ref, shift_ref,
    ) = refs
    rows, _, buses = bar_ref.shape
    gen = bar_ref[0]
    dual = jnp.broadcast_to(bal_ref[0:1, :], (TECH, buses))
    new = jnp.maximum(
        0.0, gen - primal_step * (vc_ref[...] + dual + lim_ref[0] + halo_ref[:TECH] - ramp_ref[0])
    )
    row_ref[...] = new
    bal, sto = bal_ref[...], sto_ref[...]
    flow = network_product(others, high_ref, low_ref)
    flow_ref[...] = flow
    ang_step = primal_step * flow
    angbar_ref[...] = ang_ref[...] + 2.0 * ang_step
    pow_old = pow_ref[...]
    pow_new = pow_old - primal_step * (bal + sto)
    pownew_ref[...] = pow_new
    powbar_ref[...] = 2.0 * pow_new - pow_old
    shift_ref[8 : 8 + rows] = sto
    shift_ref[7:8] = halo_ref[TECH : TECH + 1]
    lev_old = lev_ref[...]
    lev_new = jnp.maximum(0.0, lev_old - primal_step * (shift_ref[7 : 7 + rows] - sto))
    levnew_ref[...] = lev_new
    levbar_ref[...] = 2.0 * lev_new - lev_old
    squares = add_squares(
        square_ref[...], new - gen, ang_step, pow_new - pow_old, lev_new - lev_old
    )
    put_totals(
        total_ref, invest_ref[...], squares,
        (levbar_ref[0:1], levbar_ref[rows - 1 : rows], powbar_ref[rows - 1 : rows]),
        (2.0 * new - gen, bar_ref[rows - 1]),
    )


def residual_one_body(
    pieces, bar_ref, total_ref, powbar_ref, load_ref, high_ref, low_ref, *refs,
):
    sources, (out_ref, sum_ref) = refs[:pieces], refs[pieces:]
    rows, _, buses = bar_ref.shape
    unroll = divisor(rows, 7)
    flow = network_product(sources, high_ref, low_ref)

    def several(j, _):
        for k in range(unroll):
            t = j * unroll + k
            sum_ref[pl.ds(t, 1), :] = jnp.sum(bar_ref[t], axis=0, keepdims=True)
        return 0

    lax.fori_loop(0, rows // unroll, several, 0)
    sum_ref[0:1] = jnp.sum(total_ref[:, 2 * buses : 3 * buses], axis=0, keepdims=True)
    out_ref[...] = sum_ref[...] + powbar_ref[...] - flow - load_ref[...]


def product_body(pieces, high_ref, low_ref, *refs):
    refs[pieces][...] = network_product(refs[:pieces], high_ref, low_ref)


def capacity_of(hours, cap_ref, inv_ref, invest):
    return jnp.maximum(0.0, cap_ref[...] - capacity_step * (inv_ref[...] - invest / float(hours)))


def middle_body(
    hours, entries, steps, here_ref, squares_ref, other_ref, mine_ref, *refs,
):
    passed, refs = refs[:steps], refs[steps:]
    (
        cap_ref, inv_ref, rr_ref, vc_ref,
        bar_ref, new_ref, row_ref, lim_ref, ramp_ref, avail_ref, halo_ref,
        bal_ref, res_ref, resflow_ref, flow_ref, ang_ref, pownew_ref, powbar_ref, levnew_ref, levbar_ref, sto_ref,
        capout_ref, gen2_ref, lim2_ref, ramp2_ref, bal2_ref, sto2_ref, ang2_ref, angbar2_ref, pow2_ref,
        powbar2_ref, lev2_ref, levbar2_ref, out_ref, shift_ref,
    ) = refs
    rows, _, buses = bar_ref.shape
    invest, step_size = get_totals(entries, buses, here_ref, squares_ref, other_ref)

    def lone(ahead, row):
        return neighbour(passed, ahead, (slice(row, row + 1), slice(buses, 2 * buses)))

    def hour(ahead, place):
        return neighbour(passed, ahead, (slice(None), slice(place * buses, (place + 1) * buses)))

    lev_front, bar_front = lone(True, 1), hour(True, 2)
    lev_behind, pow_behind, bar_behind = lone(False, 2), lone(False, 3), hour(False, 3)
    cap_new = capacity_of(hours, cap_ref, inv_ref, invest)
    capout_ref[...] = cap_new
    cap_bar = 2.0 * cap_new - cap_ref[...]
    rate = rr_ref[...]
    ramp_cap = rate * cap_bar
    cost = vc_ref[...]

    bal = bal_ref[...] + step_size * res_ref[...]
    bal2_ref[...] = bal
    lev_bar, pow_bar = levbar_ref[...], powbar_ref[...]
    shift_ref[8 : 8 + rows] = lev_bar
    shift_ref[8 + rows : 9 + rows] = lev_front
    sto = sto_ref[...] + step_size * (shift_ref[9 : 9 + rows] - lev_bar + pow_bar)
    sto2_ref[...] = sto
    sto_before = halo_ref[TECH : TECH + 1] + step_size * (
        levbar_ref[0:1] - lev_behind + pow_behind
    )
    shift_ref[8 : 8 + rows] = sto
    shift_ref[7:8] = sto_before
    ang_step = primal_step * (flow_ref[...] + step_size * resflow_ref[...])
    ang_old = ang_ref[...] + primal_step * flow_ref[...]
    ang2_ref[...] = ang_old + ang_step
    angbar2_ref[...] = ang_old + 2.0 * ang_step
    pow_old = pownew_ref[...]
    pow_new = pow_old - primal_step * (bal + sto)
    pow2_ref[...] = pow_new
    powbar2_ref[...] = 2.0 * pow_new - pow_old
    lev_old = levnew_ref[...]
    lev_new = jnp.maximum(0.0, lev_old - primal_step * (shift_ref[7 : 7 + rows] - sto))
    lev2_ref[...] = lev_new
    levbar2_ref[...] = 2.0 * lev_new - lev_old
    squares = add_squares(
        jnp.zeros((TECH, buses), F32), ang_step, pow_new - pow_old, lev_new - lev_old
    )

    unroll = divisor(rows, 7)

    def step(t, carry, first=False, last=False):
        bar, before, limit_sum, ramp_sum, squares = carry
        old = row_ref[...] if first else new_ref[t]
        bar_next = bar_front if last else bar_ref[t + 1]
        avail = avail_ref[t]
        lim = jnp.maximum(0.0, lim_ref[t] + step_size * (bar - avail * cap_bar))
        ramp = jnp.maximum(0.0, ramp_ref[t] + step_size * (bar_next - bar - ramp_cap))
        dual = jnp.broadcast_to(bal2_ref[pl.ds(t, 1), :], (TECH, buses))
        gen = jnp.maximum(0.0, old - primal_step * (cost + dual + lim + before - ramp))
        squares += (gen - old) ** 2
        limit_sum += avail * lim
        ramp_sum += ramp
        gen2_ref[t] = gen
        lim2_ref[t] = lim
        ramp2_ref[t] = ramp
        if first:
            out_ref[:, 2 * buses :] = 2.0 * gen - old
        return bar_next, ramp, limit_sum, ramp_sum, squares

    bar = mine_ref[:, 2 * buses : 3 * buses]
    before = jnp.maximum(0.0, halo_ref[:TECH] + step_size * (bar - bar_behind - ramp_cap))
    zero = jnp.zeros((TECH, buses), F32)
    carry = (bar, before, zero, zero, squares)
    for t in range(unroll):
        carry = step(t, carry, first=t == 0)

    def several(j, carry):
        for k in range(unroll):
            carry = step(j * unroll + k, carry)
        return carry

    carry = lax.fori_loop(1, rows // unroll - 1, several, carry)
    for t in range(rows - unroll, rows):
        carry = step(t, carry, last=t == rows - 1)
    _, _, limit_sum, ramp_sum, squares = carry
    put_totals(out_ref, limit_sum + rate * ramp_sum, squares, (levbar2_ref[0:1],), ())


def residual_two_body(
    pieces, gen_ref, ang_ref, lev_ref, pow_ref, new_ref, row_ref, powbar_ref, load_ref, high_ref, low_ref, *refs,
):
    sources, refs = refs[:pieces], refs[pieces:]
    out_ref, bar_ref, gen_h, ang_h, lev_h, pow_h, sum_ref, sems = refs
    copies = [
        pltpu.make_async_copy(source, target, sems.at[k])
        for k, (source, target) in enumerate(
            ((gen_ref, gen_h), (ang_ref, ang_h), (lev_ref, lev_h), (pow_ref, pow_h))
        )
    ]
    for copy in copies:
        copy.start()
    rows, _, buses = gen_ref.shape
    unroll = divisor(rows, 7)
    flow = network_product(sources, high_ref, low_ref)

    def one(t, old):
        bar = 2.0 * gen_ref[t] - old
        bar_ref[t] = bar
        sum_ref[pl.ds(t, 1), :] = jnp.sum(bar, axis=0, keepdims=True)

    for t in range(unroll):
        one(t, new_ref[t] if t else row_ref[...])

    def several(j, _):
        for k in range(unroll):
            one(j * unroll + k, new_ref[j * unroll + k])
        return 0

    lax.fori_loop(1, rows // unroll, several, 0)
    out_ref[...] = sum_ref[...] + powbar_ref[...] - flow - load_ref[...]
    for copy in copies:
        copy.wait()


def last_body(
    hours, entries, steps, here_ref, squares_ref, other_ref, *refs,
):
    passed, refs = refs[:steps], refs[steps:]
    (
        cap_ref, inv_ref, rr_ref,
        bar_ref, lim_ref, ramp_ref, avail_ref, bal_ref, res_ref, sto_ref, levbar_ref, powbar_ref,
        capout_ref, lim_h, ramp_h, balout_ref, stoout_ref, lim_v, ramp_v, shift_ref, sems,
    ) = refs
    rows, _, buses = bar_ref.shape
    chunk = divisor(rows, 28)
    unroll = divisor(chunk, 7)
    chunks = rows // chunk
    invest, step_size = get_totals(entries, buses, here_ref, squares_ref, other_ref)
    lev_front = neighbour(passed, True, (slice(1, 2), slice(buses, 2 * buses)))
    bar_front = neighbour(passed, True, (slice(None), slice(2 * buses, 3 * buses)))
    cap_new = capacity_of(hours, cap_ref, inv_ref, invest)
    capout_ref[...] = cap_new
    cap_bar = 2.0 * cap_new - cap_ref[...]
    ramp_cap = rr_ref[...] * cap_bar

    def copies(i):
        rows_here = pl.ds(i * chunk, chunk)
        return [
            pltpu.make_async_copy(source.at[rows_here], target.at[rows_here], sems.at[i, k])
            for k, (source, target) in enumerate(((lim_v, lim_h), (ramp_v, ramp_h)))
        ]

    def step(t, bar, last=False):
        bar_next = bar_front if last else bar_ref[t + 1]
        lim_v[t] = jnp.maximum(0.0, lim_ref[t] + step_size * (bar - avail_ref[t] * cap_bar))
        ramp_v[t] = jnp.maximum(0.0, ramp_ref[t] + step_size * (bar_next - bar - ramp_cap))
        return bar_next

    bar = bar_ref[0]
    for i in range(chunks):
        end = (i + 1) * chunk
        stop = end - unroll if i == chunks - 1 else end

        def several(j, bar, start=i * chunk):
            for k in range(unroll):
                bar = step(start + j * unroll + k, bar)
            return bar

        bar = lax.fori_loop(0, (stop - i * chunk) // unroll, several, bar)
        for t in range(stop, end):
            bar = step(t, bar, last=t == rows - 1)
        for copy in copies(i):
            copy.start()
    balout_ref[...] = bal_ref[...] + step_size * res_ref[...]
    lev_bar = levbar_ref[...]
    shift_ref[8 : 8 + rows] = lev_bar
    shift_ref[8 + rows : 9 + rows] = lev_front
    stoout_ref[...] = sto_ref[...] + step_size * (shift_ref[9 : 9 + rows] - lev_bar + powbar_ref[...])
    for i in range(chunks):
        for copy in copies(i):
            copy.wait()


def per_device(
    demand,
    avail_factor,
    tech_mask,
    var_cost,
    inv_cost,
    ramp_rate,
    network,
    pattern,
    live_hours,
    generation,
    angles,
    levels,
    net_power,
    capacity,
    balance_dual,
    storage_dual,
    limit_dual,
    ramp_dual,
):
    rows, buses = demand.shape
    hours = rows * lax.axis_size("hour")
    entries = float(hours * (TECH + 3) * BUS)
    swap = lax.axis_size("region") == 2
    pieces = 2 if swap else 1
    cube, flat, tech = (rows, TECH, buses), (rows, buses), (TECH, buses)
    shift = pltpu.VMEM((rows + 24, buses), F32)
    chunks = rows // divisor(rows, 28)

    def all_buses(block):
        if swap:
            return block, partner(block, "region", 1)
        return (lax.all_gather(block, "region", axis=1, tiled=True),)

    steps = len(distances("hour"))

    def totals(block, *work):
        row = lax.broadcasted_iota(jnp.int32, block.shape, 0)
        lane = lax.broadcasted_iota(jnp.int32, block.shape, 1)
        adds = (lane < buses) | ((lane < 2 * buses) & (row == 0))
        passed = []
        for k, distance in enumerate(distances("hour")):
            got = partner(block, "hour", distance)
            passed.append(got)
            if k < len(work) and work[k]:
                block = after(block, work[k]())
            block = got + jnp.where(adds, block, 0.0)
        squares = block
        *inner, outer = distances("region")
        for distance in inner:
            squares = squares + partner(squares, "region", distance)
        return block, squares, partner(squares, "region", outer), passed

    halo = jnp.concatenate(
        [ramp_dual[-1], jnp.broadcast_to(storage_dual[-1:], (TECH, buses))], axis=0
    )
    halo = shifted(halo, "hour", 1)
    balances = all_buses(balance_dual)

    bar, new, lim, ramp, avail, high, low, invest, square, load = call(
        functools.partial(load_body, swap),
        (generation, limit_dual, ramp_dual, avail_factor, network, tech_mask, var_cost, ramp_rate,
         balance_dual, demand, pattern, live_hours),
        [HBM] * 11 + [SMEM],
        [(cube, F32)] * 5 + [((buses, BUS), jnp.bfloat16)] * 2 + [(tech, F32)] * 2 + [(flat, F32)],
        scratch=(
            pltpu.VMEM(cube, jnp.bfloat16),
            pltpu.VMEM((buses, BUS), F32),
            pltpu.VMEM(tech, jnp.int32),
            pltpu.VMEM(tech, F32),
            pltpu.VMEM(tech, F32),
            pltpu.VMEM(flat, F32),
            pltpu.VMEM(flat, F32),
            pltpu.SMEM(pattern.shape, jnp.int32),
            pltpu.SemaphoreType.DMA((chunks, 4)),
            pltpu.SemaphoreType.DMA((pieces,)),
            pltpu.SemaphoreType.DMA((6,)),
        ),
        name="load",
    )
    (
        row, flow, ang_bar, pow_new, pow_bar, lev_new, lev_bar, total,
    ) = call(
        functools.partial(first_body, pieces),
        (bar, lim, ramp, halo, var_cost, invest, square, balance_dual, *balances,
         angles, net_power, levels, storage_dual, high, low),
        [VMEM] * (8 + pieces + 6),
        [(tech, F32)] + [(flat, F32)] * 6 + [((TECH, 4 * buses), F32)],
        scratch=(shift,),
        name="first",
    )
    sources = all_buses(ang_bar)
    made = {}

    def residual():
        (made["res"],) = call(
            functools.partial(residual_one_body, pieces),
            (bar, total, pow_bar, load, high, low, *sources),
            [VMEM] * (6 + pieces),
            [(flat, F32)],
            scratch=(pltpu.VMEM(flat, F32),),
            name="residual1",
        )
        return made["res"]

    def product():
        (made["flow"],) = call(
            functools.partial(product_body, pieces),
            (high, low, *all_buses(made["res"])),
            [VMEM] * (2 + pieces),
            [(flat, F32)],
            name="product",
        )
        return made["flow"]

    here, squares, other, passed = totals(total, None, residual, None, product)
    res, res_flow = made["res"], made["flow"]
    (
        cap, gen2, lim1, ramp1, bal1, sto1, ang2, ang_bar2, pow2, pow_bar2, lev2, lev_bar2, total2,
    ) = call(
        functools.partial(middle_body, hours, entries, steps),
        (here, squares, other, total, *passed, capacity, inv_cost, ramp_rate, var_cost, bar, new, row, lim, ramp, avail,
         halo, balance_dual, res, res_flow, flow, angles, pow_new, pow_bar, lev_new, lev_bar,
         storage_dual),
        [VMEM] * (25 + steps),
        [(tech, F32)] + [(cube, F32)] * 3 + [(flat, F32)] * 8 + [((TECH, 3 * buses), F32)],
        scratch=(shift,),
        name="middle",
    )
    sources2 = all_buses(ang_bar2)

    def residual2():
        made["two"] = call(
            functools.partial(residual_two_body, pieces),
            (gen2, ang2, lev2, pow2, new, row, pow_bar2, load, high, low, *sources2),
            [VMEM] * (10 + pieces),
            [(flat, F32), (cube, F32), (cube, F32)] + [(flat, F32)] * 3,
            out_specs=[VMEM] * 2 + [HBM] * 4,
            scratch=(pltpu.VMEM(flat, F32), pltpu.SemaphoreType.DMA((4,))),
            name="residual2",
        )
        return made["two"][0]

    here2, squares2, other2, passed2 = totals(total2, None, residual2)
    res2, bar2, gen2, ang2, lev2, pow2 = made["two"]
    cap2, lim2, ramp2, bal2, sto2 = call(
        functools.partial(last_body, hours, entries, steps),
        (here2, squares2, other2, *passed2, cap, inv_cost, ramp_rate, bar2, lim1, ramp1, avail, bal1, res2, sto1,
         lev_bar2, pow_bar2),
        [VMEM] * (15 + steps),
        [(tech, F32), (cube, F32), (cube, F32), (flat, F32), (flat, F32)],
        out_specs=[VMEM, HBM, HBM, VMEM, VMEM],
        scratch=(
            pltpu.VMEM(cube, F32), pltpu.VMEM(cube, F32), shift, pltpu.SemaphoreType.DMA((chunks, 2)),
        ),
        name="last",
    )
    return gen2, ang2, lev2, pow2, cap2, bal2, sto2, lim2, ramp2


def solution(mesh):
    return jax.shard_map(
        per_device,
        mesh=mesh,
        in_specs=(
            P("hour", "region"),
            P("hour", None, "region"),
            P(None, "region"),
            P(None, "region"),
            P(None, "region"),
            P(None, "region"),
            P("region", None),
            P(),
            P(),
            P("hour", None, "region"),
            P("hour", "region"),
            P("hour", "region"),
            P("hour", "region"),
            P(None, "region"),
            P("hour", "region"),
            P("hour", "region"),
            P("hour", None, "region"),
            P("hour", None, "region"),
        ),
        out_specs=(
            P("hour", None, "region"),
            P("hour", "region"),
            P("hour", "region"),
            P("hour", "region"),
            P(None, "region"),
            P("hour", "region"),
            P("hour", "region"),
            P("hour", None, "region"),
            P("hour", None, "region"),
        ),
        check_vma=False,
    )
```

time: 320 us -> 60 us (0.19)
  blocking collectives: 236 us -> 0 us
  other arithmetic: 33.9 us -> 0.67 us
  Pallas kernels: 0 us -> 19.4 us
  matrix products: 13.8 us -> 0 us
  waiting for transfers between devices: 5.53 us -> 17.2 us
  local copies, waits for them, and re-layouts: 8.49 us -> 1.5 us
  between operations: 8.08 us -> 1.53 us
  starting transfers between devices: 13 us -> 19.3 us
    psum x4 -> x0, blocking collectives: 225 us -> none  [the longest x2 151 us: per_device(): invest = lax.psum(invest_part, 'hour')]
    pallas_call x0 -> x7, Pallas kernels: none -> 19.4 us  [call(): pl.pallas_call(body, out_shape=[jax.ShapeDtypeStruct(shape, dtype) for sh...]
    reduce_sum x7 -> x0, other arithmetic: 18.4 us -> none  [the longest x1 6.08 us: per_device(): jnp.sum(gen_bar, axis=1) + pow_bar]
    ppermute x0 -> x14, waiting for transfers between devices: none -> 17.2 us  [partner(): lax.ppermute(block, axis, [(i, i ^ distance) for i in range(lax.axis_size...]
    ppermute x0 -> x14, starting transfers between devices: none -> 16.7 us  [partner(): lax.ppermute(block, axis, [(i, i ^ distance) for i in range(lax.axis_size...]
    dot_general x4 -> x0, matrix products: 13.8 us -> none  [fold_part(): lax.dot_general(segment, matrix, (((1,), (1,)), ((), ())), precision=lax....]
    all_gather x4 -> x0, blocking collectives: 11.2 us -> none  [the longest x2 6.11 us: per_device(): lax.all_gather(ang_bar, 'region', axis=1, tiled=True)]
    ppermute x8 -> x1, starting transfers between devices: 13 us -> 2.55 us  [shifted(): return lax.ppermute(block, axis, route)]
  transfers between devices with their start and end apart: 8 -> 15, of which waited for: 2 -> 10; matrix products, arithmetic and copies ran while one was open for 11% -> 3% of each run, Pallas kernels for 0% -> 19%
where the time goes in v2:
time: 60 us; the launch traced here: 59.6 us
  Pallas kernels  19.4 us (32%)
  starting transfers between devices  19.3 us (32%)
  waiting for transfers between devices  17.2 us (29%)
  between operations  1.53 us (3%)
  local copies, waits for them, and re-layouts  1.5 us (2%)
  other arithmetic  0.67 us (1%)
    pallas_call x7, Pallas kernels, call(): pl.pallas_call(body, out_shape=[jax.ShapeDtypeStruct(shape, dtype) for sh...  19.4 us
    ppermute x14, waiting for transfers between devices, partner(): lax.ppermute(block, axis, [(i, i ^ distance) for i in range(lax.axis_size...  17.2 us
    ppermute x14, starting transfers between devices, partner(): lax.ppermute(block, axis, [(i, i ^ distance) for i in range(lax.axis_size...  16.7 us
    ppermute x1, starting transfers between devices, shifted(): return lax.ppermute(block, axis, route)  2.55 us
  transfers between devices with their start and end apart: 15, of which 10 were waited for; matrix products, arithmetic and copies ran while one was open for 3% of the time, Pallas kernels for 19%

profile of v2, /device:TPU:0, one launch (start us, length us, event | category | flops | bytes accessed | tf_op | source)
XLA Modules:
  0.0 59.6 jit_solution(4009429168305933856)
XLA Ops:
  0.6 0.5 collective-permute-start.1
  1.2 0.7 %slice_bitcast_fusion = f32[8,512]{1,0:T(8,128)S(1)} fusion(f32[140,8,512]{2,1,0:T(8,128)} %ramp_h.1), kind=kLoop, calls=%fused_computation.11 | loop fusion | bytes 32768 | tf_op jit(solution)/shard_map/squeeze | solution.py:550
  1.9 0.7 %slice.7 = f32[1,512]{1,0:T(1,128)S(1)} slice(f32[140,512]{1,0:T(8,128)} %refs_24_.1), slice={[139:140], [0:512]} | slice | bytes 4096 | tf_op jit(solution)/shard_map/slice | solution.py:550
  2.6 2.6 %collective-permute-start = (f32[16,512]{1,0:T(8,128)S(1)}, f32[16,512]{1,0:T(8,128)S(1)}, u32[]{:S(2)}, u32[]{:S(2)}) collective-permute-start(f32[16,512]{1,0:T(8,128)S(1)} %pad_maximum_fusion), channel_id=1, source_target_pairs={{30,0},{0,2},{2,4},{4,6},{6,8},{8,10},{10,12},{12,14},{14,16},{16,... | collective-permute-start | bytes 98312 | tf_op jit(solution)/shard_map/ppermute | solution.py:28
  5.8 0.0 copy-start
  5.8 0.0 copy-start.1
  5.8 0.0 copy-start.2
  5.9 0.0 copy-start.3
  5.9 0.0 copy-start.4
  5.9 0.0 copy-start.5
  5.9 6.3 %load.1 = (f32[140,8,512]{2,1,0:T(8,128)S(1)}, f32[140,8,512]{2,1,0:T(8,128)S(1)}, f32[140,8,512]{2,1,0:T(8,128)S(1)}, f32[140,8,512]{2,1,0:T(8,128)S(1)}, f32[1...) custom-call(f32[140,8,512]{2,1,0:T(8,128)} %gen_h.1, ...), custom_call_target="tpu_custom_call" | custom-call | flops 4194304 | bytes 8388608 | tf_op jit(solution)/shard_map/load/pallas_call | solution.py:78
  12.3 1.5 %first.1 = (f32[8,512]{1,0:T(8,128)S(1)}, f32[140,512]{1,0:T(8,128)S(1)}, f32[140,512]{1,0:T(8,128)S(1)}, f32[140,512]{1,0:T(8,128)S(1)}, f32[140,512]{1,0:T(8,1...) custom-call(f32[140,8,512]{2,1,0:T(8,128)S(1)} %get-tuple-element.54.bar_ref.refs_8_, ...), custom_call_target="tpu_custom_call" | custom-call | flops 4194304 | bytes 8388608 | tf_op jit(solution)/shard_map/first/pallas_call | solution.py:78
  13.8 1.6 %collective-permute-start.2 = (f32[8,2048]{1,0:T(8,128)S(1)}, f32[8,2048]{1,0:T(8,128)S(1)}, u32[]{:S(2)}, u32[]{:S(2)}) collective-permute-start(f32[8,2048]{1,0:T(8,128)S(1)} %get-tuple-element.61.total_ref.mine_ref), channel_id=1, source_target_pairs={{0,2},{2,0},{4,6},{6,4},{8,10},{10,8},{12,14},{14,12},{16,18},{18,... | collective-permute-start | bytes 196616 | tf_op jit(solution)/shard_map/ppermute | solution.py:32
  15.4 2.8 %collective-permute-done.2.refs_0_ = f32[8,2048]{1,0:T(8,128)S(1)} collective-permute-done((f32[8,2048]{1,0:T(8,128)S(1)}, f32[8,2048]{1,0:T(8,128)S(1)}, u32[]{:S(2)}, u32[]{:S(2)}) %collective-permute-start.2) | collective-permute-done | bytes 65568 | tf_op jit(solution)/shard_map/ppermute | solution.py:32
  18.1 0.1 select_add_fusion.3
  18.2 1.6 %collective-permute-start.3 = (f32[8,2048]{1,0:T(8,128)S(1)}, f32[8,2048]{1,0:T(8,128)S(1)}, u32[]{:S(2)}, u32[]{:S(2)}) collective-permute-start(f32[8,2048]{1,0:T(8,128)S(1)} %select_add_fusion.3), channel_id=1, source_target_pairs={{0,4},{2,6},{4,0},{6,2},{8,12},{10,14},{12,8},{14,10},{16,20},{18,... | collective-permute-start | bytes 196616 | tf_op jit(solution)/shard_map/ppermute | solution.py:32
  19.8 2.0 %residual1.1.refs_0_.refs_16_ = f32[140,512]{1,0:T(8,128)S(1)} custom-call(f32[140,8,512]{2,1,0:T(8,128)S(1)} %get-tuple-element.54.bar_ref.refs_8_, f32[8,2048]{1,0:T(8,128)S(1)} %get-tuple-element.61.total_ref.mine_ref, f32[140,512]{1,0:T(8,128)S(1)} %get-tuple-element.62.powbar_ref.refs_21_, f32[140,512]{1,0:T(8,128)S(1)} %get-tuple-element.63.load_ref, ...), custom_call_target="tpu_custom_call" | custom-call | flops 4194304 | bytes 8388608 | tf_op jit(solution)/shard_map/residual1/pallas_call | solution.py:78
  21.8 0.0 copy-start.6
  21.8 0.0 copy-start.7
  21.8 0.0 copy-start.8
  21.8 0.7 %collective-permute-done.3.refs_1_ = f32[8,2048]{1,0:T(8,128)S(1)} collective-permute-done((f32[8,2048]{1,0:T(8,128)S(1)}, f32[8,2048]{1,0:T(8,128)S(1)}, u32[]{:S(2)}, u32[]{:S(2)}) %collective-permute-start.3) | collective-permute-done | bytes 65568 | tf_op jit(solution)/shard_map/ppermute | solution.py:32
  22.5 0.1 select_add_fusion.2
  22.6 1.6 %collective-permute-start.5 = (f32[8,2048]{1,0:T(8,128)S(1)}, f32[8,2048]{1,0:T(8,128)S(1)}, u32[]{:S(2)}, u32[]{:S(2)}) collective-permute-start(f32[8,2048]{1,0:T(8,128)S(1)} %select_add_fusion.2), channel_id=1, source_target_pairs={{0,8},{2,10},{4,12},{6,14},{8,0},{10,2},{12,4},{14,6},{16,24},{18,... | collective-permute-start | bytes 196616 | tf_op jit(solution)/shard_map/ppermute | solution.py:32
  24.3 2.7 %collective-permute-done.5.refs_2_ = f32[8,2048]{1,0:T(8,128)S(1)} collective-permute-done((f32[8,2048]{1,0:T(8,128)S(1)}, f32[8,2048]{1,0:T(8,128)S(1)}, u32[]{:S(2)}, u32[]{:S(2)}) %collective-permute-start.5) | collective-permute-done | bytes 65568 | tf_op jit(solution)/shard_map/ppermute | solution.py:32
  27.0 0.1 select_add_fusion.1
  27.0 3.1 %collective-permute-start.6 = (f32[8,2048]{1,0:T(8,128)S(1)}, f32[8,2048]{1,0:T(8,128)S(1)}, u32[]{:S(2)}, u32[]{:S(2)}) collective-permute-start(f32[8,2048]{1,0:T(8,128)S(1)} %select_add_fusion.1), channel_id=1, source_target_pairs={{0,16},{2,18},{4,20},{6,22},{8,24},{10,26},{12,28},{14,30},{16,0},... | collective-permute-start | bytes 196616 | tf_op jit(solution)/shard_map/ppermute | solution.py:32
  30.1 1.2 %product.1.refs_17_ = f32[140,512]{1,0:T(8,128)S(1)} custom-call(bf16[512,1024]{1,0:T(8,128)(2,1)S(1)} %get-tuple-element.59.refs_6_.high_ref, bf16[512,1024]{1,0:T(8,128)(2,1)S(1)} %get-tuple-element.60.refs_7_.low_ref, f32[140,512]{1,0:T(8,128)S(1)} %residual1.1.refs_0_.refs_16_, f32[140,512]{1,0:T(8,128)S(1)} %collective-permute-done.7.refs_1_), custom_call_target="tpu_custom_call" | custom-call | flops 4194304 | bytes 8388608 | tf_op jit(solution)/shard_map/product/pallas_call | solution.py:78
  31.3 1.1 %collective-permute-done.6.refs_3_ = f32[8,2048]{1,0:T(8,128)S(1)} collective-permute-done((f32[8,2048]{1,0:T(8,128)S(1)}, f32[8,2048]{1,0:T(8,128)S(1)}, u32[]{:S(2)}, u32[]{:S(2)}) %collective-permute-start.6) | collective-permute-done | bytes 65568 | tf_op jit(solution)/shard_map/ppermute | solution.py:32
  32.4 0.1 select_add_fusion.here_ref.squares_ref
  32.5 0.1 collective-permute-start.8
  32.5 1.2 %collective-permute-done.8.other_ref = f32[8,2048]{1,0:T(8,128)S(1)} collective-permute-done((f32[8,2048]{1,0:T(8,128)S(1)}, f32[8,2048]{1,0:T(8,128)S(1)}, u32[]{:S(2)}, u32[]{:S(2)}) %collective-permute-start.8) | collective-permute-done | bytes 65568 | tf_op jit(solution)/shard_map/ppermute | solution.py:32
  33.8 3.0 %middle.1 = (f32[8,512]{1,0:T(8,128)S(1)}, f32[140,8,512]{2,1,0:T(8,128)S(1)}, f32[140,8,512]{2,1,0:T(8,128)S(1)}, f32[140,8,512]{2,1,0:T(8,128)S(1)}, f32[140,5...) custom-call(f32[8,2048]{1,0:T(8,128)S(1)} %select_add_fusion.here_re, ...), custom_call_target="tpu_custom_call" | custom-call | flops 4194304 | bytes 8388608 | tf_op jit(solution)/shard_map/middle/pallas_call | solution.py:78
  36.8 1.6 %collective-permute-start.10 = (f32[8,1536]{1,0:T(8,128)S(1)}, f32[8,1536]{1,0:T(8,128)S(1)}, u32[]{:S(2)}, u32[]{:S(2)}) collective-permute-start(f32[8,1536]{1,0:T(8,128)S(1)} %get-tuple-element.84), channel_id=1, source_target_pairs={{0,2},{2,0},{4,6},{6,4},{8,10},{10,8},{12,14},{14,12},{16,18},{18,... | collective-permute-start | bytes 147464 | tf_op jit(solution)/shard_map/ppermute | solution.py:32
  38.4 2.6 %collective-permute-done.10.refs_0_ = f32[8,1536]{1,0:T(8,128)S(1)} collective-permute-done((f32[8,1536]{1,0:T(8,128)S(1)}, f32[8,1536]{1,0:T(8,128)S(1)}, u32[]{:S(2)}, u32[]{:S(2)}) %collective-permute-start.10) | collective-permute-done | bytes 49184 | tf_op jit(solution)/shard_map/ppermute | solution.py:32
  41.0 0.1 select_add_fusion.7
  41.1 1.8 %collective-permute-start.11 = (f32[8,1536]{1,0:T(8,128)S(1)}, f32[8,1536]{1,0:T(8,128)S(1)}, u32[]{:S(2)}, u32[]{:S(2)}) collective-permute-start(f32[8,1536]{1,0:T(8,128)S(1)} %select_add_fusion.7), channel_id=1, source_target_pairs={{0,4},{2,6},{4,0},{6,2},{8,12},{10,14},{12,8},{14,10},{16,20},{18,... | collective-permute-start | bytes 147464 | tf_op jit(solution)/shard_map/ppermute | solution.py:32
  42.8 2.1 %residual2.1 = (f32[140,512]{1,0:T(8,128)S(1)}, f32[140,8,512]{2,1,0:T(8,128)S(1)}, f32[140,8,512]{2,1,0:T(8,128)}, f32[140,512]{1,0:T(8,128)}, f32[140,512]{1,0:T(8,128)}, /*index=5*/f32[140,512]{1,0:T(8,128)}) custom-call(f32[140,8,512]{2,1,0:T(8,128)S(1)} %get-tuple-element.74.gen_ref, f32[140,512]{1,0:T(8,128)S(1)} %get-tuple-element.75.ang_ref, ...), custom_call_target="tpu_custom_call" | custom-call | flops 4194304 | bytes 8388608 | tf_op jit(solution)/shard_map/residual2/pallas_call | solution.py:78
  44.9 0.3 collective-permute-done.11.refs_1_
  45.2 0.1 select_add_fusion.6
  45.3 1.5 %collective-permute-start.12 = (f32[8,1536]{1,0:T(8,128)S(1)}, f32[8,1536]{1,0:T(8,128)S(1)}, u32[]{:S(2)}, u32[]{:S(2)}) collective-permute-start(f32[8,1536]{1,0:T(8,128)S(1)} %select_add_fusion.6), channel_id=1, source_target_pairs={{0,8},{2,10},{4,12},{6,14},{8,0},{10,2},{12,4},{14,6},{16,24},{18,... | collective-permute-start | bytes 147464 | tf_op jit(solution)/shard_map/ppermute | solution.py:32
  46.8 2.6 %collective-permute-done.12.refs_2_ = f32[8,1536]{1,0:T(8,128)S(1)} collective-permute-done((f32[8,1536]{1,0:T(8,128)S(1)}, f32[8,1536]{1,0:T(8,128)S(1)}, u32[]{:S(2)}, u32[]{:S(2)}) %collective-permute-start.12) | collective-permute-done | bytes 49184 | tf_op jit(solution)/shard_map/ppermute | solution.py:32
  49.4 0.1 select_add_fusion.5
  49.5 3.3 %collective-permute-start.13 = (f32[8,1536]{1,0:T(8,128)S(1)}, f32[8,1536]{1,0:T(8,128)S(1)}, u32[]{:S(2)}, u32[]{:S(2)}) collective-permute-start(f32[8,1536]{1,0:T(8,128)S(1)} %select_add_fusion.5), channel_id=1, source_target_pairs={{0,16},{2,18},{4,20},{6,22},{8,24},{10,26},{12,28},{14,30},{16,0},... | collective-permute-start | bytes 147464 | tf_op jit(solution)/shard_map/ppermute | solution.py:32
  52.8 2.1 %collective-permute-done.13.refs_3_ = f32[8,1536]{1,0:T(8,128)S(1)} collective-permute-done((f32[8,1536]{1,0:T(8,128)S(1)}, f32[8,1536]{1,0:T(8,128)S(1)}, u32[]{:S(2)}, u32[]{:S(2)}) %collective-permute-start.13) | collective-permute-done | bytes 49184 | tf_op jit(solution)/shard_map/ppermute | solution.py:32
  54.9 0.1 select_add_fusion.4.here_ref.squares_ref
  55.0 0.1 collective-permute-start.14
  55.1 1.2 %collective-permute-done.14.other_ref = f32[8,1536]{1,0:T(8,128)S(1)} collective-permute-done((f32[8,1536]{1,0:T(8,128)S(1)}, f32[8,1536]{1,0:T(8,128)S(1)}, u32[]{:S(2)}, u32[]{:S(2)}) %collective-permute-start.14) | collective-permute-done | bytes 49184 | tf_op jit(solution)/shard_map/ppermute | solution.py:32
  56.3 3.3 %last.1 = (f32[8,512]{1,0:T(8,128)}, f32[140,8,512]{2,1,0:T(8,128)}, f32[140,8,512]{2,1,0:T(8,128)}, f32[140,512]{1,0:T(8,128)}, f32[140,512]{1,0:T(8,128)}) custom-call(f32[8,1536]{1,0:T(8,128)S(1)} %select_add_fusion.4.here_ref.squares_ref, f32[8,1536]{1,0:T(8,128)S(1)} %select_add_fusion.4.here_ref.squares_ref, ...), custom_call_target="tpu_custom_call" | custom-call | flops 4194304 | bytes 8388608 | tf_op jit(solution)/shard_map/last/pallas_call | solution.py:78
  (22 shorter events, 0.1 us)
Async XLA Ops:
  0.6 11.6 %collective-permute-start.1 = (f32[140,512]{1,0:T(8,128)}, f32[140,512]{1,0:T(8,128)S(1)}, u32[]{:S(2)}, u32[]{:S(2)}) collective-permute-start(f32[140,512]{1,0:T(8,128)} %refs_15_.1), channel_id=1, source_target_pairs={{0,1},{1,0},{2,3},{3,2},{4,5},{5,4},{6,7},{7,6},{8,9},{9,8},{10,11... | collective-permute-start | bytes 860168 | tf_op jit(solution)/shard_map/ppermute | solution.py:32
  2.6 9.6 %collective-permute-start = (f32[16,512]{1,0:T(8,128)S(1)}, f32[16,512]{1,0:T(8,128)S(1)}, u32[]{:S(2)}, u32[]{:S(2)}) collective-permute-start(f32[16,512]{1,0:T(8,128)S(1)} %pad_maximum_fusion), channel_id=1, source_target_pairs={{30,0},{0,2},{2,4},{4,6},{6,8},{8,10},{10,12},{12,14},{14,16},{16,... | collective-permute-start | bytes 98312 | tf_op jit(solution)/shard_map/ppermute | solution.py:28
  5.8 6.4 %copy-start = (f32[140,512]{1,0:T(8,128)S(1)}, f32[140,512]{1,0:T(8,128)}, u32[]{:S(2)}) copy-start(f32[140,512]{1,0:T(8,128)} %refs_15_.1) | copy-start | bytes 860164
  5.8 6.4 %copy-start.1 = (f32[140,512]{1,0:T(8,128)S(1)}, f32[140,512]{1,0:T(8,128)}, u32[]{:S(2)}) copy-start(f32[140,512]{1,0:T(8,128)} %refs_24_.1) | copy-start | bytes 860164
  5.8 6.4 %copy-start.2 = (f32[140,512]{1,0:T(8,128)S(1)}, f32[140,512]{1,0:T(8,128)}, u32[]{:S(2)}) copy-start(f32[140,512]{1,0:T(8,128)} %refs_19_.1) | copy-start | bytes 860164
  5.9 6.4 %copy-start.3 = (f32[140,512]{1,0:T(8,128)S(1)}, f32[140,512]{1,0:T(8,128)}, u32[]{:S(2)}) copy-start(f32[140,512]{1,0:T(8,128)} %refs_3_.1) | copy-start | bytes 860164
  5.9 6.4 %copy-start.4 = (f32[140,512]{1,0:T(8,128)S(1)}, f32[140,512]{1,0:T(8,128)}, u32[]{:S(2)}) copy-start(f32[140,512]{1,0:T(8,128)} %refs_4_.2) | copy-start | bytes 860164
  5.9 6.4 %copy-start.5 = (f32[8,512]{1,0:T(8,128)S(1)}, f32[8,512]{1,0:T(8,128)}, u32[]{:S(2)}) copy-start(f32[8,512]{1,0:T(8,128)} %refs_7_.1) | copy-start | bytes 49156
  13.8 4.3 %collective-permute-start.2 = (f32[8,2048]{1,0:T(8,128)S(1)}, f32[8,2048]{1,0:T(8,128)S(1)}, u32[]{:S(2)}, u32[]{:S(2)}) collective-permute-start(f32[8,2048]{1,0:T(8,128)S(1)} %get-tuple-element.61.total_ref.mine_ref), channel_id=1, source_target_pairs={{0,2},{2,0},{4,6},{6,4},{8,10},{10,8},{12,14},{14,12},{16,18},{18,... | collective-permute-start | bytes 196616 | tf_op jit(solution)/shard_map/ppermute | solution.py:32
  15.4 4.4 %collective-permute-start.4 = (f32[140,512]{1,0:T(8,128)S(1)}, f32[140,512]{1,0:T(8,128)S(1)}, u32[]{:S(2)}, u32[]{:S(2)}) collective-permute-start(f32[140,512]{1,0:T(8,128)S(1)} %get-tuple-element.64.refs_0_), channel_id=1, source_target_pairs={{0,1},{1,0},{2,3},{3,2},{4,5},{5,4},{6,7},{7,6},{8,9},{9,8},{10,11... | collective-permute-start | bytes 860168 | tf_op jit(solution)/shard_map/ppermute | solution.py:32
  18.2 4.3 %collective-permute-start.3 = (f32[8,2048]{1,0:T(8,128)S(1)}, f32[8,2048]{1,0:T(8,128)S(1)}, u32[]{:S(2)}, u32[]{:S(2)}) collective-permute-start(f32[8,2048]{1,0:T(8,128)S(1)} %select_add_fusion.3), channel_id=1, source_target_pairs={{0,4},{2,6},{4,0},{6,2},{8,12},{10,14},{12,8},{14,10},{16,20},{18,... | collective-permute-start | bytes 196616 | tf_op jit(solution)/shard_map/ppermute | solution.py:32
  21.8 12.0 %copy-start.6 = (f32[8,512]{1,0:T(8,128)S(1)}, f32[8,512]{1,0:T(8,128)}, u32[]{:S(2)}) copy-start(f32[8,512]{1,0:T(8,128)} %refs_6_.3) | copy-start | bytes 49156
  21.8 12.0 %copy-start.7 = (f32[8,512]{1,0:T(8,128)S(1)}, f32[8,512]{1,0:T(8,128)}, u32[]{:S(2)}) copy-start(f32[8,512]{1,0:T(8,128)} %refs_5_.5) | copy-start | bytes 49156
  21.8 12.0 %copy-start.8 = (f32[8,512]{1,0:T(8,128)S(1)}, f32[8,512]{1,0:T(8,128)}, u32[]{:S(2)}) copy-start(f32[8,512]{1,0:T(8,128)} %refs_4_.3) | copy-start | bytes 49156
  22.6 4.3 %collective-permute-start.5 = (f32[8,2048]{1,0:T(8,128)S(1)}, f32[8,2048]{1,0:T(8,128)S(1)}, u32[]{:S(2)}, u32[]{:S(2)}) collective-permute-start(f32[8,2048]{1,0:T(8,128)S(1)} %select_add_fusion.2), channel_id=1, source_target_pairs={{0,8},{2,10},{4,12},{6,14},{8,0},{10,2},{12,4},{14,6},{16,24},{18,... | collective-permute-start | bytes 196616 | tf_op jit(solution)/shard_map/ppermute | solution.py:32
  24.3 5.9 %collective-permute-start.7 = (f32[140,512]{1,0:T(8,128)S(1)}, f32[140,512]{1,0:T(8,128)S(1)}, u32[]{:S(2)}, u32[]{:S(2)}) collective-permute-start(f32[140,512]{1,0:T(8,128)S(1)} %residual1.1.refs_0_.refs_16_), channel_id=1, source_target_pairs={{0,1},{1,0},{2,3},{3,2},{4,5},{5,4},{6,7},{7,6},{8,9},{9,8},{10,11... | collective-permute-start | bytes 860168 | tf_op jit(solution)/shard_map/ppermute | solution.py:32
  27.0 5.3 %collective-permute-start.6 = (f32[8,2048]{1,0:T(8,128)S(1)}, f32[8,2048]{1,0:T(8,128)S(1)}, u32[]{:S(2)}, u32[]{:S(2)}) collective-permute-start(f32[8,2048]{1,0:T(8,128)S(1)} %select_add_fusion.1), channel_id=1, source_target_pairs={{0,16},{2,18},{4,20},{6,22},{8,24},{10,26},{12,28},{14,30},{16,0},... | collective-permute-start | bytes 196616 | tf_op jit(solution)/shard_map/ppermute | solution.py:32
  32.5 1.3 %collective-permute-start.8 = (f32[8,2048]{1,0:T(8,128)S(1)}, f32[8,2048]{1,0:T(8,128)S(1)}, u32[]{:S(2)}, u32[]{:S(2)}) collective-permute-start(f32[8,2048]{1,0:T(8,128)S(1)} %select_add_fusion.here_ref.squares_ref), channel_id=1, source_target_pairs={{0,1},{1,0},{2,3},{3,2},{4,5},{5,4},{6,7},{7,6},{8,9},{9,8},{10,11... | collective-permute-start | bytes 196616 | tf_op jit(solution)/shard_map/ppermute | solution.py:32
  36.8 4.2 %collective-permute-start.10 = (f32[8,1536]{1,0:T(8,128)S(1)}, f32[8,1536]{1,0:T(8,128)S(1)}, u32[]{:S(2)}, u32[]{:S(2)}) collective-permute-start(f32[8,1536]{1,0:T(8,128)S(1)} %get-tuple-element.84), channel_id=1, source_target_pairs={{0,2},{2,0},{4,6},{6,4},{8,10},{10,8},{12,14},{14,12},{16,18},{18,... | collective-permute-start | bytes 147464 | tf_op jit(solution)/shard_map/ppermute | solution.py:32
  38.4 4.4 %collective-permute-start.9 = (f32[140,512]{1,0:T(8,128)S(1)}, f32[140,512]{1,0:T(8,128)S(1)}, u32[]{:S(2)}, u32[]{:S(2)}) collective-permute-start(f32[140,512]{1,0:T(8,128)S(1)} %get-tuple-element.79.refs_0_), channel_id=1, source_target_pairs={{0,1},{1,0},{2,3},{3,2},{4,5},{5,4},{6,7},{7,6},{8,9},{9,8},{10,11... | collective-permute-start | bytes 860168 | tf_op jit(solution)/shard_map/ppermute | solution.py:32
  41.1 4.2 %collective-permute-start.11 = (f32[8,1536]{1,0:T(8,128)S(1)}, f32[8,1536]{1,0:T(8,128)S(1)}, u32[]{:S(2)}, u32[]{:S(2)}) collective-permute-start(f32[8,1536]{1,0:T(8,128)S(1)} %select_add_fusion.7), channel_id=1, source_target_pairs={{0,4},{2,6},{4,0},{6,2},{8,12},{10,14},{12,8},{14,10},{16,20},{18,... | collective-permute-start | bytes 147464 | tf_op jit(solution)/shard_map/ppermute | solution.py:32
  45.3 4.2 %collective-permute-start.12 = (f32[8,1536]{1,0:T(8,128)S(1)}, f32[8,1536]{1,0:T(8,128)S(1)}, u32[]{:S(2)}, u32[]{:S(2)}) collective-permute-start(f32[8,1536]{1,0:T(8,128)S(1)} %select_add_fusion.6), channel_id=1, source_target_pairs={{0,8},{2,10},{4,12},{6,14},{8,0},{10,2},{12,4},{14,6},{16,24},{18,... | collective-permute-start | bytes 147464 | tf_op jit(solution)/shard_map/ppermute | solution.py:32
  49.5 5.4 %collective-permute-start.13 = (f32[8,1536]{1,0:T(8,128)S(1)}, f32[8,1536]{1,0:T(8,128)S(1)}, u32[]{:S(2)}, u32[]{:S(2)}) collective-permute-start(f32[8,1536]{1,0:T(8,128)S(1)} %select_add_fusion.5), channel_id=1, source_target_pairs={{0,16},{2,18},{4,20},{6,22},{8,24},{10,26},{12,28},{14,30},{16,0},... | collective-permute-start | bytes 147464 | tf_op jit(solution)/shard_map/ppermute | solution.py:32
  55.0 1.3 %collective-permute-start.14 = (f32[8,1536]{1,0:T(8,128)S(1)}, f32[8,1536]{1,0:T(8,128)S(1)}, u32[]{:S(2)}, u32[]{:S(2)}) collective-permute-start(f32[8,1536]{1,0:T(8,128)S(1)} %select_add_fusion.4.here_ref.squares_ref), channel_id=1, source_target_pairs={{0,1},{1,0},{2,3},{3,2},{4,5},{5,4},{6,7},{7,6},{8,9},{9,8},{10,11... | collective-permute-start | bytes 147464 | tf_op jit(solution)/shard_map/ppermute | solution.py:32

commit v3 on v2

--- a/solution.py
+++ b/solution.py
@@ -87,106 +87,91 @@
     )(*operands)
 
 
+def pack_body(ramp_h, sto_h, *refs):
+    halo_ref, sto_v, sems = refs[-3:]
+    rows = ramp_h.shape[0]
+    start = (rows - 1) // TECH * TECH
+    copies = [
+        pltpu.make_async_copy(ramp_h.at[rows - 1], halo_ref.at[pl.ds(0, TECH)], sems.at[0]),
+        pltpu.make_async_copy(sto_h.at[pl.ds(start, rows - start)], sto_v, sems.at[1]),
+    ]
+    for copy in copies:
+        copy.start()
+    for copy in copies:
+        copy.wait()
+    halo_ref[TECH:] = jnp.broadcast_to(sto_v[rows - 1 - start : rows - start], (TECH, sto_v.shape[1]))
+
+
 def load_body(
-    swap, gen_h, lim_h, ramp_h, av_h, net_h, mask_h, vc_h, rr_h, bal_h, demand_h, pat_h, live_s,
-    bar_ref, new_ref, lim_ref, ramp_ref, avail_ref, high_ref, low_ref, invest_ref, square_ref, load_ref,
-    av_v, net_v, mask_v, vc_v, rr_v, bal_v, demand_v, pat_s, sems, net_sem, small_sem,
+    swap, gen_ref, lim_ref, ramp_ref, av_ref, net_ref, mask_ref, vc_ref, rr_ref, bal_ref, demand_ref, pat_s, live_s,
+    ang_ref, pow_ref, sto_ref, *refs,
 ):
-    rows, _, buses = gen_h.shape
-    chunk = divisor(rows, 28)
-    unroll = divisor(chunk, 7)
-    chunks = rows // chunk
+    (
+        bar_ref, new_ref, avail_ref, high_ref, low_ref, invest_ref, square_ref, load_ref,
+        flow_ref, angbar_ref, pownew_ref, powbar_ref,
+    ) = refs[-12:]
+    others = refs[:-12]
+    rows, _, buses = gen_ref.shape
+    unroll = divisor(rows, 7)
     region = lax.axis_index("region")
     pieces = 2 if swap else 1
     width = BUS // pieces
-
-    def network_copy(piece):
-        at = pl.multiple_of(lax.rem(region + piece, pieces) * width, BLOCK) if swap else 0
-        return pltpu.make_async_copy(
-            net_h.at[:, pl.ds(at, width)], net_v.at[:, pl.ds(piece * width, width)], net_sem.at[piece]
-        )
-
-    def copies(i):
-        rows_here = pl.ds(i * chunk, chunk)
-        return [
-            pltpu.make_async_copy(source.at[rows_here], target.at[rows_here], sems.at[i, k])
-            for k, (source, target) in enumerate(
-                ((gen_h, bar_ref), (lim_h, lim_ref), (ramp_h, ramp_ref), (av_h, av_v))
-            )
-        ]
-
-    small = [
-        pltpu.make_async_copy(source, target, small_sem.at[k])
-        for k, (source, target) in enumerate(
-            ((pat_h, pat_s), (mask_h, mask_v), (vc_h, vc_v), (rr_h, rr_v), (bal_h, bal_v),
-             (demand_h, demand_v))
-        )
-    ]
-    for copy in small[:-1]:
-        copy.start()
-    for piece in range(pieces):
-        network_copy(piece).start()
-    for i in range(chunks):
-        for copy in copies(i):
-            copy.start()
-    small[-1].start()
-
-    for copy in small[:-1]:
-        copy.wait()
     blocks = buses // BLOCK
     shift = region * blocks if swap else 0
-    for piece in range(pieces):
-        network_copy(piece).wait()
-        for i in range(blocks):
-            for j in range(piece * width // BLOCK, (piece + 1) * width // BLOCK):
-                at = (slice(i * BLOCK, (i + 1) * BLOCK), slice(j * BLOCK, (j + 1) * BLOCK))
-                coupled = pat_s[region * blocks + i, lax.rem(j + shift, BUS // BLOCK)].astype(F32)
-                high, low = split(net_v[at] * coupled)
-                high_ref[at] = high
-                low_ref[at] = low
-
-    mask = mask_v[...].astype(F32)
-    cost = vc_v[...]
+    for i in range(blocks):
+        for j in range(BUS // BLOCK):
+            at = (slice(i * BLOCK, (i + 1) * BLOCK), slice(j * BLOCK, (j + 1) * BLOCK))
+            place = lax.rem(j + shift, BUS // BLOCK)
+            coupled = pat_s[region * blocks + i, place].astype(F32)
+            source = net_ref[at[0], pl.ds(pl.multiple_of(place * BLOCK, BLOCK), BLOCK)]
+            high, low = split(source * coupled)
+            high_ref[at] = high
+            low_ref[at] = low
+
+    mask = mask_ref[...].astype(F32)
+    cost = vc_ref[...]
     live = live_s[0] - lax.axis_index("hour") * rows
 
     def step(t, carry, first=False):
         before, limit_sum, ramp_sum, squares = carry
-        gen, lim, ramp = bar_ref[t], lim_ref[t], ramp_ref[t]
+        gen, lim, ramp = gen_ref[t], lim_ref[t], ramp_ref[t]
         alive = jnp.where(t < live, 1.0, 0.0).astype(F32)
-        avail = av_v[t].astype(F32) * mask * alive
+        avail = av_ref[t].astype(F32) * mask * alive
         avail_ref[t] = avail
         limit_sum += avail * lim
         ramp_sum += ramp
         if not first:
-            dual = jnp.broadcast_to(bal_v[pl.ds(t, 1), :], (TECH, buses))
+            dual = jnp.broadcast_to(bal_ref[pl.ds(t, 1), :], (TECH, buses))
             new = jnp.maximum(0.0, gen - primal_step * (cost + dual + lim + before - ramp))
             squares += (new - gen) ** 2
             new_ref[t] = new
             bar_ref[t] = 2.0 * new - gen
+        else:
+            bar_ref[t] = gen
         return ramp, limit_sum, ramp_sum, squares
 
     carry = (jnp.zeros((TECH, buses), F32),) * 4
-    for i in range(chunks):
-        for copy in copies(i):
-            copy.wait()
-        start = i * chunk
-        if i == 0:
-            for t in range(unroll):
-                carry = step(t, carry, t == 0)
-            start = unroll
-
-        def several(j, carry, start=start):
-            for k in range(unroll):
-                carry = step(start + j * unroll + k, carry)
-            return carry
-
-        carry = lax.fori_loop(0, ((i + 1) * chunk - start) // unroll, several, carry)
-    _, limit_sum, ramp_sum, squares = carry
-    invest_ref[...] = limit_sum + rr_v[...] * ramp_sum
-    square_ref[...] = squares
-    small[-1].wait()
+    for t in range(unroll):
+        carry = step(t, carry, t == 0)
+
+    def several(j, carry):
+        for k in range(unroll):
+            carry = step(j * unroll + k, carry)
+        return carry
+
+    _, limit_sum, ramp_sum, squares = lax.fori_loop(1, rows // unroll, several, carry)
+    invest_ref[...] = limit_sum + rr_ref[...] * ramp_sum
+    flow = network_product(others, high_ref, low_ref)
+    flow_ref[...] = flow
+    ang_step = primal_step * flow
+    angbar_ref[...] = ang_ref[...] + 2.0 * ang_step
+    pow_old = pow_ref[...]
+    pow_new = pow_old - primal_step * (bal_ref[...] + sto_ref[...])
+    pownew_ref[...] = pow_new
+    powbar_ref[...] = 2.0 * pow_new - pow_old
+    square_ref[...] = add_squares(squares, ang_step, pow_new - pow_old)
     row = lax.broadcasted_iota(jnp.int32, (rows, buses), 0)
-    load_ref[...] = jnp.where(row < live, demand_v[...], 0.0)
+    load_ref[...] = jnp.where(row < live, demand_ref[...], 0.0)
 
 
 def fold_rows(square):
@@ -196,20 +181,46 @@
     return total, square[full:]
 
 
-def put_totals(out_ref, invest, squares, rows_of_one, cubes):
+def layout(buses, lone):
+    width = max(BLOCK, buses * (1 << (lone + 1).bit_length() - 1) // TECH)
+    return width, buses // width
+
+
+def put_totals(out_ref, lone, invest, squares, rows_of_one):
     buses = invest.shape[1]
+    width, parts = layout(buses, lone)
+    lanes = slice(buses, buses + width)
     out_ref[:, :buses] = invest
-    lone = [jnp.sum(squares, axis=0, keepdims=True), *rows_of_one]
-    for i, row in enumerate(lone):
-        out_ref[i : i + 1, buses : 2 * buses] = row
-    out_ref[len(lone) :, buses : 2 * buses] = jnp.zeros((TECH - len(lone), buses), F32)
+    out_ref[:, lanes] = jnp.zeros((TECH, width), F32)
+    for i, row in enumerate((jnp.sum(squares, axis=0, keepdims=True), *rows_of_one)):
+        for j in range(parts):
+            out_ref[i * parts + j : i * parts + j + 1, lanes] = row[:, j * width : (j + 1) * width]
+
+
+def put_cubes(out_ref, lone, *cubes):
+    start = cubes[0].shape[1] + layout(cubes[0].shape[1], lone)[0]
     for i, cube in enumerate(cubes):
-        out_ref[:, (i + 2) * buses : (i + 3) * buses] = cube
-
-
-def get_totals(entries, buses, here_ref, squares_ref, other_ref):
-    squares = jnp.sum(squares_ref[0:1, buses : 2 * buses] + other_ref[0:1, buses : 2 * buses])
+        out_ref[:, start + i * cube.shape[1] : start + (i + 1) * cube.shape[1]] = cube
+
+
+def get_totals(entries, buses, lone, here_ref, squares_ref, other_ref):
+    width, parts = layout(buses, lone)
+    at = (slice(0, parts), slice(buses, buses + width))
+    squares = jnp.sum(squares_ref[at] + other_ref[at])
     return here_ref[:, :buses], dual_scale * lax.rsqrt(jnp.full((1, 1), squares / entries + 1e-06, F32))
+
+
+def get_row(buses, lone, index, read):
+    width, parts = layout(buses, lone)
+    lanes = slice(buses, buses + width)
+    return jnp.concatenate(
+        [read((slice(i, i + 1), lanes)) for i in range(index * parts, (index + 1) * parts)], axis=1
+    )
+
+
+def get_cube(buses, lone, index, read):
+    start = buses + layout(buses, lone)[0] + index * buses
+    return read((slice(None), slice(start, start + buses)))
 
 
 def neighbour(passed, ahead, index):
@@ -234,14 +245,9 @@
 
 
 def first_body(
-    pieces, bar_ref, lim_ref, ramp_ref, halo_ref, vc_ref, invest_ref, square_ref, bal_ref, *refs,
+    bar_ref, lim_ref, ramp_ref, halo_ref, vc_ref, invest_ref, square_ref, bal_ref, lev_ref, sto_ref, powbar_ref,
+    row_ref, levnew_ref, levbar_ref, total_ref, shift_ref,
 ):
-    others, refs = refs[: pieces], refs[pieces:]
-    (
-        ang_ref, pow_ref, lev_ref, sto_ref, high_ref, low_ref,
-        row_ref, flow_ref, angbar_ref, pownew_ref, powbar_ref, levnew_ref, levbar_ref,
-        total_ref, shift_ref,
-    ) = refs
     rows, _, buses = bar_ref.shape
     gen = bar_ref[0]
     dual = jnp.broadcast_to(bal_ref[0:1, :], (TECH, buses))
@@ -249,29 +255,18 @@
         0.0, gen - primal_step * (vc_ref[...] + dual + lim_ref[0] + halo_ref[:TECH] - ramp_ref[0])
     )
     row_ref[...] = new
-    bal, sto = bal_ref[...], sto_ref[...]
-    flow = network_product(others, high_ref, low_ref)
-    flow_ref[...] = flow
-    ang_step = primal_step * flow
-    angbar_ref[...] = ang_ref[...] + 2.0 * ang_step
-    pow_old = pow_ref[...]
-    pow_new = pow_old - primal_step * (bal + sto)
-    pownew_ref[...] = pow_new
-    powbar_ref[...] = 2.0 * pow_new - pow_old
+    sto = sto_ref[...]
     shift_ref[8 : 8 + rows] = sto
     shift_ref[7:8] = halo_ref[TECH : TECH + 1]
     lev_old = lev_ref[...]
     lev_new = jnp.maximum(0.0, lev_old - primal_step * (shift_ref[7 : 7 + rows] - sto))
     levnew_ref[...] = lev_new
     levbar_ref[...] = 2.0 * lev_new - lev_old
-    squares = add_squares(
-        square_ref[...], new - gen, ang_step, pow_new - pow_old, lev_new - lev_old
-    )
     put_totals(
-        total_ref, invest_ref[...], squares,
+        total_ref, 3, invest_ref[...], add_squares(square_ref[...], new - gen, lev_new - lev_old),
         (levbar_ref[0:1], levbar_ref[rows - 1 : rows], powbar_ref[rows - 1 : rows]),
-        (2.0 * new - gen, bar_ref[rows - 1]),
-    )
+    )
+    put_cubes(total_ref, 3, 2.0 * new - gen, bar_ref[rows - 1])
 
 
 def residual_one_body(
@@ -289,7 +284,8 @@
         return 0
 
     lax.fori_loop(0, rows // unroll, several, 0)
-    sum_ref[0:1] = jnp.sum(total_ref[:, 2 * buses : 3 * buses], axis=0, keepdims=True)
+    bar = get_cube(buses, 3, 0, total_ref.__getitem__)
+    sum_ref[0:1] = jnp.sum(bar, axis=0, keepdims=True)
     out_ref[...] = sum_ref[...] + powbar_ref[...] - flow - load_ref[...]
 
 
@@ -313,16 +309,14 @@
         powbar2_ref, lev2_ref, levbar2_ref, out_ref, shift_ref,
     ) = refs
     rows, _, buses = bar_ref.shape
-    invest, step_size = get_totals(entries, buses, here_ref, squares_ref, other_ref)
-
-    def lone(ahead, row):
-        return neighbour(passed, ahead, (slice(row, row + 1), slice(buses, 2 * buses)))
-
-    def hour(ahead, place):
-        return neighbour(passed, ahead, (slice(None), slice(place * buses, (place + 1) * buses)))
-
-    lev_front, bar_front = lone(True, 1), hour(True, 2)
-    lev_behind, pow_behind, bar_behind = lone(False, 2), lone(False, 3), hour(False, 3)
+    invest, step_size = get_totals(entries, buses, 3, here_ref, squares_ref, other_ref)
+    from_next = functools.partial(neighbour, passed, True)
+    from_last = functools.partial(neighbour, passed, False)
+    lev_front = get_row(buses, 3, 1, from_next)
+    bar_front = get_cube(buses, 3, 0, from_next)
+    lev_behind = get_row(buses, 3, 2, from_last)
+    pow_behind = get_row(buses, 3, 3, from_last)
+    bar_behind = get_cube(buses, 3, 1, from_last)
     cap_new = capacity_of(hours, cap_ref, inv_ref, invest)
     capout_ref[...] = cap_new
     cap_bar = 2.0 * cap_new - cap_ref[...]
@@ -376,10 +370,10 @@
         lim2_ref[t] = lim
         ramp2_ref[t] = ramp
         if first:
-            out_ref[:, 2 * buses :] = 2.0 * gen - old
+            put_cubes(out_ref, 1, 2.0 * gen - old)
         return bar_next, ramp, limit_sum, ramp_sum, squares
 
-    bar = mine_ref[:, 2 * buses : 3 * buses]
+    bar = get_cube(buses, 3, 0, mine_ref.__getitem__)
     before = jnp.maximum(0.0, halo_ref[:TECH] + step_size * (bar - bar_behind - ramp_cap))
     zero = jnp.zeros((TECH, buses), F32)
     carry = (bar, before, zero, zero, squares)
@@ -395,7 +389,7 @@
     for t in range(rows - unroll, rows):
         carry = step(t, carry, last=t == rows - 1)
     _, _, limit_sum, ramp_sum, squares = carry
-    put_totals(out_ref, limit_sum + rate * ramp_sum, squares, (levbar2_ref[0:1],), ())
+    put_totals(out_ref, 1, limit_sum + rate * ramp_sum, squares, (levbar2_ref[0:1],))
 
 
 def residual_two_body(
@@ -447,9 +441,10 @@
     chunk = divisor(rows, 28)
     unroll = divisor(chunk, 7)
     chunks = rows // chunk
-    invest, step_size = get_totals(entries, buses, here_ref, squares_ref, other_ref)
-    lev_front = neighbour(passed, True, (slice(1, 2), slice(buses, 2 * buses)))
-    bar_front = neighbour(passed, True, (slice(None), slice(2 * buses, 3 * buses)))
+    invest, step_size = get_totals(entries, buses, 1, here_ref, squares_ref, other_ref)
+    from_next = functools.partial(neighbour, passed, True)
+    lev_front = get_row(buses, 1, 1, from_next)
+    bar_front = get_cube(buses, 1, 0, from_next)
     cap_new = capacity_of(hours, cap_ref, inv_ref, invest)
     capout_ref[...] = cap_new
     cap_bar = 2.0 * cap_new - cap_ref[...]
@@ -529,10 +524,11 @@
 
     steps = len(distances("hour"))
 
-    def totals(block, *work):
+    def totals(block, lone, *work):
         row = lax.broadcasted_iota(jnp.int32, block.shape, 0)
         lane = lax.broadcasted_iota(jnp.int32, block.shape, 1)
-        adds = (lane < buses) | ((lane < 2 * buses) & (row == 0))
+        width, parts = layout(buses, lone)
+        adds = (lane < buses) | ((lane < buses + width) & (row < parts))
         passed = []
         for k, distance in enumerate(distances("hour")):
             got = partner(block, "hour", distance)
@@ -546,41 +542,33 @@
             squares = squares + partner(squares, "region", distance)
         return block, squares, partner(squares, "region", outer), passed
 
-    halo = jnp.concatenate(
-        [ramp_dual[-1], jnp.broadcast_to(storage_dual[-1:], (TECH, buses))], axis=0
-    )
+    (halo,) = call(
+        pack_body,
+        (ramp_dual, storage_dual, generation, limit_dual, network, avail_factor, demand, tech_mask,
+         angles, net_power, levels),
+        [HBM] * 11,
+        [((2 * TECH, buses), F32)],
+        scratch=(pltpu.VMEM((rows - (rows - 1) // TECH * TECH, buses), F32), pltpu.SemaphoreType.DMA((2,))),
+        moved=1 << 28,
+        name="pack",
+    )
+    balances = all_buses(after(balance_dual, halo))
     halo = shifted(halo, "hour", 1)
-    balances = all_buses(balance_dual)
-
-    bar, new, lim, ramp, avail, high, low, invest, square, load = call(
+
+    bar, new, avail, high, low, invest, square, load, flow, ang_bar, pow_new, pow_bar = call(
         functools.partial(load_body, swap),
         (generation, limit_dual, ramp_dual, avail_factor, network, tech_mask, var_cost, ramp_rate,
-         balance_dual, demand, pattern, live_hours),
-        [HBM] * 11 + [SMEM],
-        [(cube, F32)] * 5 + [((buses, BUS), jnp.bfloat16)] * 2 + [(tech, F32)] * 2 + [(flat, F32)],
-        scratch=(
-            pltpu.VMEM(cube, jnp.bfloat16),
-            pltpu.VMEM((buses, BUS), F32),
-            pltpu.VMEM(tech, jnp.int32),
-            pltpu.VMEM(tech, F32),
-            pltpu.VMEM(tech, F32),
-            pltpu.VMEM(flat, F32),
-            pltpu.VMEM(flat, F32),
-            pltpu.SMEM(pattern.shape, jnp.int32),
-            pltpu.SemaphoreType.DMA((chunks, 4)),
-            pltpu.SemaphoreType.DMA((pieces,)),
-            pltpu.SemaphoreType.DMA((6,)),
-        ),
+         balance_dual, demand, pattern, live_hours, angles, net_power, storage_dual, *balances),
+        [VMEM] * 10 + [SMEM] * 2 + [VMEM] * (3 + pieces),
+        [(cube, F32)] * 3 + [((buses, BUS), jnp.bfloat16)] * 2 + [(tech, F32)] * 2 + [(flat, F32)] * 5,
         name="load",
     )
-    (
-        row, flow, ang_bar, pow_new, pow_bar, lev_new, lev_bar, total,
-    ) = call(
-        functools.partial(first_body, pieces),
-        (bar, lim, ramp, halo, var_cost, invest, square, balance_dual, *balances,
-         angles, net_power, levels, storage_dual, high, low),
-        [VMEM] * (8 + pieces + 6),
-        [(tech, F32)] + [(flat, F32)] * 6 + [((TECH, 4 * buses), F32)],
+    lim, ramp = limit_dual, ramp_dual
+    row, lev_new, lev_bar, total = call(
+        first_body,
+        (bar, lim, ramp, halo, var_cost, invest, square, balance_dual, levels, storage_dual, pow_bar),
+        [VMEM] * 11,
+        [(tech, F32)] + [(flat, F32)] * 2 + [((TECH, 3 * buses + layout(buses, 3)[0]), F32)],
         scratch=(shift,),
         name="first",
     )
@@ -608,7 +596,7 @@
         )
         return made["flow"]
 
-    here, squares, other, passed = totals(total, None, residual, None, product)
+    here, squares, other, passed = totals(total, 3, None, residual, None, product)
     res, res_flow = made["res"], made["flow"]
     (
         cap, gen2, lim1, ramp1, bal1, sto1, ang2, ang_bar2, pow2, pow_bar2, lev2, lev_bar2, total2,
@@ -618,7 +606,7 @@
          halo, balance_dual, res, res_flow, flow, angles, pow_new, pow_bar, lev_new, lev_bar,
          storage_dual),
         [VMEM] * (25 + steps),
-        [(tech, F32)] + [(cube, F32)] * 3 + [(flat, F32)] * 8 + [((TECH, 3 * buses), F32)],
+        [(tech, F32)] + [(cube, F32)] * 3 + [(flat, F32)] * 8 + [((TECH, 2 * buses + layout(buses, 1)[0]), F32)],
         scratch=(shift,),
         name="middle",
     )
@@ -636,7 +624,7 @@
         )
         return made["two"][0]
 
-    here2, squares2, other2, passed2 = totals(total2, None, residual2)
+    here2, squares2, other2, passed2 = totals(total2, 1, None, residual2)
     res2, bar2, gen2, ang2, lev2, pow2 = made["two"]
     cap2, lim2, ramp2, bal2, sto2 = call(
         functools.partial(last_body, hours, entries, steps),

time: 60 us -> 55.8 us (0.930)
  starting transfers between devices: 19.3 us -> 16.6 us
  Pallas kernels: 19.4 us -> 17.1 us
  waiting for transfers between devices: 17.2 us -> 19.4 us
  local copies, waits for them, and re-layouts: 1.5 us -> 0.23 us
    ppermute x14, starting transfers between devices: 16.7 us -> 14.1 us  [partner(): lax.ppermute(block, axis, [(i, i ^ distance) for i in range(lax.axis_size...]
    pallas_call x7 -> x8, Pallas kernels: 19.4 us -> 17.1 us  [call(): pl.pallas_call(body, out_shape=[jax.ShapeDtypeStruct(shape, dtype) for sh...]
    ppermute x1, waiting for transfers between devices: 0.01 us -> 1.11 us  [shifted(): return lax.ppermute(block, axis, route)]
    ppermute x14, waiting for transfers between devices: 17.2 us -> 18.3 us  [partner(): lax.ppermute(block, axis, [(i, i ^ distance) for i in range(lax.axis_size...]
    slice x1 -> x0, local copies, waits for them, and re-layouts: 0.72 us -> none  [per_device(): storage_dual[-1:]]
    squeeze x1 -> x0, local copies, waits for them, and re-layouts: 0.72 us -> none  [per_device(): ramp_dual[-1]]
  transfers between devices with their start and end apart: 15 -> 15, of which waited for: 10 -> 11; matrix products, arithmetic and copies ran while one was open for 3% -> 0% of each run, Pallas kernels for 19% -> 17%
where the time goes in v3:
time: 55.8 us; the launch traced here: 55.6 us
  waiting for transfers between devices  19.4 us (35%)
  Pallas kernels  17.1 us (31%)
  starting transfers between devices  16.6 us (30%)
  between operations  1.64 us (3%)
  other arithmetic  0.67 us (1%)
    ppermute x14, waiting for transfers between devices, partner(): lax.ppermute(block, axis, [(i, i ^ distance) for i in range(lax.axis_size...  18.3 us
    pallas_call x8, Pallas kernels, call(): pl.pallas_call(body, out_shape=[jax.ShapeDtypeStruct(shape, dtype) for sh...  17.1 us
    ppermute x14, starting transfers between devices, partner(): lax.ppermute(block, axis, [(i, i ^ distance) for i in range(lax.axis_size...  14.1 us
    ppermute x1, starting transfers between devices, shifted(): return lax.ppermute(block, axis, route)  2.49 us
  transfers between devices with their start and end apart: 15, of which 11 were waited for; matrix products, arithmetic and copies ran while one was open for 0% of the time, Pallas kernels for 17%

profile of v3, /device:TPU:0, one launch (start us, length us, event | category | flops | bytes accessed | tf_op | source)
XLA Modules:
  0.0 55.6 jit_solution(8547327744539767360)
XLA Ops:
  0.8 0.9 %pack.1 = f32[16,512]{1,0:T(8,128)S(1)} custom-call(f32[140,8,512]{2,1,0:T(8,128)} %refs_12_.1, f32[140,512]{1,0:T(8,128)} %refs_24_.1, f32[140,8,512]{2,1,0:T(8,128)} %gen_ref.1, f32[140,8,512]{2,1,0:T(8,128)} %refs_11_.1, f32[512,1024]{1,0:T(8,128)} %net_ref.1, bf16[140,8,512]{2,1,0:T(8,128)(2,1)} %av_ref.1, f32[140,512]{1,0:T(8,128)} %demand_ref.1, ...), custom_call_target="tpu_custom_call" | custom-call | flops 4194304 | bytes 268435456 | tf_op jit(solution)/shard_map/pack/pallas_call | solution.py:78
  1.7 0.2 copy-done.4
  1.9 0.5 collective-permute-start
  2.3 2.5 %collective-permute-start.1 = (f32[16,512]{1,0:T(8,128)S(1)}, f32[16,512]{1,0:T(8,128)S(1)}, u32[]{:S(2)}, u32[]{:S(2)}) collective-permute-start(f32[16,512]{1,0:T(8,128)S(1)} %pack.1), channel_id=1, source_target_pairs={{30,0},{0,2},{2,4},{4,6},{6,8},{8,10},{10,12},{12,14},{14,16},{16,... | collective-permute-start | bytes 98312 | tf_op jit(solution)/shard_map/ppermute | solution.py:28
  5.5 0.0 copy-start.10
  5.5 0.0 collective-permute-done.refs_1_
  5.6 4.1 %load.1 = (f32[140,8,512]{2,1,0:T(8,128)S(1)}, f32[140,8,512]{2,1,0:T(8,128)S(1)}, f32[140,8,512]{2,1,0:T(8,128)S(1)}, bf16[512,1024]{1,0:T(8,128)(2,1)S(1)}, bf...) custom-call(f32[140,8,512]{2,1,0:T(8,128)S(1)} %copy-done.2, ...), custom_call_target="tpu_custom_call" | custom-call | flops 4194304 | bytes 8388608 | tf_op jit(solution)/shard_map/load/pallas_call | solution.py:78
  9.8 1.1 %collective-permute-done.1.halo_ref.refs_14_ = f32[16,512]{1,0:T(8,128)S(1)} collective-permute-done((f32[16,512]{1,0:T(8,128)S(1)}, f32[16,512]{1,0:T(8,128)S(1)}, u32[]{:S(2)}, u32[]{:S(2)}) %collective-permute-start.1) | collective-permute-done | bytes 32800 | tf_op jit(solution)/shard_map/ppermute | solution.py:28
  10.9 0.2 first.1
  11.1 1.2 %collective-permute-start.2 = (f32[8,1792]{1,0:T(8,128)S(1)}, f32[8,1792]{1,0:T(8,128)S(1)}, u32[]{:S(2)}, u32[]{:S(2)}) collective-permute-start(f32[8,1792]{1,0:T(8,128)S(1)} %get-tuple-element.58.total_ref.mine_ref), channel_id=1, source_target_pairs={{0,2},{2,0},{4,6},{6,4},{8,10},{10,8},{12,14},{14,12},{16,18},{18,... | collective-permute-start | bytes 172040 | tf_op jit(solution)/shard_map/ppermute | solution.py:32
  12.3 0.0 collective-permute-start.4
  12.3 3.0 %collective-permute-done.2.refs_0_ = f32[8,1792]{1,0:T(8,128)S(1)} collective-permute-done((f32[8,1792]{1,0:T(8,128)S(1)}, f32[8,1792]{1,0:T(8,128)S(1)}, u32[]{:S(2)}, u32[]{:S(2)}) %collective-permute-start.2) | collective-permute-done | bytes 57376 | tf_op jit(solution)/shard_map/ppermute | solution.py:32
  15.4 0.1 select_add_fusion.3
  15.4 1.3 %collective-permute-start.3 = (f32[8,1792]{1,0:T(8,128)S(1)}, f32[8,1792]{1,0:T(8,128)S(1)}, u32[]{:S(2)}, u32[]{:S(2)}) collective-permute-start(f32[8,1792]{1,0:T(8,128)S(1)} %select_add_fusion.3), channel_id=1, source_target_pairs={{0,4},{2,6},{4,0},{6,2},{8,12},{10,14},{12,8},{14,10},{16,20},{18,... | collective-permute-start | bytes 172040 | tf_op jit(solution)/shard_map/ppermute | solution.py:32
  16.7 2.0 %residual1.1.refs_0_.refs_16_ = f32[140,512]{1,0:T(8,128)S(1)} custom-call(f32[140,8,512]{2,1,0:T(8,128)S(1)} %get-tuple-element.54.bar_ref.refs_8_, f32[8,1792]{1,0:T(8,128)S(1)} %get-tuple-element.58.total_ref.mine_ref, f32[140,512]{1,0:T(8,128)S(1)} %get-tuple-element.57.powbar_ref.refs_21_, f32[140,512]{1,0:T(8,128)S(1)} %get-tuple-element.59.load_ref, ...), custom_call_target="tpu_custom_call" | custom-call | flops 4194304 | bytes 8388608 | tf_op jit(solution)/shard_map/residual1/pallas_call | solution.py:78
  18.7 0.0 copy-start.14
  18.7 0.0 copy-start.15
  18.7 1.0 %collective-permute-done.3.refs_1_ = f32[8,1792]{1,0:T(8,128)S(1)} collective-permute-done((f32[8,1792]{1,0:T(8,128)S(1)}, f32[8,1792]{1,0:T(8,128)S(1)}, u32[]{:S(2)}, u32[]{:S(2)}) %collective-permute-start.3) | collective-permute-done | bytes 57376 | tf_op jit(solution)/shard_map/ppermute | solution.py:32
  19.7 0.1 select_add_fusion.2
  19.8 1.3 %collective-permute-start.5 = (f32[8,1792]{1,0:T(8,128)S(1)}, f32[8,1792]{1,0:T(8,128)S(1)}, u32[]{:S(2)}, u32[]{:S(2)}) collective-permute-start(f32[8,1792]{1,0:T(8,128)S(1)} %select_add_fusion.2), channel_id=1, source_target_pairs={{0,8},{2,10},{4,12},{6,14},{8,0},{10,2},{12,4},{14,6},{16,24},{18,... | collective-permute-start | bytes 172040 | tf_op jit(solution)/shard_map/ppermute | solution.py:32
  21.1 2.9 %collective-permute-done.5.refs_2_ = f32[8,1792]{1,0:T(8,128)S(1)} collective-permute-done((f32[8,1792]{1,0:T(8,128)S(1)}, f32[8,1792]{1,0:T(8,128)S(1)}, u32[]{:S(2)}, u32[]{:S(2)}) %collective-permute-start.5) | collective-permute-done | bytes 57376 | tf_op jit(solution)/shard_map/ppermute | solution.py:32
  24.0 0.1 select_add_fusion.1
  24.1 2.7 %collective-permute-start.6 = (f32[8,1792]{1,0:T(8,128)S(1)}, f32[8,1792]{1,0:T(8,128)S(1)}, u32[]{:S(2)}, u32[]{:S(2)}) collective-permute-start(f32[8,1792]{1,0:T(8,128)S(1)} %select_add_fusion.1), channel_id=1, source_target_pairs={{0,16},{2,18},{4,20},{6,22},{8,24},{10,26},{12,28},{14,30},{16,0},... | collective-permute-start | bytes 172040 | tf_op jit(solution)/shard_map/ppermute | solution.py:32
  26.8 0.0 collective-permute-done.7.refs_1_
  26.8 1.2 %product.1.refs_17_ = f32[140,512]{1,0:T(8,128)S(1)} custom-call(bf16[512,1024]{1,0:T(8,128)(2,1)S(1)} %get-tuple-element.60.high_ref, bf16[512,1024]{1,0:T(8,128)(2,1)S(1)} %get-tuple-element.61.low_ref, f32[140,512]{1,0:T(8,128)S(1)} %residual1.1.refs_0_.refs_16_, f32[140,512]{1,0:T(8,128)S(1)} %collective-permute-done.7.refs_1_), custom_call_target="tpu_custom_call" | custom-call | flops 4194304 | bytes 8388608 | tf_op jit(solution)/shard_map/product/pallas_call | solution.py:78
  28.0 1.3 %collective-permute-done.6.refs_3_ = f32[8,1792]{1,0:T(8,128)S(1)} collective-permute-done((f32[8,1792]{1,0:T(8,128)S(1)}, f32[8,1792]{1,0:T(8,128)S(1)}, u32[]{:S(2)}, u32[]{:S(2)}) %collective-permute-start.6) | collective-permute-done | bytes 57376 | tf_op jit(solution)/shard_map/ppermute | solution.py:32
  29.2 0.1 select_add_fusion.here_ref.squares_ref
  29.3 0.1 collective-permute-start.8
  29.4 1.2 %collective-permute-done.8.other_ref = f32[8,1792]{1,0:T(8,128)S(1)} collective-permute-done((f32[8,1792]{1,0:T(8,128)S(1)}, f32[8,1792]{1,0:T(8,128)S(1)}, u32[]{:S(2)}, u32[]{:S(2)}) %collective-permute-start.8) | collective-permute-done | bytes 57376 | tf_op jit(solution)/shard_map/ppermute | solution.py:32
  30.6 3.1 %middle.1 = (f32[8,512]{1,0:T(8,128)S(1)}, f32[140,8,512]{2,1,0:T(8,128)S(1)}, f32[140,8,512]{2,1,0:T(8,128)S(1)}, f32[140,8,512]{2,1,0:T(8,128)S(1)}, f32[140,5...) custom-call(f32[8,1792]{1,0:T(8,128)S(1)} %select_add_fusion.here_re, ...), custom_call_target="tpu_custom_call" | custom-call | flops 4194304 | bytes 8388608 | tf_op jit(solution)/shard_map/middle/pallas_call | solution.py:78
  33.7 1.5 %collective-permute-start.10 = (f32[8,1152]{1,0:T(8,128)S(1)}, f32[8,1152]{1,0:T(8,128)S(1)}, u32[]{:S(2)}, u32[]{:S(2)}) collective-permute-start(f32[8,1152]{1,0:T(8,128)S(1)} %get-tuple-element.82), channel_id=1, source_target_pairs={{0,2},{2,0},{4,6},{6,4},{8,10},{10,8},{12,14},{14,12},{16,18},{18,... | collective-permute-start | bytes 110600 | tf_op jit(solution)/shard_map/ppermute | solution.py:32
  35.2 0.0 collective-permute-start.9
  35.2 2.5 %collective-permute-done.10.refs_0_ = f32[8,1152]{1,0:T(8,128)S(1)} collective-permute-done((f32[8,1152]{1,0:T(8,128)S(1)}, f32[8,1152]{1,0:T(8,128)S(1)}, u32[]{:S(2)}, u32[]{:S(2)}) %collective-permute-start.10) | collective-permute-done | bytes 36896 | tf_op jit(solution)/shard_map/ppermute | solution.py:32
  37.7 0.1 select_add_fusion.7
  37.8 1.5 %collective-permute-start.11 = (f32[8,1152]{1,0:T(8,128)S(1)}, f32[8,1152]{1,0:T(8,128)S(1)}, u32[]{:S(2)}, u32[]{:S(2)}) collective-permute-start(f32[8,1152]{1,0:T(8,128)S(1)} %select_add_fusion.7), channel_id=1, source_target_pairs={{0,4},{2,6},{4,0},{6,2},{8,12},{10,14},{12,8},{14,10},{16,20},{18,... | collective-permute-start | bytes 110600 | tf_op jit(solution)/shard_map/ppermute | solution.py:32
  39.3 0.0 collective-permute-done.9.refs_1_
  39.3 2.2 %residual2.1 = (f32[140,512]{1,0:T(8,128)S(1)}, f32[140,8,512]{2,1,0:T(8,128)S(1)}, f32[140,8,512]{2,1,0:T(8,128)}, f32[140,512]{1,0:T(8,128)}, f32[140,512]{1,0:T(8,128)}, /*index=5*/f32[140,512]{1,0:T(8,128)}) custom-call(f32[140,8,512]{2,1,0:T(8,128)S(1)} %get-tuple-element.72.gen_ref, f32[140,512]{1,0:T(8,128)S(1)} %get-tuple-element.73.ang_ref, ...), custom_call_target="tpu_custom_call" | custom-call | flops 4194304 | bytes 8388608 | tf_op jit(solution)/shard_map/residual2/pallas_call | solution.py:78
  41.5 0.3 collective-permute-done.11.refs_1_
  41.8 0.1 select_add_fusion.6
  41.9 1.3 %collective-permute-start.12 = (f32[8,1152]{1,0:T(8,128)S(1)}, f32[8,1152]{1,0:T(8,128)S(1)}, u32[]{:S(2)}, u32[]{:S(2)}) collective-permute-start(f32[8,1152]{1,0:T(8,128)S(1)} %select_add_fusion.6), channel_id=1, source_target_pairs={{0,8},{2,10},{4,12},{6,14},{8,0},{10,2},{12,4},{14,6},{16,24},{18,... | collective-permute-start | bytes 110600 | tf_op jit(solution)/shard_map/ppermute | solution.py:32
  43.2 2.7 %collective-permute-done.12.refs_2_ = f32[8,1152]{1,0:T(8,128)S(1)} collective-permute-done((f32[8,1152]{1,0:T(8,128)S(1)}, f32[8,1152]{1,0:T(8,128)S(1)}, u32[]{:S(2)}, u32[]{:S(2)}) %collective-permute-start.12) | collective-permute-done | bytes 36896 | tf_op jit(solution)/shard_map/ppermute | solution.py:32
  45.9 0.1 select_add_fusion.5
  46.0 2.8 %collective-permute-start.13 = (f32[8,1152]{1,0:T(8,128)S(1)}, f32[8,1152]{1,0:T(8,128)S(1)}, u32[]{:S(2)}, u32[]{:S(2)}) collective-permute-start(f32[8,1152]{1,0:T(8,128)S(1)} %select_add_fusion.5), channel_id=1, source_target_pairs={{0,16},{2,18},{4,20},{6,22},{8,24},{10,26},{12,28},{14,30},{16,0},... | collective-permute-start | bytes 110600 | tf_op jit(solution)/shard_map/ppermute | solution.py:32
  48.8 2.1 %collective-permute-done.13.refs_3_ = f32[8,1152]{1,0:T(8,128)S(1)} collective-permute-done((f32[8,1152]{1,0:T(8,128)S(1)}, f32[8,1152]{1,0:T(8,128)S(1)}, u32[]{:S(2)}, u32[]{:S(2)}) %collective-permute-start.13) | collective-permute-done | bytes 36896 | tf_op jit(solution)/shard_map/ppermute | solution.py:32
  50.9 0.1 select_add_fusion.4.here_ref.squares_ref
  51.0 0.1 collective-permute-start.14
  51.1 1.2 %collective-permute-done.14.other_ref = f32[8,1152]{1,0:T(8,128)S(1)} collective-permute-done((f32[8,1152]{1,0:T(8,128)S(1)}, f32[8,1152]{1,0:T(8,128)S(1)}, u32[]{:S(2)}, u32[]{:S(2)}) %collective-permute-start.14) | collective-permute-done | bytes 36896 | tf_op jit(solution)/shard_map/ppermute | solution.py:32
  52.3 3.3 %last.1 = (f32[8,512]{1,0:T(8,128)}, f32[140,8,512]{2,1,0:T(8,128)}, f32[140,8,512]{2,1,0:T(8,128)}, f32[140,512]{1,0:T(8,128)}, f32[140,512]{1,0:T(8,128)}) custom-call(f32[8,1152]{1,0:T(8,128)S(1)} %select_add_fusion.4.here_ref.squares_ref, f32[8,1152]{1,0:T(8,128)S(1)} %select_add_fusion.4.here_ref.squares_ref, ...), custom_call_target="tpu_custom_call" | custom-call | flops 4194304 | bytes 8388608 | tf_op jit(solution)/shard_map/last/pallas_call | solution.py:78
  (36 shorter events, 0.1 us)
Async XLA Ops:
  0.6 4.8 %copy-start.2 = (f32[140,8,512]{2,1,0:T(8,128)S(1)}, f32[140,8,512]{2,1,0:T(8,128)}, u32[]{:S(2)}) copy-start(f32[140,8,512]{2,1,0:T(8,128)} %gen_ref.1) | copy-start | bytes 6881284
  0.7 4.8 %copy-start = (f32[140,8,512]{2,1,0:T(8,128)S(1)}, f32[140,8,512]{2,1,0:T(8,128)}, u32[]{:S(2)}) copy-start(f32[140,8,512]{2,1,0:T(8,128)} %refs_11_.1) | copy-start | bytes 6881284
  0.7 4.8 %copy-start.1 = (f32[140,8,512]{2,1,0:T(8,128)S(1)}, f32[140,8,512]{2,1,0:T(8,128)}, u32[]{:S(2)}) copy-start(f32[140,8,512]{2,1,0:T(8,128)} %refs_12_.1) | copy-start | bytes 6881284
  0.7 4.8 %copy-start.6 = (bf16[140,8,512]{2,1,0:T(8,128)(2,1)S(1)}, bf16[140,8,512]{2,1,0:T(8,128)(2,1)}, u32[]{:S(2)}) copy-start(bf16[140,8,512]{2,1,0:T(8,128)(2,1)} %av_ref.1) | copy-start | bytes 3440644
  0.7 4.8 %copy-start.3 = (f32[512,1024]{1,0:T(8,128)S(1)}, f32[512,1024]{1,0:T(8,128)}, u32[]{:S(2)}) copy-start(f32[512,1024]{1,0:T(8,128)} %net_ref.1) | copy-start | bytes 6291460
  0.7 4.8 %copy-start.13 = (s32[8,512]{1,0:T(8,128)S(1)}, s32[8,512]{1,0:T(8,128)}, u32[]{:S(2)}) copy-start(s32[8,512]{1,0:T(8,128)} %mask_ref.1) | copy-start | bytes 49156
  0.7 4.8 %copy-start.8 = (f32[140,512]{1,0:T(8,128)S(1)}, f32[140,512]{1,0:T(8,128)}, u32[]{:S(2)}) copy-start(f32[140,512]{1,0:T(8,128)} %demand_ref.1) | copy-start | bytes 860164
  0.7 4.8 %copy-start.7 = (f32[140,512]{1,0:T(8,128)S(1)}, f32[140,512]{1,0:T(8,128)}, u32[]{:S(2)}) copy-start(f32[140,512]{1,0:T(8,128)} %refs_19_.1) | copy-start | bytes 860164
  0.7 4.8 %copy-start.9 = (f32[140,512]{1,0:T(8,128)S(1)}, f32[140,512]{1,0:T(8,128)}, u32[]{:S(2)}) copy-start(f32[140,512]{1,0:T(8,128)} %pow_ref.1) | copy-start | bytes 860164
  0.7 4.8 %copy-start.5 = (f32[140,512]{1,0:T(8,128)S(1)}, f32[140,512]{1,0:T(8,128)}, u32[]{:S(2)}) copy-start(f32[140,512]{1,0:T(8,128)} %refs_24_.1) | copy-start | bytes 860164
  0.7 1.1 %copy-start.4 = (f32[140,512]{1,0:T(8,128)S(1)}, f32[140,512]{1,0:T(8,128)}, u32[]{:S(2)}) copy-start(f32[140,512]{1,0:T(8,128)} %refs_15_.1) | copy-start | bytes 860164
  0.8 4.8 %copy-start.11 = (f32[8,512]{1,0:T(8,128)S(1)}, f32[8,512]{1,0:T(8,128)}, u32[]{:S(2)}) copy-start(f32[8,512]{1,0:T(8,128)} %refs_7_.3) | copy-start | bytes 49156
  0.8 4.8 %copy-start.12 = (f32[8,512]{1,0:T(8,128)S(1)}, f32[8,512]{1,0:T(8,128)}, u32[]{:S(2)}) copy-start(f32[8,512]{1,0:T(8,128)} %refs_6_.5) | copy-start | bytes 49156
  0.8 4.8 %copy-start.16 = (s32[8,8]{1,0:T(8,128)S(1)}, s32[8,8]{1,0:T(8,128)}, u32[]{:S(2)}) copy-start(s32[8,8]{1,0:T(8,128)} %pat_s.1) | copy-start | bytes 772
  1.9 3.6 %collective-permute-start = (f32[140,512]{1,0:T(8,128)S(1)}, f32[140,512]{1,0:T(8,128)S(1)}, u32[]{:S(2)}, u32[]{:S(2)}) collective-permute-start(f32[140,512]{1,0:T(8,128)S(1)} %copy-done.4), channel_id=1, source_target_pairs={{0,1},{1,0},{2,3},{3,2},{4,5},{5,4},{6,7},{7,6},{8,9},{9,8},{10,11... | collective-permute-start | bytes 860168 | tf_op jit(solution)/shard_map/ppermute | solution.py:32
  2.3 8.5 %collective-permute-start.1 = (f32[16,512]{1,0:T(8,128)S(1)}, f32[16,512]{1,0:T(8,128)S(1)}, u32[]{:S(2)}, u32[]{:S(2)}) collective-permute-start(f32[16,512]{1,0:T(8,128)S(1)} %pack.1), channel_id=1, source_target_pairs={{30,0},{0,2},{2,4},{4,6},{6,8},{8,10},{10,12},{12,14},{14,16},{16,... | collective-permute-start | bytes 98312 | tf_op jit(solution)/shard_map/ppermute | solution.py:28
  5.5 5.4 %copy-start.10 = (f32[140,512]{1,0:T(8,128)S(1)}, f32[140,512]{1,0:T(8,128)}, u32[]{:S(2)}) copy-start(f32[140,512]{1,0:T(8,128)} %lev_ref.1) | copy-start | bytes 860164
  11.1 4.2 %collective-permute-start.2 = (f32[8,1792]{1,0:T(8,128)S(1)}, f32[8,1792]{1,0:T(8,128)S(1)}, u32[]{:S(2)}, u32[]{:S(2)}) collective-permute-start(f32[8,1792]{1,0:T(8,128)S(1)} %get-tuple-element.58.total_ref.mine_ref), channel_id=1, source_target_pairs={{0,2},{2,0},{4,6},{6,4},{8,10},{10,8},{12,14},{14,12},{16,18},{18,... | collective-permute-start | bytes 172040 | tf_op jit(solution)/shard_map/ppermute | solution.py:32
  12.3 4.4 %collective-permute-start.4 = (f32[140,512]{1,0:T(8,128)S(1)}, f32[140,512]{1,0:T(8,128)S(1)}, u32[]{:S(2)}, u32[]{:S(2)}) collective-permute-start(f32[140,512]{1,0:T(8,128)S(1)} %get-tuple-element.62.refs_0_), channel_id=1, source_target_pairs={{0,1},{1,0},{2,3},{3,2},{4,5},{5,4},{6,7},{7,6},{8,9},{9,8},{10,11... | collective-permute-start | bytes 860168 | tf_op jit(solution)/shard_map/ppermute | solution.py:32
  15.4 4.2 %collective-permute-start.3 = (f32[8,1792]{1,0:T(8,128)S(1)}, f32[8,1792]{1,0:T(8,128)S(1)}, u32[]{:S(2)}, u32[]{:S(2)}) collective-permute-start(f32[8,1792]{1,0:T(8,128)S(1)} %select_add_fusion.3), channel_id=1, source_target_pairs={{0,4},{2,6},{4,0},{6,2},{8,12},{10,14},{12,8},{14,10},{16,20},{18,... | collective-permute-start | bytes 172040 | tf_op jit(solution)/shard_map/ppermute | solution.py:32
  18.7 11.9 %copy-start.14 = (f32[8,512]{1,0:T(8,128)S(1)}, f32[8,512]{1,0:T(8,128)}, u32[]{:S(2)}) copy-start(f32[8,512]{1,0:T(8,128)} %refs_5_.5) | copy-start | bytes 49156
  18.7 11.9 %copy-start.15 = (f32[8,512]{1,0:T(8,128)S(1)}, f32[8,512]{1,0:T(8,128)}, u32[]{:S(2)}) copy-start(f32[8,512]{1,0:T(8,128)} %refs_4_.3) | copy-start | bytes 49156
  19.8 4.2 %collective-permute-start.5 = (f32[8,1792]{1,0:T(8,128)S(1)}, f32[8,1792]{1,0:T(8,128)S(1)}, u32[]{:S(2)}, u32[]{:S(2)}) collective-permute-start(f32[8,1792]{1,0:T(8,128)S(1)} %select_add_fusion.2), channel_id=1, source_target_pairs={{0,8},{2,10},{4,12},{6,14},{8,0},{10,2},{12,4},{14,6},{16,24},{18,... | collective-permute-start | bytes 172040 | tf_op jit(solution)/shard_map/ppermute | solution.py:32
  21.1 5.7 %collective-permute-start.7 = (f32[140,512]{1,0:T(8,128)S(1)}, f32[140,512]{1,0:T(8,128)S(1)}, u32[]{:S(2)}, u32[]{:S(2)}) collective-permute-start(f32[140,512]{1,0:T(8,128)S(1)} %residual1.1.refs_0_.refs_16_), channel_id=1, source_target_pairs={{0,1},{1,0},{2,3},{3,2},{4,5},{5,4},{6,7},{7,6},{8,9},{9,8},{10,11... | collective-permute-start | bytes 860168 | tf_op jit(solution)/shard_map/ppermute | solution.py:32
  24.1 5.1 %collective-permute-start.6 = (f32[8,1792]{1,0:T(8,128)S(1)}, f32[8,1792]{1,0:T(8,128)S(1)}, u32[]{:S(2)}, u32[]{:S(2)}) collective-permute-start(f32[8,1792]{1,0:T(8,128)S(1)} %select_add_fusion.1), channel_id=1, source_target_pairs={{0,16},{2,18},{4,20},{6,22},{8,24},{10,26},{12,28},{14,30},{16,0},... | collective-permute-start | bytes 172040 | tf_op jit(solution)/shard_map/ppermute | solution.py:32
  29.3 1.3 %collective-permute-start.8 = (f32[8,1792]{1,0:T(8,128)S(1)}, f32[8,1792]{1,0:T(8,128)S(1)}, u32[]{:S(2)}, u32[]{:S(2)}) collective-permute-start(f32[8,1792]{1,0:T(8,128)S(1)} %select_add_fusion.here_ref.squares_ref), channel_id=1, source_target_pairs={{0,1},{1,0},{2,3},{3,2},{4,5},{5,4},{6,7},{7,6},{8,9},{9,8},{10,11... | collective-permute-start | bytes 172040 | tf_op jit(solution)/shard_map/ppermute | solution.py:32
  33.7 4.0 %collective-permute-start.10 = (f32[8,1152]{1,0:T(8,128)S(1)}, f32[8,1152]{1,0:T(8,128)S(1)}, u32[]{:S(2)}, u32[]{:S(2)}) collective-permute-start(f32[8,1152]{1,0:T(8,128)S(1)} %get-tuple-element.82), channel_id=1, source_target_pairs={{0,2},{2,0},{4,6},{6,4},{8,10},{10,8},{12,14},{14,12},{16,18},{18,... | collective-permute-start | bytes 110600 | tf_op jit(solution)/shard_map/ppermute | solution.py:32
  35.2 4.1 %collective-permute-start.9 = (f32[140,512]{1,0:T(8,128)S(1)}, f32[140,512]{1,0:T(8,128)S(1)}, u32[]{:S(2)}, u32[]{:S(2)}) collective-permute-start(f32[140,512]{1,0:T(8,128)S(1)} %get-tuple-element.77.refs_0_), channel_id=1, source_target_pairs={{0,1},{1,0},{2,3},{3,2},{4,5},{5,4},{6,7},{7,6},{8,9},{9,8},{10,11... | collective-permute-start | bytes 860168 | tf_op jit(solution)/shard_map/ppermute | solution.py:32
  37.8 4.0 %collective-permute-start.11 = (f32[8,1152]{1,0:T(8,128)S(1)}, f32[8,1152]{1,0:T(8,128)S(1)}, u32[]{:S(2)}, u32[]{:S(2)}) collective-permute-start(f32[8,1152]{1,0:T(8,128)S(1)} %select_add_fusion.7), channel_id=1, source_target_pairs={{0,4},{2,6},{4,0},{6,2},{8,12},{10,14},{12,8},{14,10},{16,20},{18,... | collective-permute-start | bytes 110600 | tf_op jit(solution)/shard_map/ppermute | solution.py:32
  41.9 4.0 %collective-permute-start.12 = (f32[8,1152]{1,0:T(8,128)S(1)}, f32[8,1152]{1,0:T(8,128)S(1)}, u32[]{:S(2)}, u32[]{:S(2)}) collective-permute-start(f32[8,1152]{1,0:T(8,128)S(1)} %select_add_fusion.6), channel_id=1, source_target_pairs={{0,8},{2,10},{4,12},{6,14},{8,0},{10,2},{12,4},{14,6},{16,24},{18,... | collective-permute-start | bytes 110600 | tf_op jit(solution)/shard_map/ppermute | solution.py:32
  46.0 4.9 %collective-permute-start.13 = (f32[8,1152]{1,0:T(8,128)S(1)}, f32[8,1152]{1,0:T(8,128)S(1)}, u32[]{:S(2)}, u32[]{:S(2)}) collective-permute-start(f32[8,1152]{1,0:T(8,128)S(1)} %select_add_fusion.5), channel_id=1, source_target_pairs={{0,16},{2,18},{4,20},{6,22},{8,24},{10,26},{12,28},{14,30},{16,0},... | collective-permute-start | bytes 110600 | tf_op jit(solution)/shard_map/ppermute | solution.py:32
  51.0 1.3 %collective-permute-start.14 = (f32[8,1152]{1,0:T(8,128)S(1)}, f32[8,1152]{1,0:T(8,128)S(1)}, u32[]{:S(2)}, u32[]{:S(2)}) collective-permute-start(f32[8,1152]{1,0:T(8,128)S(1)} %select_add_fusion.4.here_ref.squares_ref), channel_id=1, source_target_pairs={{0,1},{1,0},{2,3},{3,2},{4,5},{5,4},{6,7},{7,6},{8,9},{9,8},{10,11... | collective-permute-start | bytes 110600 | tf_op jit(solution)/shard_map/ppermute | solution.py:32

commit v4 on v3

--- a/solution.py
+++ b/solution.py
@@ -266,11 +266,13 @@
         total_ref, 3, invest_ref[...], add_squares(square_ref[...], new - gen, lev_new - lev_old),
         (levbar_ref[0:1], levbar_ref[rows - 1 : rows], powbar_ref[rows - 1 : rows]),
     )
-    put_cubes(total_ref, 3, 2.0 * new - gen, bar_ref[rows - 1])
+    odd = lax.rem(lax.axis_index("hour"), 2) == 1
+    begin, end = 2.0 * new - gen, bar_ref[rows - 1]
+    put_cubes(total_ref, 3, jnp.where(odd, end, begin), jnp.where(odd, begin, end))
 
 
 def residual_one_body(
-    pieces, bar_ref, total_ref, powbar_ref, load_ref, high_ref, low_ref, *refs,
+    pieces, bar_ref, row_ref, powbar_ref, load_ref, high_ref, low_ref, *refs,
 ):
     sources, (out_ref, sum_ref) = refs[:pieces], refs[pieces:]
     rows, _, buses = bar_ref.shape
@@ -284,8 +286,7 @@
         return 0
 
     lax.fori_loop(0, rows // unroll, several, 0)
-    bar = get_cube(buses, 3, 0, total_ref.__getitem__)
-    sum_ref[0:1] = jnp.sum(bar, axis=0, keepdims=True)
+    sum_ref[0:1] = jnp.sum(2.0 * row_ref[...] - bar_ref[0], axis=0, keepdims=True)
     out_ref[...] = sum_ref[...] + powbar_ref[...] - flow - load_ref[...]
 
 
@@ -298,7 +299,7 @@
 
 
 def middle_body(
-    hours, entries, steps, here_ref, squares_ref, other_ref, mine_ref, *refs,
+    hours, entries, steps, here_ref, squares_ref, other_ref, *refs,
 ):
     passed, refs = refs[:steps], refs[steps:]
     (
@@ -313,10 +314,12 @@
     from_next = functools.partial(neighbour, passed, True)
     from_last = functools.partial(neighbour, passed, False)
     lev_front = get_row(buses, 3, 1, from_next)
-    bar_front = get_cube(buses, 3, 0, from_next)
     lev_behind = get_row(buses, 3, 2, from_last)
     pow_behind = get_row(buses, 3, 3, from_last)
-    bar_behind = get_cube(buses, 3, 1, from_last)
+    odd = lax.rem(lax.axis_index("hour"), 2) == 1
+    direct = get_cube(buses, 3, 1, passed[0].__getitem__)
+    bar_front = jnp.where(odd, get_cube(buses, 3, 0, from_next), direct)
+    bar_behind = jnp.where(odd, direct, get_cube(buses, 3, 0, from_last))
     cap_new = capacity_of(hours, cap_ref, inv_ref, invest)
     capout_ref[...] = cap_new
     cap_bar = 2.0 * cap_new - cap_ref[...]
@@ -373,7 +376,7 @@
             put_cubes(out_ref, 1, 2.0 * gen - old)
         return bar_next, ramp, limit_sum, ramp_sum, squares
 
-    bar = get_cube(buses, 3, 0, mine_ref.__getitem__)
+    bar = 2.0 * row_ref[...] - bar_ref[0]
     before = jnp.maximum(0.0, halo_ref[:TECH] + step_size * (bar - bar_behind - ramp_cap))
     zero = jnp.zeros((TECH, buses), F32)
     carry = (bar, before, zero, zero, squares)
@@ -435,7 +438,7 @@
     (
         cap_ref, inv_ref, rr_ref,
         bar_ref, lim_ref, ramp_ref, avail_ref, bal_ref, res_ref, sto_ref, levbar_ref, powbar_ref,
-        capout_ref, lim_h, ramp_h, balout_ref, stoout_ref, lim_v, ramp_v, shift_ref, sems,
+        cap_h, lim_h, ramp_h, bal_h, sto_h, cap_v, lim_v, ramp_v, bal_v, sto_v, shift_ref, sems, small_sems,
     ) = refs
     rows, _, buses = bar_ref.shape
     chunk = divisor(rows, 28)
@@ -446,7 +449,18 @@
     lev_front = get_row(buses, 1, 1, from_next)
     bar_front = get_cube(buses, 1, 0, from_next)
     cap_new = capacity_of(hours, cap_ref, inv_ref, invest)
-    capout_ref[...] = cap_new
+    cap_v[...] = cap_new
+    bal_v[...] = bal_ref[...] + step_size * res_ref[...]
+    lev_bar = levbar_ref[...]
+    shift_ref[8 : 8 + rows] = lev_bar
+    shift_ref[8 + rows : 9 + rows] = lev_front
+    sto_v[...] = sto_ref[...] + step_size * (shift_ref[9 : 9 + rows] - lev_bar + powbar_ref[...])
+    small = [
+        pltpu.make_async_copy(source, target, small_sems.at[k])
+        for k, (source, target) in enumerate(((cap_v, cap_h), (bal_v, bal_h), (sto_v, sto_h)))
+    ]
+    for copy in small:
+        copy.start()
     cap_bar = 2.0 * cap_new - cap_ref[...]
     ramp_cap = rr_ref[...] * cap_bar
 
@@ -478,14 +492,11 @@
             bar = step(t, bar, last=t == rows - 1)
         for copy in copies(i):
             copy.start()
-    balout_ref[...] = bal_ref[...] + step_size * res_ref[...]
-    lev_bar = levbar_ref[...]
-    shift_ref[8 : 8 + rows] = lev_bar
-    shift_ref[8 + rows : 9 + rows] = lev_front
-    stoout_ref[...] = sto_ref[...] + step_size * (shift_ref[9 : 9 + rows] - lev_bar + powbar_ref[...])
     for i in range(chunks):
         for copy in copies(i):
             copy.wait()
+    for copy in small:
+        copy.wait()
 
 
 def per_device(
@@ -524,7 +535,7 @@
 
     steps = len(distances("hour"))
 
-    def totals(block, lone, *work):
+    def totals(block, lone, once, *work):
         row = lax.broadcasted_iota(jnp.int32, block.shape, 0)
         lane = lax.broadcasted_iota(jnp.int32, block.shape, 1)
         width, parts = layout(buses, lone)
@@ -535,7 +546,9 @@
             passed.append(got)
             if k < len(work) and work[k]:
                 block = after(block, work[k]())
-            block = got + jnp.where(adds, block, 0.0)
+            block = got + jnp.where(adds[:, : block.shape[1]], block, 0.0)
+            if k == 0:
+                block = block[:, : block.shape[1] - once]
         squares = block
         *inner, outer = distances("region")
         for distance in inner:
@@ -552,7 +565,7 @@
         moved=1 << 28,
         name="pack",
     )
-    balances = all_buses(after(balance_dual, halo))
+    balances = all_buses(balance_dual)
     halo = shifted(halo, "hour", 1)
 
     bar, new, avail, high, low, invest, square, load, flow, ang_bar, pow_new, pow_bar = call(
@@ -578,7 +591,7 @@
     def residual():
         (made["res"],) = call(
             functools.partial(residual_one_body, pieces),
-            (bar, total, pow_bar, load, high, low, *sources),
+            (bar, row, pow_bar, load, high, low, *sources),
             [VMEM] * (6 + pieces),
             [(flat, F32)],
             scratch=(pltpu.VMEM(flat, F32),),
@@ -596,16 +609,16 @@
         )
         return made["flow"]
 
-    here, squares, other, passed = totals(total, 3, None, residual, None, product)
+    here, squares, other, passed = totals(total, 3, buses, None, residual, None, product)
     res, res_flow = made["res"], made["flow"]
     (
         cap, gen2, lim1, ramp1, bal1, sto1, ang2, ang_bar2, pow2, pow_bar2, lev2, lev_bar2, total2,
     ) = call(
         functools.partial(middle_body, hours, entries, steps),
-        (here, squares, other, total, *passed, capacity, inv_cost, ramp_rate, var_cost, bar, new, row, lim, ramp, avail,
+        (here, squares, other, *passed, capacity, inv_cost, ramp_rate, var_cost, bar, new, row, lim, ramp, avail,
          halo, balance_dual, res, res_flow, flow, angles, pow_new, pow_bar, lev_new, lev_bar,
          storage_dual),
-        [VMEM] * (25 + steps),
+        [VMEM] * (24 + steps),
         [(tech, F32)] + [(cube, F32)] * 3 + [(flat, F32)] * 8 + [((TECH, 2 * buses + layout(buses, 1)[0]), F32)],
         scratch=(shift,),
         name="middle",
@@ -624,7 +637,7 @@
         )
         return made["two"][0]
 
-    here2, squares2, other2, passed2 = totals(total2, 1, None, residual2)
+    here2, squares2, other2, passed2 = totals(total2, 1, 0, None, residual2)
     res2, bar2, gen2, ang2, lev2, pow2 = made["two"]
     cap2, lim2, ramp2, bal2, sto2 = call(
         functools.partial(last_body, hours, entries, steps),
@@ -632,9 +645,10 @@
          lev_bar2, pow_bar2),
         [VMEM] * (15 + steps),
         [(tech, F32), (cube, F32), (cube, F32), (flat, F32), (flat, F32)],
-        out_specs=[VMEM, HBM, HBM, VMEM, VMEM],
+        out_specs=[HBM] * 5,
         scratch=(
-            pltpu.VMEM(cube, F32), pltpu.VMEM(cube, F32), shift, pltpu.SemaphoreType.DMA((chunks, 2)),
+            pltpu.VMEM(tech, F32), pltpu.VMEM(cube, F32), pltpu.VMEM(cube, F32), pltpu.VMEM(flat, F32),
+            pltpu.VMEM(flat, F32), shift, pltpu.SemaphoreType.DMA((chunks, 2)), pltpu.SemaphoreType.DMA((3,)),
         ),
         name="last",
     )

time: 55.8 us -> 54.4 us (0.975)
  starting transfers between devices: 16.6 us -> 15.2 us
  waiting for transfers between devices: 19.4 us -> 20.3 us
  Pallas kernels: 17.1 us -> 16.5 us
    ppermute x14, starting transfers between devices: 14.1 us -> 12.8 us  [partner(): lax.ppermute(block, axis, [(i, i ^ distance) for i in range(lax.axis_size...]
    ppermute x14, waiting for transfers between devices: 18.3 us -> 19.1 us  [partner(): lax.ppermute(block, axis, [(i, i ^ distance) for i in range(lax.axis_size...]
    pallas_call x8, Pallas kernels: 17.1 us -> 16.5 us  [call(): pl.pallas_call(body, out_shape=[jax.ShapeDtypeStruct(shape, dtype) for sh...]
  transfers between devices with their start and end apart: 15 -> 15, of which waited for: 11 -> 11; matrix products, arithmetic and copies ran while one was open for 0% -> 0% of each run, Pallas kernels for 17% -> 19%
where the time goes in v4:
time: 54.4 us; the launch traced here: 54.2 us
  waiting for transfers between devices  20.3 us (37%)
  Pallas kernels  16.5 us (30%)
  starting transfers between devices  15.2 us (28%)
  between operations  1.65 us (3%)
    ppermute x14, waiting for transfers between devices, partner(): lax.ppermute(block, axis, [(i, i ^ distance) for i in range(lax.axis_size...  19.1 us
    pallas_call x8, Pallas kernels, call(): pl.pallas_call(body, out_shape=[jax.ShapeDtypeStruct(shape, dtype) for sh...  16.5 us
    ppermute x14, starting transfers between devices, partner(): lax.ppermute(block, axis, [(i, i ^ distance) for i in range(lax.axis_size...  12.8 us
    ppermute x1, starting transfers between devices, shifted(): return lax.ppermute(block, axis, route)  2.39 us
    ppermute x1, waiting for transfers between devices, shifted(): return lax.ppermute(block, axis, route)  1.24 us
  transfers between devices with their start and end apart: 15, of which 11 were waited for; matrix products, arithmetic and copies ran while one was open for 0% of the time, Pallas kernels for 19%

profile of v4, /device:TPU:0, one launch (start us, length us, event | category | flops | bytes accessed | tf_op | source)
XLA Modules:
  0.0 54.2 jit_solution(13485691039424569175)
XLA Ops:
  0.6 0.0 copy-start.4
  0.8 0.5 collective-permute-start
  1.3 1.1 %pack.1 = f32[16,512]{1,0:T(8,128)S(1)} custom-call(f32[140,8,512]{2,1,0:T(8,128)} %refs_12_.1, f32[140,512]{1,0:T(8,128)} %refs_24_.1, f32[140,8,512]{2,1,0:T(8,128)} %refs_0_.3, f32[140,8,512]{2,1,0:T(8,128)} %refs_11_.1, f32[512,1024]{1,0:T(8,128)} %refs_2_.1, bf16[140,8,512]{2,1,0:T(8,128)(2,1)} %refs_3_.1, f32[140,512]{1,0:T(8,128)} %refs_4_.2, ...), custom_call_target="tpu_custom_call" | custom-call | flops 4194304 | bytes 268435456 | tf_op jit(solution)/shard_map/pack/pallas_call | solution.py:78
  2.4 2.4 %collective-permute-start.1 = (f32[16,512]{1,0:T(8,128)S(1)}, f32[16,512]{1,0:T(8,128)S(1)}, u32[]{:S(2)}, u32[]{:S(2)}) collective-permute-start(f32[16,512]{1,0:T(8,128)S(1)} %pack.1), channel_id=1, source_target_pairs={{30,0},{0,2},{2,4},{4,6},{6,8},{8,10},{10,12},{12,14},{14,16},{16,... | collective-permute-start | bytes 98312 | tf_op jit(solution)/shard_map/ppermute | solution.py:28
  5.4 0.0 copy-start.10
  5.4 0.0 collective-permute-done.refs_1_
  5.6 4.1 %load.1 = (f32[140,8,512]{2,1,0:T(8,128)S(1)}, f32[140,8,512]{2,1,0:T(8,128)S(1)}, f32[140,8,512]{2,1,0:T(8,128)S(1)}, bf16[512,1024]{1,0:T(8,128)(2,1)S(1)}, bf...) custom-call(f32[140,8,512]{2,1,0:T(8,128)S(1)} %copy-done.2, ...), custom_call_target="tpu_custom_call" | custom-call | flops 4194304 | bytes 8388608 | tf_op jit(solution)/shard_map/load/pallas_call | solution.py:78
  9.7 1.2 %collective-permute-done.1.halo_ref.refs_14_ = f32[16,512]{1,0:T(8,128)S(1)} collective-permute-done((f32[16,512]{1,0:T(8,128)S(1)}, f32[16,512]{1,0:T(8,128)S(1)}, u32[]{:S(2)}, u32[]{:S(2)}) %collective-permute-start.1) | collective-permute-done | bytes 32800 | tf_op jit(solution)/shard_map/ppermute | solution.py:28
  10.9 0.2 first.1
  11.2 1.1 %collective-permute-start.2 = (f32[8,1792]{1,0:T(8,128)S(1)}, f32[8,1792]{1,0:T(8,128)S(1)}, u32[]{:S(2)}, u32[]{:S(2)}) collective-permute-start(f32[8,1792]{1,0:T(8,128)S(1)} %get-tuple-element.56), channel_id=1, source_target_pairs={{0,2},{2,0},{4,6},{6,4},{8,10},{10,8},{12,14},{14,12},{16,18},{18,... | collective-permute-start | bytes 172040 | tf_op jit(solution)/shard_map/ppermute | solution.py:32
  12.3 0.1 and_or_fusion
  12.4 0.1 collective-permute-start.4
  12.5 2.9 %collective-permute-done.2.refs_0_ = f32[8,1792]{1,0:T(8,128)S(1)} collective-permute-done((f32[8,1792]{1,0:T(8,128)S(1)}, f32[8,1792]{1,0:T(8,128)S(1)}, u32[]{:S(2)}, u32[]{:S(2)}) %collective-permute-start.2) | collective-permute-done | bytes 57376 | tf_op jit(solution)/shard_map/ppermute | solution.py:32
  15.4 1.2 %collective-permute-start.3 = (f32[8,1280]{1,0:T(8,128)S(1)}, f32[8,1280]{1,0:T(8,128)S(1)}, u32[]{:S(2)}, u32[]{:S(2)}) collective-permute-start(f32[8,1280]{1,0:T(8,128)S(1)} %slice_add_fusion), channel_id=1, source_target_pairs={{0,4},{2,6},{4,0},{6,2},{8,12},{10,14},{12,8},{14,10},{16,20},{18,... | collective-permute-start | bytes 122888 | tf_op jit(solution)/shard_map/ppermute | solution.py:32
  16.6 0.0 collective-permute-done.4.refs_1_
  16.6 2.0 %residual1.1.refs_0_.refs_16_ = f32[140,512]{1,0:T(8,128)S(1)} custom-call(f32[140,8,512]{2,1,0:T(8,128)S(1)} %get-tuple-element.52.bar_ref.refs_8_, f32[8,512]{1,0:T(8,128)S(1)} %get-tuple-element.57.row_ref.refs_10_, f32[140,512]{1,0:T(8,128)S(1)} %get-tuple-element.55.powbar_ref.refs_21_, f32[140,512]{1,0:T(8,128)S(1)} %get-tuple-element.58.load_ref, ...), custom_call_target="tpu_custom_call" | custom-call | flops 4194304 | bytes 8388608 | tf_op jit(solution)/shard_map/residual1/pallas_call | solution.py:78
  18.6 0.0 copy-start.14
  18.6 0.0 copy-start.15
  18.6 0.9 %collective-permute-done.3.refs_1_ = f32[8,1280]{1,0:T(8,128)S(1)} collective-permute-done((f32[8,1280]{1,0:T(8,128)S(1)}, f32[8,1280]{1,0:T(8,128)S(1)}, u32[]{:S(2)}, u32[]{:S(2)}) %collective-permute-start.3) | collective-permute-done | bytes 40992 | tf_op jit(solution)/shard_map/ppermute | solution.py:32
  19.5 1.2 %collective-permute-start.5 = (f32[8,1280]{1,0:T(8,128)S(1)}, f32[8,1280]{1,0:T(8,128)S(1)}, u32[]{:S(2)}, u32[]{:S(2)}) collective-permute-start(f32[8,1280]{1,0:T(8,128)S(1)} %select_add_fusion.2), channel_id=1, source_target_pairs={{0,8},{2,10},{4,12},{6,14},{8,0},{10,2},{12,4},{14,6},{16,24},{18,... | collective-permute-start | bytes 122888 | tf_op jit(solution)/shard_map/ppermute | solution.py:32
  20.7 0.0 collective-permute-start.7
  20.7 2.8 %collective-permute-done.5.refs_2_ = f32[8,1280]{1,0:T(8,128)S(1)} collective-permute-done((f32[8,1280]{1,0:T(8,128)S(1)}, f32[8,1280]{1,0:T(8,128)S(1)}, u32[]{:S(2)}, u32[]{:S(2)}) %collective-permute-start.5) | collective-permute-done | bytes 40992 | tf_op jit(solution)/shard_map/ppermute | solution.py:32
  23.6 2.4 %collective-permute-start.6 = (f32[8,1280]{1,0:T(8,128)S(1)}, f32[8,1280]{1,0:T(8,128)S(1)}, u32[]{:S(2)}, u32[]{:S(2)}) collective-permute-start(f32[8,1280]{1,0:T(8,128)S(1)} %select_add_fusion.1), channel_id=1, source_target_pairs={{0,16},{2,18},{4,20},{6,22},{8,24},{10,26},{12,28},{14,30},{16,0},... | collective-permute-start | bytes 122888 | tf_op jit(solution)/shard_map/ppermute | solution.py:32
  26.0 0.0 collective-permute-done.7.refs_1_
  26.0 1.2 %product.1.refs_17_ = f32[140,512]{1,0:T(8,128)S(1)} custom-call(bf16[512,1024]{1,0:T(8,128)(2,1)S(1)} %get-tuple-element.59.high_ref, bf16[512,1024]{1,0:T(8,128)(2,1)S(1)} %get-tuple-element.60.low_ref, f32[140,512]{1,0:T(8,128)S(1)} %residual1.1.refs_0_.refs_16_, f32[140,512]{1,0:T(8,128)S(1)} %collective-permute-done.7.refs_1_), custom_call_target="tpu_custom_call" | custom-call | flops 4194304 | bytes 8388608 | tf_op jit(solution)/shard_map/product/pallas_call | solution.py:78
  27.2 1.4 %collective-permute-done.6.refs_3_ = f32[8,1280]{1,0:T(8,128)S(1)} collective-permute-done((f32[8,1280]{1,0:T(8,128)S(1)}, f32[8,1280]{1,0:T(8,128)S(1)}, u32[]{:S(2)}, u32[]{:S(2)}) %collective-permute-start.6) | collective-permute-done | bytes 40992 | tf_op jit(solution)/shard_map/ppermute | solution.py:32
  28.6 0.1 collective-permute-start.8
  28.7 1.2 %collective-permute-done.8.other_ref = f32[8,1280]{1,0:T(8,128)S(1)} collective-permute-done((f32[8,1280]{1,0:T(8,128)S(1)}, f32[8,1280]{1,0:T(8,128)S(1)}, u32[]{:S(2)}, u32[]{:S(2)}) %collective-permute-start.8) | collective-permute-done | bytes 40992 | tf_op jit(solution)/shard_map/ppermute | solution.py:32
  29.8 0.0 copy-done.14
  29.9 3.0 %middle.1 = (f32[8,512]{1,0:T(8,128)S(1)}, f32[140,8,512]{2,1,0:T(8,128)S(1)}, f32[140,8,512]{2,1,0:T(8,128)S(1)}, f32[140,8,512]{2,1,0:T(8,128)S(1)}, f32[140,5...) custom-call(f32[8,1280]{1,0:T(8,128)S(1)} %select_add_fusion.here_re, ...), custom_call_target="tpu_custom_call" | custom-call | flops 4194304 | bytes 8388608 | tf_op jit(solution)/shard_map/middle/pallas_call | solution.py:78
  32.9 1.2 %collective-permute-start.10 = (f32[8,1152]{1,0:T(8,128)S(1)}, f32[8,1152]{1,0:T(8,128)S(1)}, u32[]{:S(2)}, u32[]{:S(2)}) collective-permute-start(f32[8,1152]{1,0:T(8,128)S(1)} %get-tuple-element.80), channel_id=1, source_target_pairs={{0,2},{2,0},{4,6},{6,4},{8,10},{10,8},{12,14},{14,12},{16,18},{18,... | collective-permute-start | bytes 110600 | tf_op jit(solution)/shard_map/ppermute | solution.py:32
  34.1 0.0 collective-permute-start.9
  34.1 2.8 %collective-permute-done.10.refs_0_ = f32[8,1152]{1,0:T(8,128)S(1)} collective-permute-done((f32[8,1152]{1,0:T(8,128)S(1)}, f32[8,1152]{1,0:T(8,128)S(1)}, u32[]{:S(2)}, u32[]{:S(2)}) %collective-permute-start.10) | collective-permute-done | bytes 36896 | tf_op jit(solution)/shard_map/ppermute | solution.py:32
  36.9 0.1 select_add_fusion.6
  37.0 1.2 %collective-permute-start.11 = (f32[8,1152]{1,0:T(8,128)S(1)}, f32[8,1152]{1,0:T(8,128)S(1)}, u32[]{:S(2)}, u32[]{:S(2)}) collective-permute-start(f32[8,1152]{1,0:T(8,128)S(1)} %select_add_fusion.6), channel_id=1, source_target_pairs={{0,4},{2,6},{4,0},{6,2},{8,12},{10,14},{12,8},{14,10},{16,20},{18,... | collective-permute-start | bytes 110600 | tf_op jit(solution)/shard_map/ppermute | solution.py:32
  38.2 0.0 collective-permute-done.9.refs_1_
  38.2 2.2 %residual2.1 = (f32[140,512]{1,0:T(8,128)S(1)}, f32[140,8,512]{2,1,0:T(8,128)S(1)}, f32[140,8,512]{2,1,0:T(8,128)}, f32[140,512]{1,0:T(8,128)}, f32[140,512]{1,0:T(8,128)}, /*index=5*/f32[140,512]{1,0:T(8,128)}) custom-call(f32[140,8,512]{2,1,0:T(8,128)S(1)} %get-tuple-element.70.gen_ref, f32[140,512]{1,0:T(8,128)S(1)} %get-tuple-element.71.ang_ref, ...), custom_call_target="tpu_custom_call" | custom-call | flops 4194304 | bytes 8388608 | tf_op jit(solution)/shard_map/residual2/pallas_call | solution.py:78
  40.4 0.6 %collective-permute-done.11.refs_1_ = f32[8,1152]{1,0:T(8,128)S(1)} collective-permute-done((f32[8,1152]{1,0:T(8,128)S(1)}, f32[8,1152]{1,0:T(8,128)S(1)}, u32[]{:S(2)}, u32[]{:S(2)}) %collective-permute-start.11) | collective-permute-done | bytes 36896 | tf_op jit(solution)/shard_map/ppermute | solution.py:32
  41.0 0.1 select_add_fusion.5
  41.1 1.2 %collective-permute-start.12 = (f32[8,1152]{1,0:T(8,128)S(1)}, f32[8,1152]{1,0:T(8,128)S(1)}, u32[]{:S(2)}, u32[]{:S(2)}) collective-permute-start(f32[8,1152]{1,0:T(8,128)S(1)} %select_add_fusion.5), channel_id=1, source_target_pairs={{0,8},{2,10},{4,12},{6,14},{8,0},{10,2},{12,4},{14,6},{16,24},{18,... | collective-permute-start | bytes 110600 | tf_op jit(solution)/shard_map/ppermute | solution.py:32
  42.3 2.8 %collective-permute-done.12.refs_2_ = f32[8,1152]{1,0:T(8,128)S(1)} collective-permute-done((f32[8,1152]{1,0:T(8,128)S(1)}, f32[8,1152]{1,0:T(8,128)S(1)}, u32[]{:S(2)}, u32[]{:S(2)}) %collective-permute-start.12) | collective-permute-done | bytes 36896 | tf_op jit(solution)/shard_map/ppermute | solution.py:32
  45.1 0.1 select_add_fusion.4
  45.2 2.5 %collective-permute-start.13 = (f32[8,1152]{1,0:T(8,128)S(1)}, f32[8,1152]{1,0:T(8,128)S(1)}, u32[]{:S(2)}, u32[]{:S(2)}) collective-permute-start(f32[8,1152]{1,0:T(8,128)S(1)} %select_add_fusion.4), channel_id=1, source_target_pairs={{0,16},{2,18},{4,20},{6,22},{8,24},{10,26},{12,28},{14,30},{16,0},... | collective-permute-start | bytes 110600 | tf_op jit(solution)/shard_map/ppermute | solution.py:32
  47.7 2.4 %collective-permute-done.13.refs_3_ = f32[8,1152]{1,0:T(8,128)S(1)} collective-permute-done((f32[8,1152]{1,0:T(8,128)S(1)}, f32[8,1152]{1,0:T(8,128)S(1)}, u32[]{:S(2)}, u32[]{:S(2)}) %collective-permute-start.13) | collective-permute-done | bytes 36896 | tf_op jit(solution)/shard_map/ppermute | solution.py:32
  50.1 0.1 select_add_fusion.3.here_ref.squares_ref
  50.2 0.1 collective-permute-start.14
  50.3 1.2 %collective-permute-done.14.other_ref = f32[8,1152]{1,0:T(8,128)S(1)} collective-permute-done((f32[8,1152]{1,0:T(8,128)S(1)}, f32[8,1152]{1,0:T(8,128)S(1)}, u32[]{:S(2)}, u32[]{:S(2)}) %collective-permute-start.14) | collective-permute-done | bytes 36896 | tf_op jit(solution)/shard_map/ppermute | solution.py:32
  51.5 2.7 %last.1 = (f32[8,512]{1,0:T(8,128)}, f32[140,8,512]{2,1,0:T(8,128)}, f32[140,8,512]{2,1,0:T(8,128)}, f32[140,512]{1,0:T(8,128)}, f32[140,512]{1,0:T(8,128)}) custom-call(f32[8,1152]{1,0:T(8,128)S(1)} %select_add_fusion.3.here_ref.squares_ref, f32[8,1152]{1,0:T(8,128)S(1)} %select_add_fusion.3.here_ref.squares_ref, ...), custom_call_target="tpu_custom_call" | custom-call | flops 4194304 | bytes 8388608 | tf_op jit(solution)/shard_map/last/pallas_call | solution.py:78
  (37 shorter events, 0.1 us)
Async XLA Ops:
  0.6 4.8 %copy-start.4 = (f32[140,512]{1,0:T(8,128)S(1)}, f32[140,512]{1,0:T(8,128)}, u32[]{:S(2)}) copy-start(f32[140,512]{1,0:T(8,128)} %refs_15_.1) | copy-start | bytes 860164
  0.7 4.8 %copy-start.2 = (f32[140,8,512]{2,1,0:T(8,128)S(1)}, f32[140,8,512]{2,1,0:T(8,128)}, u32[]{:S(2)}) copy-start(f32[140,8,512]{2,1,0:T(8,128)} %refs_0_.3) | copy-start | bytes 6881284
  0.7 4.8 %copy-start = (f32[140,8,512]{2,1,0:T(8,128)S(1)}, f32[140,8,512]{2,1,0:T(8,128)}, u32[]{:S(2)}) copy-start(f32[140,8,512]{2,1,0:T(8,128)} %refs_11_.1) | copy-start | bytes 6881284
  0.7 4.8 %copy-start.1 = (f32[140,8,512]{2,1,0:T(8,128)S(1)}, f32[140,8,512]{2,1,0:T(8,128)}, u32[]{:S(2)}) copy-start(f32[140,8,512]{2,1,0:T(8,128)} %refs_12_.1) | copy-start | bytes 6881284
  0.7 4.8 %copy-start.6 = (bf16[140,8,512]{2,1,0:T(8,128)(2,1)S(1)}, bf16[140,8,512]{2,1,0:T(8,128)(2,1)}, u32[]{:S(2)}) copy-start(bf16[140,8,512]{2,1,0:T(8,128)(2,1)} %refs_3_.1) | copy-start | bytes 3440644
  0.7 4.8 %copy-start.3 = (f32[512,1024]{1,0:T(8,128)S(1)}, f32[512,1024]{1,0:T(8,128)}, u32[]{:S(2)}) copy-start(f32[512,1024]{1,0:T(8,128)} %refs_2_.1) | copy-start | bytes 6291460
  0.7 4.8 %copy-start.13 = (s32[8,512]{1,0:T(8,128)S(1)}, s32[8,512]{1,0:T(8,128)}, u32[]{:S(2)}) copy-start(s32[8,512]{1,0:T(8,128)} %refs_5_.3) | copy-start | bytes 49156
  0.7 4.8 %copy-start.8 = (f32[140,512]{1,0:T(8,128)S(1)}, f32[140,512]{1,0:T(8,128)}, u32[]{:S(2)}) copy-start(f32[140,512]{1,0:T(8,128)} %refs_4_.2) | copy-start | bytes 860164
  0.7 4.8 %copy-start.7 = (f32[140,512]{1,0:T(8,128)S(1)}, f32[140,512]{1,0:T(8,128)}, u32[]{:S(2)}) copy-start(f32[140,512]{1,0:T(8,128)} %refs_19_.1) | copy-start | bytes 860164
  0.7 4.8 %copy-start.9 = (f32[140,512]{1,0:T(8,128)S(1)}, f32[140,512]{1,0:T(8,128)}, u32[]{:S(2)}) copy-start(f32[140,512]{1,0:T(8,128)} %refs_7_.2) | copy-start | bytes 860164
  0.7 4.8 %copy-start.5 = (f32[140,512]{1,0:T(8,128)S(1)}, f32[140,512]{1,0:T(8,128)}, u32[]{:S(2)}) copy-start(f32[140,512]{1,0:T(8,128)} %refs_24_.1) | copy-start | bytes 860164
  0.8 4.8 %copy-start.11 = (f32[8,512]{1,0:T(8,128)S(1)}, f32[8,512]{1,0:T(8,128)}, u32[]{:S(2)}) copy-start(f32[8,512]{1,0:T(8,128)} %refs_7_.3) | copy-start | bytes 49156
  0.8 4.8 %copy-start.12 = (f32[8,512]{1,0:T(8,128)S(1)}, f32[8,512]{1,0:T(8,128)}, u32[]{:S(2)}) copy-start(f32[8,512]{1,0:T(8,128)} %refs_6_.5) | copy-start | bytes 49156
  0.8 4.8 %copy-start.16 = (s32[8,8]{1,0:T(8,128)S(1)}, s32[8,8]{1,0:T(8,128)}, u32[]{:S(2)}) copy-start(s32[8,8]{1,0:T(8,128)} %pat_s.1) | copy-start | bytes 772
  0.8 4.6 %collective-permute-start = (f32[140,512]{1,0:T(8,128)}, f32[140,512]{1,0:T(8,128)S(1)}, u32[]{:S(2)}, u32[]{:S(2)}) collective-permute-start(f32[140,512]{1,0:T(8,128)} %refs_15_.1), channel_id=1, source_target_pairs={{0,1},{1,0},{2,3},{3,2},{4,5},{5,4},{6,7},{7,6},{8,9},{9,8},{10,11... | collective-permute-start | bytes 860168 | tf_op jit(solution)/shard_map/ppermute | solution.py:32
  2.4 8.5 %collective-permute-start.1 = (f32[16,512]{1,0:T(8,128)S(1)}, f32[16,512]{1,0:T(8,128)S(1)}, u32[]{:S(2)}, u32[]{:S(2)}) collective-permute-start(f32[16,512]{1,0:T(8,128)S(1)} %pack.1), channel_id=1, source_target_pairs={{30,0},{0,2},{2,4},{4,6},{6,8},{8,10},{10,12},{12,14},{14,16},{16,... | collective-permute-start | bytes 98312 | tf_op jit(solution)/shard_map/ppermute | solution.py:28
  5.4 5.5 %copy-start.10 = (f32[140,512]{1,0:T(8,128)S(1)}, f32[140,512]{1,0:T(8,128)}, u32[]{:S(2)}) copy-start(f32[140,512]{1,0:T(8,128)} %lev_ref.1) | copy-start | bytes 860164
  11.2 4.2 %collective-permute-start.2 = (f32[8,1792]{1,0:T(8,128)S(1)}, f32[8,1792]{1,0:T(8,128)S(1)}, u32[]{:S(2)}, u32[]{:S(2)}) collective-permute-start(f32[8,1792]{1,0:T(8,128)S(1)} %get-tuple-element.56), channel_id=1, source_target_pairs={{0,2},{2,0},{4,6},{6,4},{8,10},{10,8},{12,14},{14,12},{16,18},{18,... | collective-permute-start | bytes 172040 | tf_op jit(solution)/shard_map/ppermute | solution.py:32
  12.4 4.2 %collective-permute-start.4 = (f32[140,512]{1,0:T(8,128)S(1)}, f32[140,512]{1,0:T(8,128)S(1)}, u32[]{:S(2)}, u32[]{:S(2)}) collective-permute-start(f32[140,512]{1,0:T(8,128)S(1)} %get-tuple-element.61.refs_0_), channel_id=1, source_target_pairs={{0,1},{1,0},{2,3},{3,2},{4,5},{5,4},{6,7},{7,6},{8,9},{9,8},{10,11... | collective-permute-start | bytes 860168 | tf_op jit(solution)/shard_map/ppermute | solution.py:32
  15.4 4.1 %collective-permute-start.3 = (f32[8,1280]{1,0:T(8,128)S(1)}, f32[8,1280]{1,0:T(8,128)S(1)}, u32[]{:S(2)}, u32[]{:S(2)}) collective-permute-start(f32[8,1280]{1,0:T(8,128)S(1)} %slice_add_fusion), channel_id=1, source_target_pairs={{0,4},{2,6},{4,0},{6,2},{8,12},{10,14},{12,8},{14,10},{16,20},{18,... | collective-permute-start | bytes 122888 | tf_op jit(solution)/shard_map/ppermute | solution.py:32
  18.6 11.3 %copy-start.14 = (f32[8,512]{1,0:T(8,128)S(1)}, f32[8,512]{1,0:T(8,128)}, u32[]{:S(2)}) copy-start(f32[8,512]{1,0:T(8,128)} %refs_5_.5) | copy-start | bytes 49156
  18.6 11.3 %copy-start.15 = (f32[8,512]{1,0:T(8,128)S(1)}, f32[8,512]{1,0:T(8,128)}, u32[]{:S(2)}) copy-start(f32[8,512]{1,0:T(8,128)} %refs_4_.3) | copy-start | bytes 49156
  19.5 4.1 %collective-permute-start.5 = (f32[8,1280]{1,0:T(8,128)S(1)}, f32[8,1280]{1,0:T(8,128)S(1)}, u32[]{:S(2)}, u32[]{:S(2)}) collective-permute-start(f32[8,1280]{1,0:T(8,128)S(1)} %select_add_fusion.2), channel_id=1, source_target_pairs={{0,8},{2,10},{4,12},{6,14},{8,0},{10,2},{12,4},{14,6},{16,24},{18,... | collective-permute-start | bytes 122888 | tf_op jit(solution)/shard_map/ppermute | solution.py:32
  20.7 5.3 %collective-permute-start.7 = (f32[140,512]{1,0:T(8,128)S(1)}, f32[140,512]{1,0:T(8,128)S(1)}, u32[]{:S(2)}, u32[]{:S(2)}) collective-permute-start(f32[140,512]{1,0:T(8,128)S(1)} %residual1.1.refs_0_.refs_16_), channel_id=1, source_target_pairs={{0,1},{1,0},{2,3},{3,2},{4,5},{5,4},{6,7},{7,6},{8,9},{9,8},{10,11... | collective-permute-start | bytes 860168 | tf_op jit(solution)/shard_map/ppermute | solution.py:32
  23.6 5.0 %collective-permute-start.6 = (f32[8,1280]{1,0:T(8,128)S(1)}, f32[8,1280]{1,0:T(8,128)S(1)}, u32[]{:S(2)}, u32[]{:S(2)}) collective-permute-start(f32[8,1280]{1,0:T(8,128)S(1)} %select_add_fusion.1), channel_id=1, source_target_pairs={{0,16},{2,18},{4,20},{6,22},{8,24},{10,26},{12,28},{14,30},{16,0},... | collective-permute-start | bytes 122888 | tf_op jit(solution)/shard_map/ppermute | solution.py:32
  28.6 1.3 %collective-permute-start.8 = (f32[8,1280]{1,0:T(8,128)S(1)}, f32[8,1280]{1,0:T(8,128)S(1)}, u32[]{:S(2)}, u32[]{:S(2)}) collective-permute-start(f32[8,1280]{1,0:T(8,128)S(1)} %select_add_fusion.here_ref.squares_ref), channel_id=1, source_target_pairs={{0,1},{1,0},{2,3},{3,2},{4,5},{5,4},{6,7},{7,6},{8,9},{9,8},{10,11... | collective-permute-start | bytes 122888 | tf_op jit(solution)/shard_map/ppermute | solution.py:32
  32.9 4.0 %collective-permute-start.10 = (f32[8,1152]{1,0:T(8,128)S(1)}, f32[8,1152]{1,0:T(8,128)S(1)}, u32[]{:S(2)}, u32[]{:S(2)}) collective-permute-start(f32[8,1152]{1,0:T(8,128)S(1)} %get-tuple-element.80), channel_id=1, source_target_pairs={{0,2},{2,0},{4,6},{6,4},{8,10},{10,8},{12,14},{14,12},{16,18},{18,... | collective-permute-start | bytes 110600 | tf_op jit(solution)/shard_map/ppermute | solution.py:32
  34.1 4.1 %collective-permute-start.9 = (f32[140,512]{1,0:T(8,128)S(1)}, f32[140,512]{1,0:T(8,128)S(1)}, u32[]{:S(2)}, u32[]{:S(2)}) collective-permute-start(f32[140,512]{1,0:T(8,128)S(1)} %get-tuple-element.75.refs_0_), channel_id=1, source_target_pairs={{0,1},{1,0},{2,3},{3,2},{4,5},{5,4},{6,7},{7,6},{8,9},{9,8},{10,11... | collective-permute-start | bytes 860168 | tf_op jit(solution)/shard_map/ppermute | solution.py:32
  37.0 4.0 %collective-permute-start.11 = (f32[8,1152]{1,0:T(8,128)S(1)}, f32[8,1152]{1,0:T(8,128)S(1)}, u32[]{:S(2)}, u32[]{:S(2)}) collective-permute-start(f32[8,1152]{1,0:T(8,128)S(1)} %select_add_fusion.6), channel_id=1, source_target_pairs={{0,4},{2,6},{4,0},{6,2},{8,12},{10,14},{12,8},{14,10},{16,20},{18,... | collective-permute-start | bytes 110600 | tf_op jit(solution)/shard_map/ppermute | solution.py:32
  41.1 4.0 %collective-permute-start.12 = (f32[8,1152]{1,0:T(8,128)S(1)}, f32[8,1152]{1,0:T(8,128)S(1)}, u32[]{:S(2)}, u32[]{:S(2)}) collective-permute-start(f32[8,1152]{1,0:T(8,128)S(1)} %select_add_fusion.5), channel_id=1, source_target_pairs={{0,8},{2,10},{4,12},{6,14},{8,0},{10,2},{12,4},{14,6},{16,24},{18,... | collective-permute-start | bytes 110600 | tf_op jit(solution)/shard_map/ppermute | solution.py:32
  45.2 4.9 %collective-permute-start.13 = (f32[8,1152]{1,0:T(8,128)S(1)}, f32[8,1152]{1,0:T(8,128)S(1)}, u32[]{:S(2)}, u32[]{:S(2)}) collective-permute-start(f32[8,1152]{1,0:T(8,128)S(1)} %select_add_fusion.4), channel_id=1, source_target_pairs={{0,16},{2,18},{4,20},{6,22},{8,24},{10,26},{12,28},{14,30},{16,0},... | collective-permute-start | bytes 110600 | tf_op jit(solution)/shard_map/ppermute | solution.py:32
  50.2 1.3 %collective-permute-start.14 = (f32[8,1152]{1,0:T(8,128)S(1)}, f32[8,1152]{1,0:T(8,128)S(1)}, u32[]{:S(2)}, u32[]{:S(2)}) collective-permute-start(f32[8,1152]{1,0:T(8,128)S(1)} %select_add_fusion.3.here_ref.squares_ref), channel_id=1, source_target_pairs={{0,1},{1,0},{2,3},{3,2},{4,5},{5,4},{6,7},{7,6},{8,9},{9,8},{10,11... | collective-permute-start | bytes 110600 | tf_op jit(solution)/shard_map/ppermute | solution.py:32

commit v5 on v4

--- a/solution.py
+++ b/solution.py
@@ -307,7 +307,7 @@
         bar_ref, new_ref, row_ref, lim_ref, ramp_ref, avail_ref, halo_ref,
         bal_ref, res_ref, resflow_ref, flow_ref, ang_ref, pownew_ref, powbar_ref, levnew_ref, levbar_ref, sto_ref,
         capout_ref, gen2_ref, lim2_ref, ramp2_ref, bal2_ref, sto2_ref, ang2_ref, angbar2_ref, pow2_ref,
-        powbar2_ref, lev2_ref, levbar2_ref, out_ref, shift_ref,
+        powbar2_ref, lev2_ref, levbar2_ref, out_ref, shift_ref, cut_ref,
     ) = refs
     rows, _, buses = bar_ref.shape
     invest, step_size = get_totals(entries, buses, 3, here_ref, squares_ref, other_ref)
@@ -355,17 +355,18 @@
         jnp.zeros((TECH, buses), F32), ang_step, pow_new - pow_old, lev_new - lev_old
     )
 
-    unroll = divisor(rows, 7)
+    unroll = divisor(rows, 10)
 
     def step(t, carry, first=False, last=False):
-        bar, before, limit_sum, ramp_sum, squares = carry
+        scaled, before, limit_sum, ramp_sum, squares = carry
         old = row_ref[...] if first else new_ref[t]
         bar_next = bar_front if last else bar_ref[t + 1]
         avail = avail_ref[t]
-        lim = jnp.maximum(0.0, lim_ref[t] + step_size * (bar - avail * cap_bar))
-        ramp = jnp.maximum(0.0, ramp_ref[t] + step_size * (bar_next - bar - ramp_cap))
-        dual = jnp.broadcast_to(bal2_ref[pl.ds(t, 1), :], (TECH, buses))
-        gen = jnp.maximum(0.0, old - primal_step * (cost + dual + lim + before - ramp))
+        scaled_next = step_size * bar_next
+        lim = jnp.maximum(0.0, lim_ref[t] + (scaled - avail * cap_step))
+        ramp = jnp.maximum(0.0, ramp_ref[t] + (scaled_next - scaled - ramp_cap_step))
+        dual = jnp.broadcast_to(cut_ref[pl.ds(t, 1), :], (TECH, buses))
+        gen = jnp.maximum(0.0, old - (cost_step + dual) - primal_step * (lim + before - ramp))
         squares += (gen - old) ** 2
         limit_sum += avail * lim
         ramp_sum += ramp
@@ -374,12 +375,14 @@
         ramp2_ref[t] = ramp
         if first:
             put_cubes(out_ref, 1, 2.0 * gen - old)
-        return bar_next, ramp, limit_sum, ramp_sum, squares
+        return scaled_next, ramp, limit_sum, ramp_sum, squares
 
     bar = 2.0 * row_ref[...] - bar_ref[0]
     before = jnp.maximum(0.0, halo_ref[:TECH] + step_size * (bar - bar_behind - ramp_cap))
     zero = jnp.zeros((TECH, buses), F32)
-    carry = (bar, before, zero, zero, squares)
+    cap_step, ramp_cap_step, cost_step = step_size * cap_bar, step_size * ramp_cap, primal_step * cost
+    cut_ref[...] = primal_step * bal
+    carry = (step_size * bar, before, zero, zero, squares)
     for t in range(unroll):
         carry = step(t, carry, first=t == 0)
 
@@ -620,7 +623,7 @@
          storage_dual),
         [VMEM] * (24 + steps),
         [(tech, F32)] + [(cube, F32)] * 3 + [(flat, F32)] * 8 + [((TECH, 2 * buses + layout(buses, 1)[0]), F32)],
-        scratch=(shift,),
+        scratch=(shift, pltpu.VMEM(flat, F32)),
         name="middle",
     )
     sources2 = all_buses(ang_bar2)

time: 54.4 us -> 54.2 us (level)
  no operation moved by 1% of the time
where the time goes in v5:
time: 54.2 us; the launch traced here: 54 us
  waiting for transfers between devices  20.3 us (37%)
  Pallas kernels  16.3 us (30%)
  starting transfers between devices  15.2 us (28%)
  between operations  1.65 us (3%)
    ppermute x14, waiting for transfers between devices, partner(): lax.ppermute(block, axis, [(i, i ^ distance) for i in range(lax.axis_size...  19.1 us
    pallas_call x8, Pallas kernels, call(): pl.pallas_call(body, out_shape=[jax.ShapeDtypeStruct(shape, dtype) for sh...  16.3 us
    ppermute x14, starting transfers between devices, partner(): lax.ppermute(block, axis, [(i, i ^ distance) for i in range(lax.axis_size...  12.8 us
    ppermute x1, starting transfers between devices, shifted(): return lax.ppermute(block, axis, route)  2.39 us
    ppermute x1, waiting for transfers between devices, shifted(): return lax.ppermute(block, axis, route)  1.24 us
  transfers between devices with their start and end apart: 15, of which 11 were waited for; matrix products, arithmetic and copies ran while one was open for 0% of the time, Pallas kernels for 19%

profile of v5, /device:TPU:0, one launch (start us, length us, event | category | flops | bytes accessed | tf_op | source)
XLA Modules:
  0.0 54.0 jit_solution(528618322494534989)
XLA Ops:
  0.6 0.0 copy-start.4
  0.8 0.5 collective-permute-start
  1.3 1.1 %pack.1 = f32[16,512]{1,0:T(8,128)S(1)} custom-call(f32[140,8,512]{2,1,0:T(8,128)} %refs_12_.1, f32[140,512]{1,0:T(8,128)} %refs_24_.1, f32[140,8,512]{2,1,0:T(8,128)} %refs_0_.3, f32[140,8,512]{2,1,0:T(8,128)} %refs_11_.1, f32[512,1024]{1,0:T(8,128)} %refs_2_.1, bf16[140,8,512]{2,1,0:T(8,128)(2,1)} %refs_3_.1, f32[140,512]{1,0:T(8,128)} %refs_4_.2, ...), custom_call_target="tpu_custom_call" | custom-call | flops 4194304 | bytes 268435456 | tf_op jit(solution)/shard_map/pack/pallas_call | solution.py:78
  2.4 2.4 %collective-permute-start.1 = (f32[16,512]{1,0:T(8,128)S(1)}, f32[16,512]{1,0:T(8,128)S(1)}, u32[]{:S(2)}, u32[]{:S(2)}) collective-permute-start(f32[16,512]{1,0:T(8,128)S(1)} %pack.1), channel_id=1, source_target_pairs={{30,0},{0,2},{2,4},{4,6},{6,8},{8,10},{10,12},{12,14},{14,16},{16,... | collective-permute-start | bytes 98312 | tf_op jit(solution)/shard_map/ppermute | solution.py:28
  5.4 0.0 copy-start.10
  5.4 0.0 collective-permute-done.refs_1_
  5.6 4.1 %load.1 = (f32[140,8,512]{2,1,0:T(8,128)S(1)}, f32[140,8,512]{2,1,0:T(8,128)S(1)}, f32[140,8,512]{2,1,0:T(8,128)S(1)}, bf16[512,1024]{1,0:T(8,128)(2,1)S(1)}, bf...) custom-call(f32[140,8,512]{2,1,0:T(8,128)S(1)} %copy-done.2, ...), custom_call_target="tpu_custom_call" | custom-call | flops 4194304 | bytes 8388608 | tf_op jit(solution)/shard_map/load/pallas_call | solution.py:78
  9.7 1.2 %collective-permute-done.1.halo_ref.refs_14_ = f32[16,512]{1,0:T(8,128)S(1)} collective-permute-done((f32[16,512]{1,0:T(8,128)S(1)}, f32[16,512]{1,0:T(8,128)S(1)}, u32[]{:S(2)}, u32[]{:S(2)}) %collective-permute-start.1) | collective-permute-done | bytes 32800 | tf_op jit(solution)/shard_map/ppermute | solution.py:28
  10.9 0.2 first.1
  11.2 1.1 %collective-permute-start.2 = (f32[8,1792]{1,0:T(8,128)S(1)}, f32[8,1792]{1,0:T(8,128)S(1)}, u32[]{:S(2)}, u32[]{:S(2)}) collective-permute-start(f32[8,1792]{1,0:T(8,128)S(1)} %get-tuple-element.56), channel_id=1, source_target_pairs={{0,2},{2,0},{4,6},{6,4},{8,10},{10,8},{12,14},{14,12},{16,18},{18,... | collective-permute-start | bytes 172040 | tf_op jit(solution)/shard_map/ppermute | solution.py:32
  12.3 0.1 and_or_fusion
  12.4 0.1 collective-permute-start.4
  12.5 2.9 %collective-permute-done.2.refs_0_ = f32[8,1792]{1,0:T(8,128)S(1)} collective-permute-done((f32[8,1792]{1,0:T(8,128)S(1)}, f32[8,1792]{1,0:T(8,128)S(1)}, u32[]{:S(2)}, u32[]{:S(2)}) %collective-permute-start.2) | collective-permute-done | bytes 57376 | tf_op jit(solution)/shard_map/ppermute | solution.py:32
  15.4 1.2 %collective-permute-start.3 = (f32[8,1280]{1,0:T(8,128)S(1)}, f32[8,1280]{1,0:T(8,128)S(1)}, u32[]{:S(2)}, u32[]{:S(2)}) collective-permute-start(f32[8,1280]{1,0:T(8,128)S(1)} %slice_add_fusion), channel_id=1, source_target_pairs={{0,4},{2,6},{4,0},{6,2},{8,12},{10,14},{12,8},{14,10},{16,20},{18,... | collective-permute-start | bytes 122888 | tf_op jit(solution)/shard_map/ppermute | solution.py:32
  16.6 0.0 collective-permute-done.4.refs_1_
  16.6 2.0 %residual1.1.refs_0_.refs_16_ = f32[140,512]{1,0:T(8,128)S(1)} custom-call(f32[140,8,512]{2,1,0:T(8,128)S(1)} %get-tuple-element.52.bar_ref.refs_8_, f32[8,512]{1,0:T(8,128)S(1)} %get-tuple-element.57.row_ref.refs_10_, f32[140,512]{1,0:T(8,128)S(1)} %get-tuple-element.55.powbar_ref.refs_21_, f32[140,512]{1,0:T(8,128)S(1)} %get-tuple-element.58.load_ref, ...), custom_call_target="tpu_custom_call" | custom-call | flops 4194304 | bytes 8388608 | tf_op jit(solution)/shard_map/residual1/pallas_call | solution.py:78
  18.6 0.0 copy-start.14
  18.6 0.0 copy-start.15
  18.6 0.9 %collective-permute-done.3.refs_1_ = f32[8,1280]{1,0:T(8,128)S(1)} collective-permute-done((f32[8,1280]{1,0:T(8,128)S(1)}, f32[8,1280]{1,0:T(8,128)S(1)}, u32[]{:S(2)}, u32[]{:S(2)}) %collective-permute-start.3) | collective-permute-done | bytes 40992 | tf_op jit(solution)/shard_map/ppermute | solution.py:32
  19.5 1.2 %collective-permute-start.5 = (f32[8,1280]{1,0:T(8,128)S(1)}, f32[8,1280]{1,0:T(8,128)S(1)}, u32[]{:S(2)}, u32[]{:S(2)}) collective-permute-start(f32[8,1280]{1,0:T(8,128)S(1)} %select_add_fusion.2), channel_id=1, source_target_pairs={{0,8},{2,10},{4,12},{6,14},{8,0},{10,2},{12,4},{14,6},{16,24},{18,... | collective-permute-start | bytes 122888 | tf_op jit(solution)/shard_map/ppermute | solution.py:32
  20.7 0.0 collective-permute-start.7
  20.7 2.8 %collective-permute-done.5.refs_2_ = f32[8,1280]{1,0:T(8,128)S(1)} collective-permute-done((f32[8,1280]{1,0:T(8,128)S(1)}, f32[8,1280]{1,0:T(8,128)S(1)}, u32[]{:S(2)}, u32[]{:S(2)}) %collective-permute-start.5) | collective-permute-done | bytes 40992 | tf_op jit(solution)/shard_map/ppermute | solution.py:32
  23.6 2.4 %collective-permute-start.6 = (f32[8,1280]{1,0:T(8,128)S(1)}, f32[8,1280]{1,0:T(8,128)S(1)}, u32[]{:S(2)}, u32[]{:S(2)}) collective-permute-start(f32[8,1280]{1,0:T(8,128)S(1)} %select_add_fusion.1), channel_id=1, source_target_pairs={{0,16},{2,18},{4,20},{6,22},{8,24},{10,26},{12,28},{14,30},{16,0},... | collective-permute-start | bytes 122888 | tf_op jit(solution)/shard_map/ppermute | solution.py:32
  26.0 0.0 collective-permute-done.7.refs_1_
  26.0 1.2 %product.1.refs_17_ = f32[140,512]{1,0:T(8,128)S(1)} custom-call(bf16[512,1024]{1,0:T(8,128)(2,1)S(1)} %get-tuple-element.59.high_ref, bf16[512,1024]{1,0:T(8,128)(2,1)S(1)} %get-tuple-element.60.low_ref, f32[140,512]{1,0:T(8,128)S(1)} %residual1.1.refs_0_.refs_16_, f32[140,512]{1,0:T(8,128)S(1)} %collective-permute-done.7.refs_1_), custom_call_target="tpu_custom_call" | custom-call | flops 4194304 | bytes 8388608 | tf_op jit(solution)/shard_map/product/pallas_call | solution.py:78
  27.2 1.4 %collective-permute-done.6.refs_3_ = f32[8,1280]{1,0:T(8,128)S(1)} collective-permute-done((f32[8,1280]{1,0:T(8,128)S(1)}, f32[8,1280]{1,0:T(8,128)S(1)}, u32[]{:S(2)}, u32[]{:S(2)}) %collective-permute-start.6) | collective-permute-done | bytes 40992 | tf_op jit(solution)/shard_map/ppermute | solution.py:32
  28.6 0.1 collective-permute-start.8
  28.7 1.2 %collective-permute-done.8.other_ref = f32[8,1280]{1,0:T(8,128)S(1)} collective-permute-done((f32[8,1280]{1,0:T(8,128)S(1)}, f32[8,1280]{1,0:T(8,128)S(1)}, u32[]{:S(2)}, u32[]{:S(2)}) %collective-permute-start.8) | collective-permute-done | bytes 40992 | tf_op jit(solution)/shard_map/ppermute | solution.py:32
  29.8 0.0 copy-done.14
  29.9 2.9 %middle.1 = (f32[8,512]{1,0:T(8,128)S(1)}, f32[140,8,512]{2,1,0:T(8,128)S(1)}, f32[140,8,512]{2,1,0:T(8,128)S(1)}, f32[140,8,512]{2,1,0:T(8,128)S(1)}, f32[140,5...) custom-call(f32[8,1280]{1,0:T(8,128)S(1)} %select_add_fusion.here_re, ...), custom_call_target="tpu_custom_call" | custom-call | flops 4194304 | bytes 8388608 | tf_op jit(solution)/shard_map/middle/pallas_call | solution.py:78
  32.7 1.2 %collective-permute-start.10 = (f32[8,1152]{1,0:T(8,128)S(1)}, f32[8,1152]{1,0:T(8,128)S(1)}, u32[]{:S(2)}, u32[]{:S(2)}) collective-permute-start(f32[8,1152]{1,0:T(8,128)S(1)} %get-tuple-element.80), channel_id=1, source_target_pairs={{0,2},{2,0},{4,6},{6,4},{8,10},{10,8},{12,14},{14,12},{16,18},{18,... | collective-permute-start | bytes 110600 | tf_op jit(solution)/shard_map/ppermute | solution.py:32
  34.0 0.0 collective-permute-start.9
  34.0 2.8 %collective-permute-done.10.refs_0_ = f32[8,1152]{1,0:T(8,128)S(1)} collective-permute-done((f32[8,1152]{1,0:T(8,128)S(1)}, f32[8,1152]{1,0:T(8,128)S(1)}, u32[]{:S(2)}, u32[]{:S(2)}) %collective-permute-start.10) | collective-permute-done | bytes 36896 | tf_op jit(solution)/shard_map/ppermute | solution.py:32
  36.8 0.1 select_add_fusion.6
  36.8 1.2 %collective-permute-start.11 = (f32[8,1152]{1,0:T(8,128)S(1)}, f32[8,1152]{1,0:T(8,128)S(1)}, u32[]{:S(2)}, u32[]{:S(2)}) collective-permute-start(f32[8,1152]{1,0:T(8,128)S(1)} %select_add_fusion.6), channel_id=1, source_target_pairs={{0,4},{2,6},{4,0},{6,2},{8,12},{10,14},{12,8},{14,10},{16,20},{18,... | collective-permute-start | bytes 110600 | tf_op jit(solution)/shard_map/ppermute | solution.py:32
  38.1 0.0 collective-permute-done.9.refs_1_
  38.1 2.2 %residual2.1 = (f32[140,512]{1,0:T(8,128)S(1)}, f32[140,8,512]{2,1,0:T(8,128)S(1)}, f32[140,8,512]{2,1,0:T(8,128)}, f32[140,512]{1,0:T(8,128)}, f32[140,512]{1,0:T(8,128)}, /*index=5*/f32[140,512]{1,0:T(8,128)}) custom-call(f32[140,8,512]{2,1,0:T(8,128)S(1)} %get-tuple-element.70.gen_ref, f32[140,512]{1,0:T(8,128)S(1)} %get-tuple-element.71.ang_ref, ...), custom_call_target="tpu_custom_call" | custom-call | flops 4194304 | bytes 8388608 | tf_op jit(solution)/shard_map/residual2/pallas_call | solution.py:78
  40.2 0.6 %collective-permute-done.11.refs_1_ = f32[8,1152]{1,0:T(8,128)S(1)} collective-permute-done((f32[8,1152]{1,0:T(8,128)S(1)}, f32[8,1152]{1,0:T(8,128)S(1)}, u32[]{:S(2)}, u32[]{:S(2)}) %collective-permute-start.11) | collective-permute-done | bytes 36896 | tf_op jit(solution)/shard_map/ppermute | solution.py:32
  40.9 0.1 select_add_fusion.5
  40.9 1.2 %collective-permute-start.12 = (f32[8,1152]{1,0:T(8,128)S(1)}, f32[8,1152]{1,0:T(8,128)S(1)}, u32[]{:S(2)}, u32[]{:S(2)}) collective-permute-start(f32[8,1152]{1,0:T(8,128)S(1)} %select_add_fusion.5), channel_id=1, source_target_pairs={{0,8},{2,10},{4,12},{6,14},{8,0},{10,2},{12,4},{14,6},{16,24},{18,... | collective-permute-start | bytes 110600 | tf_op jit(solution)/shard_map/ppermute | solution.py:32
  42.2 2.8 %collective-permute-done.12.refs_2_ = f32[8,1152]{1,0:T(8,128)S(1)} collective-permute-done((f32[8,1152]{1,0:T(8,128)S(1)}, f32[8,1152]{1,0:T(8,128)S(1)}, u32[]{:S(2)}, u32[]{:S(2)}) %collective-permute-start.12) | collective-permute-done | bytes 36896 | tf_op jit(solution)/shard_map/ppermute | solution.py:32
  45.0 0.1 select_add_fusion.4
  45.0 2.5 %collective-permute-start.13 = (f32[8,1152]{1,0:T(8,128)S(1)}, f32[8,1152]{1,0:T(8,128)S(1)}, u32[]{:S(2)}, u32[]{:S(2)}) collective-permute-start(f32[8,1152]{1,0:T(8,128)S(1)} %select_add_fusion.4), channel_id=1, source_target_pairs={{0,16},{2,18},{4,20},{6,22},{8,24},{10,26},{12,28},{14,30},{16,0},... | collective-permute-start | bytes 110600 | tf_op jit(solution)/shard_map/ppermute | solution.py:32
  47.5 2.4 %collective-permute-done.13.refs_3_ = f32[8,1152]{1,0:T(8,128)S(1)} collective-permute-done((f32[8,1152]{1,0:T(8,128)S(1)}, f32[8,1152]{1,0:T(8,128)S(1)}, u32[]{:S(2)}, u32[]{:S(2)}) %collective-permute-start.13) | collective-permute-done | bytes 36896 | tf_op jit(solution)/shard_map/ppermute | solution.py:32
  50.0 0.1 select_add_fusion.3.here_ref.squares_ref
  50.0 0.1 collective-permute-start.14
  50.1 1.2 %collective-permute-done.14.other_ref = f32[8,1152]{1,0:T(8,128)S(1)} collective-permute-done((f32[8,1152]{1,0:T(8,128)S(1)}, f32[8,1152]{1,0:T(8,128)S(1)}, u32[]{:S(2)}, u32[]{:S(2)}) %collective-permute-start.14) | collective-permute-done | bytes 36896 | tf_op jit(solution)/shard_map/ppermute | solution.py:32
  51.3 2.7 %last.1 = (f32[8,512]{1,0:T(8,128)}, f32[140,8,512]{2,1,0:T(8,128)}, f32[140,8,512]{2,1,0:T(8,128)}, f32[140,512]{1,0:T(8,128)}, f32[140,512]{1,0:T(8,128)}) custom-call(f32[8,1152]{1,0:T(8,128)S(1)} %select_add_fusion.3.here_ref.squares_ref, f32[8,1152]{1,0:T(8,128)S(1)} %select_add_fusion.3.here_ref.squares_ref, ...), custom_call_target="tpu_custom_call" | custom-call | flops 4194304 | bytes 8388608 | tf_op jit(solution)/shard_map/last/pallas_call | solution.py:78
  (37 shorter events, 0.1 us)
Async XLA Ops:
  0.6 4.8 %copy-start.4 = (f32[140,512]{1,0:T(8,128)S(1)}, f32[140,512]{1,0:T(8,128)}, u32[]{:S(2)}) copy-start(f32[140,512]{1,0:T(8,128)} %refs_15_.1) | copy-start | bytes 860164
  0.7 4.8 %copy-start.2 = (f32[140,8,512]{2,1,0:T(8,128)S(1)}, f32[140,8,512]{2,1,0:T(8,128)}, u32[]{:S(2)}) copy-start(f32[140,8,512]{2,1,0:T(8,128)} %refs_0_.3) | copy-start | bytes 6881284
  0.7 4.8 %copy-start = (f32[140,8,512]{2,1,0:T(8,128)S(1)}, f32[140,8,512]{2,1,0:T(8,128)}, u32[]{:S(2)}) copy-start(f32[140,8,512]{2,1,0:T(8,128)} %refs_11_.1) | copy-start | bytes 6881284
  0.7 4.8 %copy-start.1 = (f32[140,8,512]{2,1,0:T(8,128)S(1)}, f32[140,8,512]{2,1,0:T(8,128)}, u32[]{:S(2)}) copy-start(f32[140,8,512]{2,1,0:T(8,128)} %refs_12_.1) | copy-start | bytes 6881284
  0.7 4.8 %copy-start.6 = (bf16[140,8,512]{2,1,0:T(8,128)(2,1)S(1)}, bf16[140,8,512]{2,1,0:T(8,128)(2,1)}, u32[]{:S(2)}) copy-start(bf16[140,8,512]{2,1,0:T(8,128)(2,1)} %refs_3_.1) | copy-start | bytes 3440644
  0.7 4.8 %copy-start.3 = (f32[512,1024]{1,0:T(8,128)S(1)}, f32[512,1024]{1,0:T(8,128)}, u32[]{:S(2)}) copy-start(f32[512,1024]{1,0:T(8,128)} %refs_2_.1) | copy-start | bytes 6291460
  0.7 4.8 %copy-start.13 = (s32[8,512]{1,0:T(8,128)S(1)}, s32[8,512]{1,0:T(8,128)}, u32[]{:S(2)}) copy-start(s32[8,512]{1,0:T(8,128)} %refs_5_.3) | copy-start | bytes 49156
  0.7 4.8 %copy-start.8 = (f32[140,512]{1,0:T(8,128)S(1)}, f32[140,512]{1,0:T(8,128)}, u32[]{:S(2)}) copy-start(f32[140,512]{1,0:T(8,128)} %refs_4_.2) | copy-start | bytes 860164
  0.7 4.8 %copy-start.7 = (f32[140,512]{1,0:T(8,128)S(1)}, f32[140,512]{1,0:T(8,128)}, u32[]{:S(2)}) copy-start(f32[140,512]{1,0:T(8,128)} %refs_19_.1) | copy-start | bytes 860164
  0.7 4.8 %copy-start.9 = (f32[140,512]{1,0:T(8,128)S(1)}, f32[140,512]{1,0:T(8,128)}, u32[]{:S(2)}) copy-start(f32[140,512]{1,0:T(8,128)} %refs_7_.2) | copy-start | bytes 860164
  0.7 4.8 %copy-start.5 = (f32[140,512]{1,0:T(8,128)S(1)}, f32[140,512]{1,0:T(8,128)}, u32[]{:S(2)}) copy-start(f32[140,512]{1,0:T(8,128)} %refs_24_.1) | copy-start | bytes 860164
  0.8 4.8 %copy-start.11 = (f32[8,512]{1,0:T(8,128)S(1)}, f32[8,512]{1,0:T(8,128)}, u32[]{:S(2)}) copy-start(f32[8,512]{1,0:T(8,128)} %refs_7_.3) | copy-start | bytes 49156
  0.8 4.8 %copy-start.12 = (f32[8,512]{1,0:T(8,128)S(1)}, f32[8,512]{1,0:T(8,128)}, u32[]{:S(2)}) copy-start(f32[8,512]{1,0:T(8,128)} %refs_6_.5) | copy-start | bytes 49156
  0.8 4.8 %copy-start.16 = (s32[8,8]{1,0:T(8,128)S(1)}, s32[8,8]{1,0:T(8,128)}, u32[]{:S(2)}) copy-start(s32[8,8]{1,0:T(8,128)} %pat_s.1) | copy-start | bytes 772
  0.8 4.6 %collective-permute-start = (f32[140,512]{1,0:T(8,128)}, f32[140,512]{1,0:T(8,128)S(1)}, u32[]{:S(2)}, u32[]{:S(2)}) collective-permute-start(f32[140,512]{1,0:T(8,128)} %refs_15_.1), channel_id=1, source_target_pairs={{0,1},{1,0},{2,3},{3,2},{4,5},{5,4},{6,7},{7,6},{8,9},{9,8},{10,11... | collective-permute-start | bytes 860168 | tf_op jit(solution)/shard_map/ppermute | solution.py:32
  2.4 8.5 %collective-permute-start.1 = (f32[16,512]{1,0:T(8,128)S(1)}, f32[16,512]{1,0:T(8,128)S(1)}, u32[]{:S(2)}, u32[]{:S(2)}) collective-permute-start(f32[16,512]{1,0:T(8,128)S(1)} %pack.1), channel_id=1, source_target_pairs={{30,0},{0,2},{2,4},{4,6},{6,8},{8,10},{10,12},{12,14},{14,16},{16,... | collective-permute-start | bytes 98312 | tf_op jit(solution)/shard_map/ppermute | solution.py:28
  5.4 5.5 %copy-start.10 = (f32[140,512]{1,0:T(8,128)S(1)}, f32[140,512]{1,0:T(8,128)}, u32[]{:S(2)}) copy-start(f32[140,512]{1,0:T(8,128)} %lev_ref.1) | copy-start | bytes 860164
  11.2 4.2 %collective-permute-start.2 = (f32[8,1792]{1,0:T(8,128)S(1)}, f32[8,1792]{1,0:T(8,128)S(1)}, u32[]{:S(2)}, u32[]{:S(2)}) collective-permute-start(f32[8,1792]{1,0:T(8,128)S(1)} %get-tuple-element.56), channel_id=1, source_target_pairs={{0,2},{2,0},{4,6},{6,4},{8,10},{10,8},{12,14},{14,12},{16,18},{18,... | collective-permute-start | bytes 172040 | tf_op jit(solution)/shard_map/ppermute | solution.py:32
  12.4 4.2 %collective-permute-start.4 = (f32[140,512]{1,0:T(8,128)S(1)}, f32[140,512]{1,0:T(8,128)S(1)}, u32[]{:S(2)}, u32[]{:S(2)}) collective-permute-start(f32[140,512]{1,0:T(8,128)S(1)} %get-tuple-element.61.refs_0_), channel_id=1, source_target_pairs={{0,1},{1,0},{2,3},{3,2},{4,5},{5,4},{6,7},{7,6},{8,9},{9,8},{10,11... | collective-permute-start | bytes 860168 | tf_op jit(solution)/shard_map/ppermute | solution.py:32
  15.4 4.1 %collective-permute-start.3 = (f32[8,1280]{1,0:T(8,128)S(1)}, f32[8,1280]{1,0:T(8,128)S(1)}, u32[]{:S(2)}, u32[]{:S(2)}) collective-permute-start(f32[8,1280]{1,0:T(8,128)S(1)} %slice_add_fusion), channel_id=1, source_target_pairs={{0,4},{2,6},{4,0},{6,2},{8,12},{10,14},{12,8},{14,10},{16,20},{18,... | collective-permute-start | bytes 122888 | tf_op jit(solution)/shard_map/ppermute | solution.py:32
  18.6 11.3 %copy-start.14 = (f32[8,512]{1,0:T(8,128)S(1)}, f32[8,512]{1,0:T(8,128)}, u32[]{:S(2)}) copy-start(f32[8,512]{1,0:T(8,128)} %refs_5_.5) | copy-start | bytes 49156
  18.6 11.3 %copy-start.15 = (f32[8,512]{1,0:T(8,128)S(1)}, f32[8,512]{1,0:T(8,128)}, u32[]{:S(2)}) copy-start(f32[8,512]{1,0:T(8,128)} %refs_4_.3) | copy-start | bytes 49156
  19.5 4.1 %collective-permute-start.5 = (f32[8,1280]{1,0:T(8,128)S(1)}, f32[8,1280]{1,0:T(8,128)S(1)}, u32[]{:S(2)}, u32[]{:S(2)}) collective-permute-start(f32[8,1280]{1,0:T(8,128)S(1)} %select_add_fusion.2), channel_id=1, source_target_pairs={{0,8},{2,10},{4,12},{6,14},{8,0},{10,2},{12,4},{14,6},{16,24},{18,... | collective-permute-start | bytes 122888 | tf_op jit(solution)/shard_map/ppermute | solution.py:32
  20.7 5.3 %collective-permute-start.7 = (f32[140,512]{1,0:T(8,128)S(1)}, f32[140,512]{1,0:T(8,128)S(1)}, u32[]{:S(2)}, u32[]{:S(2)}) collective-permute-start(f32[140,512]{1,0:T(8,128)S(1)} %residual1.1.refs_0_.refs_16_), channel_id=1, source_target_pairs={{0,1},{1,0},{2,3},{3,2},{4,5},{5,4},{6,7},{7,6},{8,9},{9,8},{10,11... | collective-permute-start | bytes 860168 | tf_op jit(solution)/shard_map/ppermute | solution.py:32
  23.6 5.0 %collective-permute-start.6 = (f32[8,1280]{1,0:T(8,128)S(1)}, f32[8,1280]{1,0:T(8,128)S(1)}, u32[]{:S(2)}, u32[]{:S(2)}) collective-permute-start(f32[8,1280]{1,0:T(8,128)S(1)} %select_add_fusion.1), channel_id=1, source_target_pairs={{0,16},{2,18},{4,20},{6,22},{8,24},{10,26},{12,28},{14,30},{16,0},... | collective-permute-start | bytes 122888 | tf_op jit(solution)/shard_map/ppermute | solution.py:32
  28.6 1.3 %collective-permute-start.8 = (f32[8,1280]{1,0:T(8,128)S(1)}, f32[8,1280]{1,0:T(8,128)S(1)}, u32[]{:S(2)}, u32[]{:S(2)}) collective-permute-start(f32[8,1280]{1,0:T(8,128)S(1)} %select_add_fusion.here_ref.squares_ref), channel_id=1, source_target_pairs={{0,1},{1,0},{2,3},{3,2},{4,5},{5,4},{6,7},{7,6},{8,9},{9,8},{10,11... | collective-permute-start | bytes 122888 | tf_op jit(solution)/shard_map/ppermute | solution.py:32
  32.7 4.0 %collective-permute-start.10 = (f32[8,1152]{1,0:T(8,128)S(1)}, f32[8,1152]{1,0:T(8,128)S(1)}, u32[]{:S(2)}, u32[]{:S(2)}) collective-permute-start(f32[8,1152]{1,0:T(8,128)S(1)} %get-tuple-element.80), channel_id=1, source_target_pairs={{0,2},{2,0},{4,6},{6,4},{8,10},{10,8},{12,14},{14,12},{16,18},{18,... | collective-permute-start | bytes 110600 | tf_op jit(solution)/shard_map/ppermute | solution.py:32
  34.0 4.1 %collective-permute-start.9 = (f32[140,512]{1,0:T(8,128)S(1)}, f32[140,512]{1,0:T(8,128)S(1)}, u32[]{:S(2)}, u32[]{:S(2)}) collective-permute-start(f32[140,512]{1,0:T(8,128)S(1)} %get-tuple-element.75.refs_0_), channel_id=1, source_target_pairs={{0,1},{1,0},{2,3},{3,2},{4,5},{5,4},{6,7},{7,6},{8,9},{9,8},{10,11... | collective-permute-start | bytes 860168 | tf_op jit(solution)/shard_map/ppermute | solution.py:32
  36.8 4.0 %collective-permute-start.11 = (f32[8,1152]{1,0:T(8,128)S(1)}, f32[8,1152]{1,0:T(8,128)S(1)}, u32[]{:S(2)}, u32[]{:S(2)}) collective-permute-start(f32[8,1152]{1,0:T(8,128)S(1)} %select_add_fusion.6), channel_id=1, source_target_pairs={{0,4},{2,6},{4,0},{6,2},{8,12},{10,14},{12,8},{14,10},{16,20},{18,... | collective-permute-start | bytes 110600 | tf_op jit(solution)/shard_map/ppermute | solution.py:32
  40.9 4.0 %collective-permute-start.12 = (f32[8,1152]{1,0:T(8,128)S(1)}, f32[8,1152]{1,0:T(8,128)S(1)}, u32[]{:S(2)}, u32[]{:S(2)}) collective-permute-start(f32[8,1152]{1,0:T(8,128)S(1)} %select_add_fusion.5), channel_id=1, source_target_pairs={{0,8},{2,10},{4,12},{6,14},{8,0},{10,2},{12,4},{14,6},{16,24},{18,... | collective-permute-start | bytes 110600 | tf_op jit(solution)/shard_map/ppermute | solution.py:32
  45.0 4.9 %collective-permute-start.13 = (f32[8,1152]{1,0:T(8,128)S(1)}, f32[8,1152]{1,0:T(8,128)S(1)}, u32[]{:S(2)}, u32[]{:S(2)}) collective-permute-start(f32[8,1152]{1,0:T(8,128)S(1)} %select_add_fusion.4), channel_id=1, source_target_pairs={{0,16},{2,18},{4,20},{6,22},{8,24},{10,26},{12,28},{14,30},{16,0},... | collective-permute-start | bytes 110600 | tf_op jit(solution)/shard_map/ppermute | solution.py:32
  50.0 1.3 %collective-permute-start.14 = (f32[8,1152]{1,0:T(8,128)S(1)}, f32[8,1152]{1,0:T(8,128)S(1)}, u32[]{:S(2)}, u32[]{:S(2)}) collective-permute-start(f32[8,1152]{1,0:T(8,128)S(1)} %select_add_fusion.3.here_ref.squares_ref), channel_id=1, source_target_pairs={{0,1},{1,0},{2,3},{3,2},{4,5},{5,4},{6,7},{7,6},{8,9},{9,8},{10,11... | collective-permute-start | bytes 110600 | tf_op jit(solution)/shard_map/ppermute | solution.py:32
